TPU v7x, 128 devices: a whole 4x4x4 slice. The times are simulated.
128 devices in a mesh: left: 16 (over y, z_lo, core), right: 8 (over z_hi, x).
Axes of the slice: x: 4, y: 4, z: 4 (z_hi: 2, z_lo: 2; z = z_hi * 2 + z_lo), core: 2. Of those that a mesh axis runs over, the one named last changes fastest.
Arguments:
- corner: bfloat16 [128, 256, 256], P(('left', 'right')), may hold values from -6 to 6
- edge_row: bfloat16 [256, 64, 256, 256], P('left', 'right'), may hold values from -0.046875 to 0.046875
- source_row: int32 [256, 64], P('left', 'right'), may hold values from 0 to 127, as said below
- proj_row: bfloat16 [256, 256, 256], P('left'), may hold values from -0.375 to 0.375
- edge_col: bfloat16 [32, 160, 256, 256], P('right', 'left'), may hold values from -0.03125 to 0.03125
- source_col: int32 [32, 160], P('right', 'left'), may hold values from 0 to 255, as said below
- proj_col: bfloat16 [32, 256, 256], P('right'), may hold values from -0.375 to 0.375
Outputs:
- absorbed_row: bfloat16 [256, 256, 256], P(('left', 'right'))
- new_corner: bfloat16 [32, 256, 256], P('right', 'left')
Inputs may be any that keep to these rules, and one draw needn't show every extreme that they name: source_row[f, j] is a sector whose block lies on a device with right index j // 8, that is (source_row[f, j]) % 8 == j // 8. source_col[g, j] is a sector of the left index j // 10: source_col[g, j] // 16 == j // 10.
All inputs are finite; a program needn't handle non-finite values.
Results may differ from a plain program's by a relative error of at most 0.03.
Values may be sent and summed in bfloat16 or wider, within the bound.
No kernel may reach another device: no remote copies, remote signals or barrier semaphores. Data moves between devices by JAX's collectives and lax.ppermute only.
A program may use at most 128 MiB of HBM per device.

v0:
```python
import jax
import jax.numpy as jnp
from jax import lax
from jax.sharding import PartitionSpec as P


def body(corner, edge_row, source_row, proj_row, edge_col, source_col, proj_col):
    right_count = lax.axis_size("right")
    held_count = corner.shape[0]
    gathered = lax.all_gather(corner, "left", axis=0, tiled=True)
    block_span = held_count * right_count
    local_index = source_row // block_span * held_count + source_row % held_count
    picked = jnp.take(gathered, local_index, axis=0)
    partial_value = jnp.einsum(
        "fkab,fkbc->fac", picked, edge_row, preferred_element_type=jnp.float32
    )
    rows_here = partial_value.shape[0] // right_count
    summed = lax.psum_scatter(
        partial_value.astype(jnp.bfloat16), "right", scatter_dimension=0, tiled=True
    )
    start_row = lax.axis_index("right") * rows_here
    proj_mine = lax.dynamic_slice_in_dim(proj_row, start_row, rows_here, 0)
    absorbed = jnp.einsum(
        "fba,fbc->fac", proj_mine, summed, preferred_element_type=jnp.float32
    ).astype(jnp.bfloat16)
    row_whole = lax.all_gather(absorbed, "right", axis=0, tiled=True)
    row_base = lax.axis_index("left") * row_whole.shape[0]
    picked_col = jnp.take(row_whole, source_col - row_base, axis=0)
    partial_col = jnp.einsum(
        "gkab,gkbc->gac", edge_col, picked_col, preferred_element_type=jnp.float32
    )
    col_sum = lax.psum_scatter(
        partial_col.astype(jnp.bfloat16), "left", scatter_dimension=1, tiled=True
    )
    new_corner = jnp.einsum(
        "gab,gbc->gac", col_sum, proj_col, preferred_element_type=jnp.float32
    ).astype(jnp.bfloat16)
    return (absorbed, new_corner)


def solution(mesh):
    in_specs = (
        P(("left", "right"), None, None),
        P("left", "right", None, None),
        P("left", "right"),
        P("left", None, None),
        P("right", "left", None, None),
        P("right", "left"),
        P("right", None, None),
    )
    out_specs = (P(("left", "right"), None, None), P("right", "left", None))
    return jax.shard_map(body, mesh=mesh, in_specs=in_specs, out_specs=out_specs, check_vma=False)
```

profile of v0, /device:TPU:1, one launch (start us, length us, event | category | flops | bytes accessed | tf_op | source)
XLA Modules:
  0.0 349.0 jit_solution(7558817099750532541)
XLA Ops:
  7.2 0.0 copy-start
  7.2 0.0 all-gather.3.cloned.1.call-start
  7.2 0.7 all-gather.3.cloned.1.call-update
  7.9 0.0 reduce-scatter.2.cloned.1.call-start
  8.0 0.7 compare_and_fusion
  8.7 0.1 copy.22
  8.7 0.1 reshape.16
  8.8 0.1 copy.21
  8.9 38.3 %all-gather.3.cloned.1.call-done = bf16[16,256,256]{2,1,0:T(8,128)(2,1)} async-done(((bf16[1,256,256]{2,1,0:T(8,128)(2,1)}), bf16[16,256,256]{2,1,0:T(8,128)(2,1)}) %all-gather.3.cloned.1.call-update) | async-done | bytes 2097168 | tf_op jit(solution)/shard_map/all_gather | solution.py:10
  47.2 9.9 %gather_fusion = bf16[128,256,256]{2,1,0:T(8,128)(2,1)} fusion(bf16[16,256,256]{2,1,0:T(8,128)(2,1)} %all-gather.3.cloned.1.call-done, s32[1024]{0:T(1024)S(1)} %pad_clamp_fusion.1), kind=kCustom, calls=%fused_computation | custom fusion | bytes 33554944 | tf_op jit(solution)/shard_map/jit(_take)/gather | solution.py:13
  57.1 14.3 %bitcast_convert_fusion = bf16[16,256,256]{2,1,0:T(8,128)(2,1)} fusion(bf16[16,8,256,256]{3,2,1,0:T(8,128)(2,1)} %param.8, bf16[16,8,256,256]{3,2,1,0:T(8,128)(2,1)} %bitcast.20, pred[16,8]{1,0:T(8,128)(4,1)S(1)} %copy.21), kind=kOutput, calls=%fused_computation.9 | convolution fusion | flops 4304404480 | bytes 35651712 | tf_op jit(solution)/shard_map/fkab,fkbc->fac/dot_general | solution.py:14
  71.4 0.0 reduce-scatter.2.cloned.1.call-update
  71.4 0.0 all-gather.5.cloned.1.call-start
  71.5 73.9 %reduce-scatter.2.cloned.1.call-done = bf16[2,256,256]{2,1,0:T(8,128)(2,1)} async-done(((bf16[16,256,256]{2,1,0:T(8,128)(2,1)}), bf16[2,256,256]{2,1,0:T(8,128)(2,1)}) %reduce-scatter.2.cloned.1.call-update) | async-done | bytes 262160 | tf_op jit(solution)/shard_map/reduce_scatter | solution.py:18
  145.4 0.0 copy-done
  145.4 1.9 convolution_convert_fusion
  147.3 0.0 all-gather.5.cloned.1.call-update
  147.4 0.0 all-reduce.3.cloned.1.call-start
  147.4 0.0 copy-done.2
  147.4 0.1 reshape.24
  147.5 54.7 %all-gather.5.cloned.1.call-done = bf16[16,256,256]{2,1,0:T(8,128)(2,1)} async-done(((bf16[2,256,256]{2,1,0:T(8,128)(2,1)}), bf16[16,256,256]{2,1,0:T(8,128)(2,1)}) %all-gather.5.cloned.1.call-update) | async-done | bytes 2097168 | tf_op jit(solution)/shard_map/all_gather | solution.py:26
  202.2 6.2 %gather_fusion.1 = bf16[40,256,256]{2,1,0:T(8,128)(2,1)} fusion(bf16[16,256,256]{2,1,0:T(8,128)(2,1)} %all-gather.5.cloned.1.call-done, s32[1024]{0:T(1024)S(1)} %pad_clamp_fusion), kind=kCustom, calls=%fused_computation.1 | custom fusion | bytes 10485920 | tf_op jit(solution)/shard_map/jit(_take)/gather | solution.py:28
  208.4 7.9 %copy.23 = bf16[4,10,256,256]{2,3,1,0:T(8,128)(2,1)} copy(bf16[4,10,256,256]{3,2,1,0:T(8,128)(2,1)} %bitcast.19) | data formatting | bytes 10485760 | tf_op jit(solution)/shard_map/jit(_take)/gather | solution.py:28
  216.3 5.7 %fusion.16 = bf16[4,256,256]{1,2,0:T(8,128)(2,1)S(1)} fusion(bf16[4,10,256,256]{3,2,1,0:T(8,128)(2,1)} %param.11, bf16[4,10,256,256]{2,3,1,0:T(8,128)(2,1)} %copy.23, pred[4,10]{1,0:T(4,128)(4,1)S(1)} %get-tuple-element.2), kind=kOutput, calls=%fused_computation.13 | convolution fusion | flops 1345060864 | bytes 11010088 | tf_op jit(solution)/shard_map/gkab,gkbc->gac/dot_general | solution.py:29
  222.0 1.1 copy.24
  223.0 0.0 all-reduce.3.cloned.1.call-update
  223.1 0.0 copy-done.3
  223.1 0.6 dynamic-slice
  224.3 116.6 %all-reduce.3.cloned.1.call-done = bf16[4,256,256]{2,0,1:T(4,128)(2,1)} async-done(((bf16[4,256,256]{2,0,1:T(4,128)(2,1)}), bf16[4,256,256]{2,0,1:T(4,128)(2,1)}) %all-reduce.3.cloned.1.call-update) | async-done | bytes 524304
  340.9 0.8 constant_dynamic-slice_fusion
  341.7 0.0 copy-done.1
  341.7 0.8 convolution_convert_fusion.1
  (6 shorter events, 0.0 us)
Async XLA Ops:
  7.2 138.2 %copy-start = (bf16[16,256,256]{2,1,0:T(8,128)(2,1)S(1)}, bf16[16,256,256]{2,1,0:T(8,128)(2,1)}, u32[]{:S(2)}) copy-start(bf16[16,256,256]{2,1,0:T(8,128)(2,1)} %param.10) | copy-start | bytes 6291460
  7.2 40.0 %all-gather.3.cloned.1.call-start = ((), (), s32[]{:S(2)}) async-start(), calls=%async_computation.1 | async-start | bytes 2228224 | tf_op jit(solution)/shard_map/all_gather | solution.py:10
  7.9 137.5 %reduce-scatter.2.cloned.1.call-start = ((), (), s32[]{:S(2)}) async-start(), calls=%async_computation.2 | async-start | bytes 2359296 | tf_op jit(solution)/shard_map/reduce_scatter | solution.py:18
  57.1 90.3 %copy-start.2 = (s32[4,10]{1,0:T(4,128)S(1)}, s32[4,10]{1,0:T(4,128)}, u32[]{:S(2)}) copy-start(s32[4,10]{1,0:T(4,128)} %param.12) | copy-start | bytes 484
  71.4 130.8 %all-gather.5.cloned.1.call-start = ((), (), s32[]{:S(2)}) async-start(), calls=%async_computation.3 | async-start | bytes 2359296 | tf_op jit(solution)/shard_map/all_gather | solution.py:26
  147.4 193.5 %all-reduce.3.cloned.1.call-start = ((), (), s32[]{:S(2)}) async-start(), calls=%async_computation.4 | async-start | bytes 1048576
  216.3 6.8 %copy-start.3 = (u32[128]{0:T(128)S(1)}, u32[128]{0:T(128)}, u32[]{:S(2)}) copy-start(u32[128]{0:T(128)} %constant.75) | copy-start | bytes 1540
  216.3 125.4 %copy-start.1 = (bf16[4,256,256]{2,1,0:T(8,128)(2,1)S(1)}, bf16[4,256,256]{2,1,0:T(8,128)(2,1)}, u32[]{:S(2)}) copy-start(bf16[4,256,256]{2,1,0:T(8,128)(2,1)} %param.13) | copy-start | bytes 1572868
Sparse Core Ops, SparseCore 0:
  9.7 37.4 all-gather.2
  71.5 73.8 reduce-scatter.1
  148.6 53.6 all-gather.4
  223.2 117.6 all-reduce.2
where the time goes:
time: 349 us
  waiting for transfers between devices  284 us (81%)
  local copies, waits for them, and re-layouts  26.7 us (8%)
  matrix products  22.7 us (7%)
  between operations  14.5 us (4%)
    unnamed x5, waiting for transfers between devices  117 us
    reduce_scatter x1, waiting for transfers between devices, body(): lax.psum_scatter(partial_value.astype(jnp.bfloat16), 'right', scatter_dim...  73.9 us
    all_gather x1, waiting for transfers between devices, body(): row_whole = lax.all_gather(absorbed, 'right', axis=0, tiled=True)  54.7 us
    all_gather x1, waiting for transfers between devices, body(): gathered = lax.all_gather(corner, 'left', axis=0, tiled=True)  38.3 us
    dot_general x1, matrix products, body(): jnp.einsum('fkab,fkbc->fac', picked, edge_row, preferred_element_type=jnp...  14.3 us
    gather x2, local copies, waits for them, and re-layouts, body(): picked_col = jnp.take(row_whole, source_col - row_base, axis=0)  14.1 us
    gather x1, local copies, waits for them, and re-layouts, body(): picked = jnp.take(gathered, local_index, axis=0)  9.86 us
  transfers between devices with their start and end apart: 4, of which 4 were waited for; matrix products, arithmetic and copies ran while one was open for 0% of the time, Pallas kernels for 0%

commit v1 on v0

v1 whole, which is shorter than its diff:
```python
import jax
import jax.numpy as jnp
from jax import lax
from jax.experimental import pallas as pl
from jax.experimental.pallas import tpu as pltpu
from jax.sharding import PartitionSpec as P

F32 = jnp.float32
BF16 = jnp.bfloat16
SIZE = 256


def row_kernel(slot_ref, own_ref, other_ref, edge_ref, out_ref, held, sems):
    step = pl.program_id(0)
    half = own_ref.shape[0]

    @pl.when(step == 0)
    def _():
        first = pltpu.make_async_copy(own_ref, held.at[pl.ds(0, half)], sems.at[0])
        second = pltpu.make_async_copy(other_ref, held.at[pl.ds(half, half)], sems.at[1])
        first.start()
        second.start()
        first.wait()
        second.wait()

    total = jnp.dot(held[slot_ref[step, 0]], edge_ref[0, 0], preferred_element_type=F32)
    for entry in range(1, edge_ref.shape[1]):
        total += jnp.dot(held[slot_ref[step, entry]], edge_ref[0, entry], preferred_element_type=F32)
    out_ref[0] = total.astype(BF16)


def row_partial(slots, own, other, edge_row):
    sectors, entries = edge_row.shape[:2]
    half = own.shape[0]
    return pl.pallas_call(
        row_kernel,
        out_shape=jax.ShapeDtypeStruct((sectors, SIZE, SIZE), BF16),
        grid_spec=pltpu.PrefetchScalarGridSpec(
            num_scalar_prefetch=1,
            grid=(sectors,),
            in_specs=[
                pl.BlockSpec(memory_space=pl.ANY),
                pl.BlockSpec(memory_space=pl.ANY),
                pl.BlockSpec((1, entries, SIZE, SIZE), lambda f, s: (f, 0, 0, 0)),
            ],
            out_specs=pl.BlockSpec((1, SIZE, SIZE), lambda f, s: (f, 0, 0)),
            scratch_shapes=[
                pltpu.VMEM((2 * half, SIZE, SIZE), BF16),
                pltpu.SemaphoreType.DMA((2,)),
            ],
        ),
        compiler_params=pltpu.CompilerParams(vmem_limit_bytes=24 * 2**20),
        name="row_partial",
    )(slots, own, other, edge_row)


def absorb_kernel(first_ref, part_ref, proj_ref, mine_ref, copies_ref):
    total = jnp.sum(part_ref[:, 0].astype(F32), axis=0).astype(BF16)
    value = lax.dot_general(
        proj_ref[0], total, (((0,), (0,)), ((), ())), preferred_element_type=F32
    ).astype(BF16)
    mine_ref[0] = value
    for peer in range(copies_ref.shape[0]):
        copies_ref[peer, 0] = value


def absorb(first, parts, proj_row):
    peers, held = parts.shape[:2]
    return pl.pallas_call(
        absorb_kernel,
        out_shape=(
            jax.ShapeDtypeStruct((held, SIZE, SIZE), BF16),
            jax.ShapeDtypeStruct((peers, held, SIZE, SIZE), BF16),
        ),
        grid_spec=pltpu.PrefetchScalarGridSpec(
            num_scalar_prefetch=1,
            grid=(held,),
            in_specs=[
                pl.BlockSpec((peers, 1, SIZE, SIZE), lambda f, s: (0, f, 0, 0)),
                pl.BlockSpec((1, SIZE, SIZE), lambda f, s: (s[0] + f, 0, 0)),
            ],
            out_specs=(
                pl.BlockSpec((1, SIZE, SIZE), lambda f, s: (f, 0, 0)),
                pl.BlockSpec((peers, 1, SIZE, SIZE), lambda f, s: (0, f, 0, 0)),
            ),
        ),
        name="absorb",
    )(first, parts, proj_row)


def col_kernel(slot_ref, rows_ref, edge_ref, out_ref):
    step = pl.program_id(0)
    total = jnp.dot(edge_ref[0, 0], rows_ref[slot_ref[step, 0]], preferred_element_type=F32)
    for entry in range(1, edge_ref.shape[1]):
        total += jnp.dot(edge_ref[0, entry], rows_ref[slot_ref[step, entry]], preferred_element_type=F32)
    out_ref[:, 0] = total.astype(BF16).reshape(out_ref.shape[0], out_ref.shape[2], SIZE)


def col_partial(slots, rows, edge_col, pieces):
    sectors, entries = edge_col.shape[:2]
    piece = SIZE // pieces
    return pl.pallas_call(
        col_kernel,
        out_shape=jax.ShapeDtypeStruct((pieces, sectors, piece, SIZE), BF16),
        grid_spec=pltpu.PrefetchScalarGridSpec(
            num_scalar_prefetch=1,
            grid=(sectors,),
            in_specs=[
                pl.BlockSpec(rows.shape, lambda g, s: (0, 0, 0), pipeline_mode=pl.Buffered(1)),
                pl.BlockSpec((1, entries, SIZE, SIZE), lambda g, s: (g, 0, 0, 0)),
            ],
            out_specs=pl.BlockSpec((pieces, 1, piece, SIZE), lambda g, s: (0, g, 0, 0)),
        ),
        compiler_params=pltpu.CompilerParams(vmem_limit_bytes=24 * 2**20),
        name="col_partial",
    )(slots, rows, edge_col)


def finish_kernel(part_ref, proj_ref, out_ref):
    for sector in range(proj_ref.shape[0]):
        total = jnp.sum(part_ref[:, sector].astype(F32), axis=0).astype(BF16)
        out_ref[sector] = jnp.dot(total, proj_ref[sector], preferred_element_type=F32).astype(BF16)


def finish(parts, proj_col):
    _, sectors, piece, _ = parts.shape
    return pl.pallas_call(
        finish_kernel,
        out_shape=jax.ShapeDtypeStruct((sectors, piece, SIZE), BF16),
        name="finish",
    )(parts, proj_col)


def body(corner, edge_row, source_row, proj_row, edge_col, source_col, proj_col):
    lefts, rights = lax.axis_size("left"), lax.axis_size("right")
    left, right = lax.axis_index("left"), lax.axis_index("right")

    parity = [list(range(start, lefts, 2)) for start in range(2)]
    own = lax.all_to_all(
        jnp.broadcast_to(corner, (lefts // 2, SIZE, SIZE)), "left", 0, 0, axis_index_groups=parity, tiled=True
    )
    other = lax.ppermute(own, "left", [(i, i ^ 1) for i in range(lefts)])
    owner = source_row // rights
    slots = owner // 2 + jnp.where(owner % 2 == left % 2, 0, lefts // 2)
    partial_rows = row_partial(slots, own, other, edge_row)

    sectors = edge_row.shape[0]
    held = sectors // rights
    parts = lax.all_to_all(partial_rows.reshape(rights, held, SIZE, SIZE), "right", 0, 0, tiled=True)
    first = jnp.reshape(right * held, (1,)).astype(jnp.int32)
    absorbed, copies = absorb(first, parts, proj_row)
    rows = lax.all_to_all(copies, "right", 0, 0, tiled=True).reshape(sectors, SIZE, SIZE)

    partial_cols = col_partial(source_col - left * sectors, rows, edge_col, lefts)
    col_parts = lax.all_to_all(partial_cols, "left", 0, 0, tiled=True)
    return absorbed, finish(col_parts, proj_col)


def solution(mesh):
    in_specs = (
        P(("left", "right"), None, None),
        P("left", "right", None, None),
        P("left", "right"),
        P("left", None, None),
        P("right", "left", None, None),
        P("right", "left"),
        P("right", None, None),
    )
    out_specs = (P(("left", "right"), None, None), P("right", "left", None))
    return jax.shard_map(body, mesh=mesh, in_specs=in_specs, out_specs=out_specs, check_vma=False)
```

time: 349 us -> 139 us (0.40)
  waiting for transfers between devices: 284 us -> 59.3 us
  blocking collectives: 0 us -> 34.1 us
  matrix products: 22.7 us -> 0 us
  Pallas kernels: 0 us -> 17.9 us
  local copies, waits for them, and re-layouts: 26.7 us -> 10.6 us
  starting transfers between devices: 0.16 us -> 15.4 us
  between operations: 14.5 us -> 0.68 us
    unnamed x5 -> x0, waiting for transfers between devices: 117 us -> none
    all_gather x2 -> x0, waiting for transfers between devices: 93 us -> none  [the longest x1 54.7 us: body(): row_whole = lax.all_gather(absorbed, 'right', axis=0, tiled=True)]
    reduce_scatter x1 -> x0, waiting for transfers between devices: 73.9 us -> none  [body(): lax.psum_scatter(partial_value.astype(jnp.bfloat16), 'right', scatter_dim...]
    all_to_all x0 -> x2, waiting for transfers between devices: none -> 57.1 us  [the longest x1 28.6 us: body(): lax.all_to_all(partial_rows.reshape(rights, held, SIZE, SIZE), 'right', 0...]
    all_to_all x0 -> x2, blocking collectives: none -> 34.1 us  [the longest x1 20.5 us: body(): lax.all_to_all(jnp.broadcast_to(corner, (lefts // 2, SIZE, SIZE)), 'left'...]
    gather x3 -> x0, local copies, waits for them, and re-layouts: 23.9 us -> none  [the longest x2 14.1 us: body(): picked_col = jnp.take(row_whole, source_col - row_base, axis=0)]
    dot_general x4 -> x0, matrix products: 22.7 us -> none  [the longest x1 14.3 us: body(): jnp.einsum('fkab,fkbc->fac', picked, edge_row, preferred_element_type=jnp...]
    pallas_call x0 -> x4, Pallas kernels: none -> 17.9 us  [the longest x1 10.1 us: row_partial(): pl.pallas_call(row_kernel, out_shape=jax.ShapeDtypeStruct((sectors, SIZE,...]
  transfers between devices with their start and end apart: 4 -> 3, of which waited for: 4 -> 3; matrix products, arithmetic and copies ran while one was open for 0% -> 0% of each run, Pallas kernels for 0% -> 0%
where the time goes in v1:
time: 139 us; the launch traced here: 138 us
  waiting for transfers between devices  59.3 us (43%)
  blocking collectives  34.1 us (25%)
  Pallas kernels  17.9 us (13%)
  starting transfers between devices  15.4 us (11%)
  local copies, waits for them, and re-layouts  10.6 us (8%)
    all_to_all x1, waiting for transfers between devices, body(): lax.all_to_all(partial_rows.reshape(rights, held, SIZE, SIZE), 'right', 0...  28.6 us
    all_to_all x1, waiting for transfers between devices, body(): lax.all_to_all(copies, 'right', 0, 0, tiled=True)  28.5 us
    all_to_all x1, blocking collectives, body(): lax.all_to_all(jnp.broadcast_to(corner, (lefts // 2, SIZE, SIZE)), 'left'...  20.5 us
    all_to_all x1, blocking collectives, body(): col_parts = lax.all_to_all(partial_cols, 'left', 0, 0, tiled=True)  13.6 us
    pallas_call x1, Pallas kernels, row_partial(): pl.pallas_call(row_kernel, out_shape=jax.ShapeDtypeStruct((sectors, SIZE,...  10.1 us
    unnamed x11, local copies, waits for them, and re-layouts  9.67 us
    all_to_all x1, starting transfers between devices, body(): lax.all_to_all(partial_rows.reshape(rights, held, SIZE, SIZE), 'right', 0...  7.05 us
    all_to_all x1, starting transfers between devices, body(): lax.all_to_all(copies, 'right', 0, 0, tiled=True)  6.32 us
  transfers between devices with their start and end apart: 3, of which 3 were waited for; matrix products, arithmetic and copies ran while one was open for 0% of the time, Pallas kernels for 0%

profile of v1, /device:TPU:1, one launch (start us, length us, event | category | flops | bytes accessed | tf_op | source)
XLA Modules:
  0.0 138.1 jit_solution(17142057005492462679)
XLA Ops:
  0.6 0.0 copy-start.3
  0.6 1.0 broadcast_in_dim.12
  1.6 20.5 %all_to_all.20.own_ref = bf16[8,256,256]{2,1,0:T(8,128)(2,1)S(1)} all-to-all(bf16[8,256,256]{2,1,0:T(8,128)(2,1)S(1)} %broadcast_in_dim.12), channel_id=1, replica_groups={{0,16,32,48,64,80,96,112},{8,24,40,56,72,88,104,120},{1,17,33,49,65,81,..., dimensions={0} | all-to-all | bytes 2097152 | tf_op jit(solution)/shard_map/all_to_all | solution.py:139
  22.1 2.0 %collective-permute-start = (bf16[8,256,256]{2,1,0:T(8,128)(2,1)S(1)}, bf16[8,256,256]{2,1,0:T(8,128)(2,1)S(1)}, u32[]{:S(2)}, u32[]{:S(2)}) collective-permute-start(bf16[8,256,256]{2,1,0:T(8,128)(2,1)S(1)} %all_to_all.20.own_ref), channel_id=1, source_target_pairs={{0,8},{8,0},{16,24},{24,16},{32,40},{40,32},{48,56},{56,48},{64,72... | collective-permute-start | bytes 3145736 | tf_op jit(solution)/shard_map/ppermute | solution.py:142
  24.1 0.0 copy-done.3
  24.1 0.1 copy.9
  24.2 2.2 %collective-permute-done.other_ref = bf16[8,256,256]{2,1,0:T(8,128)(2,1)S(1)} collective-permute-done((bf16[8,256,256]{2,1,0:T(8,128)(2,1)S(1)}, bf16[8,256,256]{2,1,0:T(8,128)(2,1)S(1)}, u32[]{:S(2)}, u32[]{:S(2)}) %collective-permute-start) | collective-permute-done | bytes 1048608 | tf_op jit(solution)/shard_map/ppermute | solution.py:142
  26.4 0.0 copy-start
  26.4 5.8 %copy-done = bf16[16,8,256,256]{3,2,1,0:T(8,128)(2,1)S(1)} copy-done((bf16[16,8,256,256]{3,2,1,0:T(8,128)(2,1)S(1)}, bf16[16,8,256,256]{3,2,1,0:T(8,128)(2,1)}, u32[]{:S(2)}) %copy-start) | copy-done | bytes 16777240
  32.2 10.1 %row_partial.1 = bf16[16,256,256]{2,1,0:T(8,128)(2,1)} custom-call(s32[16,8]{1,0:T(8,128)S(1)} %fusion.1.slot_ref, bf16[8,256,256]{2,1,0:T(8,128)(2,1)S(1)} %all_to_all.20.own_ref, bf16[8,256,256]{2,1,0:T(8,128)(2,1)S(1)} %collective-permute-done.other_ref, bf16[16,8,256,256]{3,2,1,0:T(8,128)(2,1)S(1)} %copy-done), custom_call_target="tpu_custom_call" | custom-call | tf_op jit(solution)/shard_map/row_partial/pallas_call | solution.py:35
  42.3 7.1 %all-to-all-start.1 = ((bf16[8,2,256,256]{3,2,1,0:T(8,128)(2,1)}), bf16[8,2,256,256]{3,2,1,0:T(8,128)(2,1)S(1)}, u32[]{:S(2)}, u32[]{:S(2)}) async-start(bf16[8,2,256,256]{3,2,1,0:T(8,128)(2,1)} %bitcast.2), calls=%async_computation.1 | async-start | bytes 4194304 | tf_op jit(solution)/shard_map/all_to_all | solution.py:149
  49.3 28.6 %all-to-all-done.1.part_ref = bf16[8,2,256,256]{3,2,1,0:T(8,128)(2,1)S(1)} async-done(((bf16[8,2,256,256]{3,2,1,0:T(8,128)(2,1)}), bf16[8,2,256,256]{3,2,1,0:T(8,128)(2,1)S(1)}, u32[]{:S(2)}, u32[]{:S(2)}) %all-to-all-start.1) | async-done | bytes 2097184 | tf_op jit(solution)/shard_map/all_to_all | solution.py:149
  77.9 0.0 copy-start.2
  77.9 1.3 copy-done.2
  79.3 3.1 %absorb.1 = (bf16[2,256,256]{2,1,0:T(8,128)(2,1)}, bf16[8,2,256,256]{3,2,1,0:T(8,128)(2,1)}) custom-call(s32[1]{0:T(128)} %bitcast.first_ref, bf16[8,2,256,256]{3,2,1,0:T(8,128)(2,1)} %copy-done.2, bf16[16,256,256]{2,1,0:T(8,128)(2,1)} %proj_ref.2), custom_call_target="tpu_custom_call" | custom-call | tf_op jit(solution)/shard_map/absorb/pallas_call | solution.py:69
  82.3 0.0 copy-start.4
  82.3 6.3 %all-to-all-start.2 = ((bf16[8,2,256,256]{3,2,1,0:T(8,128)(2,1)}), bf16[8,2,256,256]{3,2,1,0:T(8,128)(2,1)S(1)}, u32[]{:S(2)}, u32[]{:S(2)}) async-start(bf16[8,2,256,256]{3,2,1,0:T(8,128)(2,1)} %get-tuple-element.5), calls=%async_computation.2 | async-start | bytes 4194304 | tf_op jit(solution)/shard_map/all_to_all | solution.py:152
  88.6 0.0 copy-done.4
  88.7 28.5 %all-to-all-done.2 = bf16[8,2,256,256]{3,2,1,0:T(8,128)(2,1)S(1)} async-done(((bf16[8,2,256,256]{3,2,1,0:T(8,128)(2,1)}), bf16[8,2,256,256]{3,2,1,0:T(8,128)(2,1)S(1)}, u32[]{:S(2)}, u32[]{:S(2)}) %all-to-all-start.2) | async-done | bytes 2097184 | tf_op jit(solution)/shard_map/all_to_all | solution.py:152
  117.2 0.0 copy-start.1
  117.2 2.5 %copy-done.1 = bf16[4,10,256,256]{3,2,1,0:T(8,128)(2,1)S(1)} copy-done((bf16[4,10,256,256]{3,2,1,0:T(8,128)(2,1)S(1)}, bf16[4,10,256,256]{3,2,1,0:T(8,128)(2,1)}, u32[]{:S(2)}) %copy-start.1) | copy-done | bytes 5242904
  119.7 2.7 %col_partial.1 = bf16[16,4,16,256]{3,2,1,0:T(8,128)(2,1)S(1)} custom-call(s32[4,10]{1,0:T(4,128)S(1)} %broadcast_subtract_fusion.slot_ref, bf16[16,256,256]{2,1,0:T(8,128)(2,1)S(1)} %bitcast.4, bf16[4,10,256,256]{3,2,1,0:T(8,128)(2,1)S(1)} %copy-done.1), custom_call_target="tpu_custom_call" | custom-call | tf_op jit(solution)/shard_map/col_partial/pallas_call | solution.py:102
  122.4 13.6 %all_to_all.21.part_ref = bf16[16,4,16,256]{3,2,1,0:T(8,128)(2,1)} all-to-all(bf16[16,4,16,256]{3,2,1,0:T(8,128)(2,1)S(1)} %col_partial.1), channel_id=1, replica_groups=mesh['left'=16,'right'=8] {'left'}, dimensions={0} | all-to-all | bytes 1048576 | tf_op jit(solution)/shard_map/all_to_all | solution.py:155
  136.0 2.0 %finish.1 = bf16[4,16,256]{2,1,0:T(8,128)(2,1)} custom-call(bf16[16,4,16,256]{3,2,1,0:T(8,128)(2,1)} %all_to_all.21.part_ref, bf16[4,256,256]{2,1,0:T(8,128)(2,1)} %proj_ref.3), custom_call_target="tpu_custom_call" | custom-call | tf_op jit(solution)/shard_map/finish/pallas_call | solution.py:127
  (2 shorter events, 0.0 us)
Async XLA Ops:
  0.6 23.5 %copy-start.3 = (s32[16,8]{0,1:T(8,128)S(1)}, s32[16,8]{0,1:T(8,128)}, u32[]{:S(2)}) copy-start(s32[16,8]{0,1:T(8,128)} %param.9) | copy-start | bytes 1540
  22.1 4.3 %collective-permute-start = (bf16[8,256,256]{2,1,0:T(8,128)(2,1)S(1)}, bf16[8,256,256]{2,1,0:T(8,128)(2,1)S(1)}, u32[]{:S(2)}, u32[]{:S(2)}) collective-permute-start(bf16[8,256,256]{2,1,0:T(8,128)(2,1)S(1)} %all_to_all.20.own_ref), channel_id=1, source_target_pairs={{0,8},{8,0},{16,24},{24,16},{32,40},{40,32},{48,56},{56,48},{64,72... | collective-permute-start | bytes 3145736 | tf_op jit(solution)/shard_map/ppermute | solution.py:142
  26.4 5.8 %copy-start = (bf16[16,8,256,256]{3,2,1,0:T(8,128)(2,1)S(1)}, bf16[16,8,256,256]{3,2,1,0:T(8,128)(2,1)}, u32[]{:S(2)}) copy-start(bf16[16,8,256,256]{3,2,1,0:T(8,128)(2,1)} %edge_ref.2) | copy-start | bytes 50331652
  42.3 35.6 %all-to-all-start.1 = ((bf16[8,2,256,256]{3,2,1,0:T(8,128)(2,1)}), bf16[8,2,256,256]{3,2,1,0:T(8,128)(2,1)S(1)}, u32[]{:S(2)}, u32[]{:S(2)}) async-start(bf16[8,2,256,256]{3,2,1,0:T(8,128)(2,1)} %bitcast.2), calls=%async_computation.1 | async-start | bytes 4194304 | tf_op jit(solution)/shard_map/all_to_all | solution.py:149
  77.9 1.3 copy-start.2
  82.3 6.3 %copy-start.4 = (s32[4,10]{1,0:T(4,128)S(1)}, s32[4,10]{1,0:T(4,128)}, u32[]{:S(2)}) copy-start(s32[4,10]{1,0:T(4,128)} %param.12) | copy-start | bytes 484
  82.3 34.9 %all-to-all-start.2 = ((bf16[8,2,256,256]{3,2,1,0:T(8,128)(2,1)}), bf16[8,2,256,256]{3,2,1,0:T(8,128)(2,1)S(1)}, u32[]{:S(2)}, u32[]{:S(2)}) async-start(bf16[8,2,256,256]{3,2,1,0:T(8,128)(2,1)} %get-tuple-element.5), calls=%async_computation.2 | async-start | bytes 4194304 | tf_op jit(solution)/shard_map/all_to_all | solution.py:152
  117.2 2.5 %copy-start.1 = (bf16[4,10,256,256]{3,2,1,0:T(8,128)(2,1)S(1)}, bf16[4,10,256,256]{3,2,1,0:T(8,128)(2,1)}, u32[]{:S(2)}) copy-start(bf16[4,10,256,256]{3,2,1,0:T(8,128)(2,1)} %edge_ref.3) | copy-start | bytes 15728644

commit v2 on v0

v2 whole, which is shorter than its diff:
```python
import jax
import jax.numpy as jnp
from jax import lax
from jax.experimental import pallas as pl
from jax.experimental.pallas import tpu as pltpu
from jax.sharding import PartitionSpec as P

F32 = jnp.float32
BF16 = jnp.bfloat16
SIZE = 256
COUNT = 2
FLAT = COUNT * SIZE
FLIPS = (1, 3, 4)
ORDERS = ((0, 1, 2), (1, 2, 0), (2, 0, 1))
CUTS = (0, 176, 352, FLAT)
LENGTHS = tuple(CUTS[i + 1] - CUTS[i] for i in range(3))
VMEM = pl.BlockSpec(memory_space=pltpu.VMEM)
SMALL = pltpu.CompilerParams(vmem_limit_bytes=8 * 2**20)


def flip(value, pairing, size):
    return lax.ppermute(value, "right", [(i, i ^ FLIPS[pairing]) for i in range(size)])


def place_of(place, order):
    bits = [place // 4, place // 2 % 2, place % 2]
    return bits[order[0]] * 4 + bits[order[1]] * 2 + bits[order[2]]


def cost(flops, elements):
    return pl.CostEstimate(flops=flops, bytes_accessed=2 * elements, transcendentals=0)


def row_kernel(slot_ref, peer_ref, held_ref, edge_ref, *out_refs):
    step = pl.program_id(0)
    place = pl.num_programs(0) - 1 - step
    first = peer_ref[step] * COUNT
    values = []
    for sector in range(COUNT):
        total = jnp.dot(held_ref[slot_ref[first + sector, 0]], edge_ref[sector, 0], preferred_element_type=F32)
        for entry in range(1, edge_ref.shape[1]):
            total += jnp.dot(
                held_ref[slot_ref[first + sector, entry]], edge_ref[sector, entry], preferred_element_type=F32
            )
        values.append(total)
    flat = jnp.concatenate(values, axis=0)
    for part, order in enumerate(ORDERS):
        index = place_of(place, order)
        send_ref, keep_ref = out_refs[2 * part], out_refs[2 * part + 1]
        value = flat[CUTS[part] : CUTS[part + 1]]

        @pl.when(index >= 4)
        def _():
            send_ref[index - 4] = value.astype(BF16)

        @pl.when(index < 4)
        def _():
            keep_ref[index] = value


def row_partial(slots, peers, held, edge_row):
    entries = edge_row.shape[1]
    steps = peers.shape[0]
    outs = []
    for length in LENGTHS:
        outs.append(jax.ShapeDtypeStruct((steps // 2, length, SIZE), BF16))
        outs.append(jax.ShapeDtypeStruct((steps // 2, length, SIZE), F32))
    return pl.pallas_call(
        row_kernel,
        out_shape=tuple(outs),
        grid_spec=pltpu.PrefetchScalarGridSpec(
            num_scalar_prefetch=2,
            grid=(steps,),
            in_specs=[
                VMEM,
                pl.BlockSpec((COUNT, entries, SIZE, SIZE), lambda s, slots, peers: (peers[s], 0, 0, 0)),
            ],
            out_specs=tuple(VMEM for _ in outs),
        ),
        compiler_params=pltpu.CompilerParams(vmem_limit_bytes=24 * 2**20),
        cost_estimate=cost(2 * steps * COUNT * entries * SIZE**3, steps * COUNT * entries * SIZE**2),
        name="row_partial",
    )(slots, peers, held, pltpu.with_memory_space_constraint(edge_row, pltpu.HBM))


def halve_kernel(*refs):
    for part in range(3):
        keep_ref, came_ref = refs[2 * part], refs[2 * part + 1]
        send_ref, rest_ref = refs[6 + 2 * part], refs[7 + 2 * part]
        half = send_ref.shape[0]
        send_ref[...] = (keep_ref[half:] + came_ref[half:].astype(F32)).astype(BF16)
        rest_ref[...] = keep_ref[:half] + came_ref[:half].astype(F32)


def halve(keeps, came):
    half = keeps[0].shape[0] // 2
    outs = []
    for length in LENGTHS:
        outs.append(jax.ShapeDtypeStruct((half, length, SIZE), BF16))
        outs.append(jax.ShapeDtypeStruct((half, length, SIZE), F32))
    args = [value for pair in zip(keeps, came) for value in pair]
    return pl.pallas_call(
        halve_kernel,
        out_shape=tuple(outs),
        in_specs=[VMEM] * 6,
        out_specs=tuple(VMEM for _ in outs),
        compiler_params=SMALL,
        cost_estimate=cost(4 * half * FLAT * SIZE, 6 * half * FLAT * SIZE),
        name="halve",
    )(*args)


def absorb_kernel(proj_ref, *refs):
    keep_refs, came_refs, out_ref, part_refs = refs[:3], refs[3:6], refs[6], refs[7:]
    pieces = [keep[0] + came[0].astype(F32) for keep, came in zip(keep_refs, came_refs)]
    total = jnp.concatenate(pieces, axis=0).astype(BF16)
    values = []
    for sector in range(COUNT):
        value = lax.dot_general(
            proj_ref[sector],
            total[sector * SIZE : (sector + 1) * SIZE],
            (((0,), (0,)), ((), ())),
            preferred_element_type=F32,
        ).astype(BF16)
        out_ref[sector] = value
        values.append(value)
    flat = jnp.concatenate(values, axis=0)
    for part, part_ref in enumerate(part_refs):
        part_ref[0] = flat[CUTS[part] : CUTS[part + 1]]


def absorb(index, keeps, came, proj_row):
    outs = [jax.ShapeDtypeStruct((COUNT, SIZE, SIZE), BF16)]
    outs += [jax.ShapeDtypeStruct((1, length, SIZE), BF16) for length in LENGTHS]
    return pl.pallas_call(
        lambda index_ref, *refs: absorb_kernel(*refs),
        out_shape=tuple(outs),
        grid_spec=pltpu.PrefetchScalarGridSpec(
            num_scalar_prefetch=1,
            grid=(1,),
            in_specs=[pl.BlockSpec((COUNT, SIZE, SIZE), lambda s, index: (index[0], 0, 0))] + [VMEM] * 6,
            out_specs=tuple(VMEM for _ in outs),
        ),
        compiler_params=SMALL,
        cost_estimate=cost(2 * COUNT * SIZE**3, 6 * FLAT * SIZE),
        name="absorb",
    )(index, proj_row, *keeps, *came)


def double_kernel(*refs):
    for part in range(3):
        held_ref, came_ref, out_ref = refs[2 * part], refs[2 * part + 1], refs[6 + part]
        half = held_ref.shape[0]
        out_ref[:half] = held_ref[...]
        out_ref[half:] = came_ref[...]


def double(held, came):
    half = held[0].shape[0]
    args = [value for pair in zip(held, came) for value in pair]
    return pl.pallas_call(
        double_kernel,
        out_shape=tuple(jax.ShapeDtypeStruct((2 * half, length, SIZE), BF16) for length in LENGTHS),
        in_specs=[VMEM] * 6,
        out_specs=tuple(VMEM for _ in range(3)),
        compiler_params=SMALL,
        cost_estimate=cost(0, 4 * half * FLAT * SIZE),
        name="double",
    )(*args)


def col_kernel(slot_ref, *refs):
    piece_refs, (edge_ref, out_ref, held, sems) = refs[:6], refs[6:]
    step = pl.program_id(0)

    @pl.when(step == 0)
    def _():
        copies = []
        for part, order in enumerate(ORDERS):
            for place in range(8):
                index = place_of(place, order)
                source = piece_refs[2 * part + index // 4].at[index % 4]
                target = held.at[pl.ds(place * FLAT + CUTS[part], LENGTHS[part])]
                copies.append(pltpu.make_async_copy(source, target, sems.at[part * 8 + place]))
        for copy in copies:
            copy.start()
        for copy in copies:
            copy.wait()

    def block(entry):
        return held[pl.ds(pl.multiple_of(slot_ref[step, entry] * SIZE, SIZE), SIZE)]

    total = jnp.dot(edge_ref[0, 0], block(0), preferred_element_type=F32)
    for entry in range(1, edge_ref.shape[1]):
        total += jnp.dot(edge_ref[0, entry], block(entry), preferred_element_type=F32)
    out_ref[:, 0] = total.astype(BF16).reshape(out_ref.shape[0], out_ref.shape[2], SIZE)


def col_partial(slots, pieces_in, edge_col, pieces):
    sectors, entries = edge_col.shape[:2]
    piece = SIZE // pieces
    return pl.pallas_call(
        col_kernel,
        out_shape=jax.ShapeDtypeStruct((pieces, sectors, piece, SIZE), BF16),
        grid_spec=pltpu.PrefetchScalarGridSpec(
            num_scalar_prefetch=1,
            grid=(sectors,),
            in_specs=[VMEM] * 6 + [pl.BlockSpec((1, entries, SIZE, SIZE), lambda g, s: (g, 0, 0, 0))],
            out_specs=pl.BlockSpec((pieces, 1, piece, SIZE), lambda g, s: (0, g, 0, 0)),
            scratch_shapes=[pltpu.VMEM((8 * FLAT, SIZE), BF16), pltpu.SemaphoreType.DMA((24,))],
        ),
        compiler_params=pltpu.CompilerParams(vmem_limit_bytes=24 * 2**20),
        cost_estimate=cost(2 * sectors * entries * SIZE**3, sectors * entries * SIZE**2),
        name="col_partial",
    )(slots, *pieces_in, pltpu.with_memory_space_constraint(edge_col, pltpu.HBM))


def finish_kernel(part_ref, proj_ref, out_ref):
    for sector in range(proj_ref.shape[0]):
        total = jnp.sum(part_ref[:, sector].astype(F32), axis=0).astype(BF16)
        out_ref[sector] = jnp.dot(total, proj_ref[sector], preferred_element_type=F32).astype(BF16)


def finish(parts, proj_col):
    _, sectors, piece, _ = parts.shape
    return pl.pallas_call(
        finish_kernel,
        out_shape=jax.ShapeDtypeStruct((sectors, piece, SIZE), BF16),
        in_specs=[VMEM] * 2,
        compiler_params=SMALL,
        name="finish",
    )(parts, proj_col)


def body(corner, edge_row, source_row, proj_row, edge_col, source_col, proj_col):
    lefts, rights = lax.axis_size("left"), lax.axis_size("right")
    left, right = lax.axis_index("left"), lax.axis_index("right")

    parity = [list(range(start, lefts, 2)) for start in range(2)]
    own = lax.all_to_all(
        jnp.broadcast_to(corner, (lefts // 2, SIZE, SIZE)), "left", 0, 0, axis_index_groups=parity, tiled=True
    )
    other = lax.ppermute(own, "left", [(i, i ^ 1) for i in range(lefts)])
    held = jnp.concatenate([own, other], axis=0)
    source = source_row // rights
    slots = source // 2 + jnp.where(source % 2 == left % 2, 0, lefts // 2)

    offsets = [p * FLIPS[0] ^ q * FLIPS[1] ^ z * FLIPS[2] for p in range(2) for q in range(2) for z in range(2)]
    peers = jnp.bitwise_xor(right, jnp.array(offsets[::-1], jnp.int32))
    outs = row_partial(slots, peers, held, edge_row)
    for phase in range(3):
        came = [flip(outs[2 * part], ORDERS[part][phase], rights) for part in range(3)]
        keeps = outs[1::2]
        if phase < 2:
            outs = halve(keeps, came)
    absorbed, *parts = absorb(jnp.reshape(right, (1,)).astype(jnp.int32), keeps, came, proj_row)

    for phase in range(3):
        came = [flip(parts[part], ORDERS[part][2 - phase], rights) for part in range(3)]
        if phase < 2:
            parts = double(parts, came)
    pieces = [value for pair in zip(parts, came) for value in pair]

    inner = source_col - left * (rights * COUNT)
    offset = jnp.bitwise_xor(inner // COUNT, right)
    z = offset // 4
    q = offset // 2 % 2
    p = (offset + q) % 2
    partial_cols = col_partial((p * 4 + q * 2 + z) * COUNT + inner % COUNT, pieces, edge_col, lefts)
    col_parts = lax.all_to_all(partial_cols, "left", 0, 0, tiled=True)
    return absorbed, finish(col_parts, proj_col)


def solution(mesh):
    in_specs = (
        P(("left", "right"), None, None),
        P("left", "right", None, None),
        P("left", "right"),
        P("left", None, None),
        P("right", "left", None, None),
        P("right", "left"),
        P("right", None, None),
    )
    out_specs = (P(("left", "right"), None, None), P("right", "left", None))
    return jax.shard_map(body, mesh=mesh, in_specs=in_specs, out_specs=out_specs, check_vma=False)
```

time: 349 us -> 123 us (0.35)
  waiting for transfers between devices: 284 us -> 31 us
  blocking collectives: 0 us -> 42.9 us
  local copies, waits for them, and re-layouts: 26.7 us -> 1.08 us
  starting transfers between devices: 0.16 us -> 25.2 us
  matrix products: 22.7 us -> 0 us
  Pallas kernels: 0 us -> 21.4 us
  between operations: 14.5 us -> 0.74 us
    unnamed x5 -> x0, waiting for transfers between devices: 117 us -> none
    all_gather x2 -> x0, waiting for transfers between devices: 93 us -> none  [the longest x1 54.7 us: body(): row_whole = lax.all_gather(absorbed, 'right', axis=0, tiled=True)]
    reduce_scatter x1 -> x0, waiting for transfers between devices: 73.9 us -> none  [body(): lax.psum_scatter(partial_value.astype(jnp.bfloat16), 'right', scatter_dim...]
    all_to_all x0 -> x2, blocking collectives: none -> 42.9 us  [the longest x1 22.4 us: body(): col_parts = lax.all_to_all(partial_cols, 'left', 0, 0, tiled=True)]
    ppermute x0 -> x19, waiting for transfers between devices: none -> 31 us  [the longest x18 28.8 us: flip(): lax.ppermute(value, 'right', [(i, i ^ FLIPS[pairing]) for i in range(size)])]
    ppermute x0 -> x19, starting transfers between devices: none -> 25.2 us  [the longest x18 23.2 us: flip(): lax.ppermute(value, 'right', [(i, i ^ FLIPS[pairing]) for i in range(size)])]
    gather x3 -> x0, local copies, waits for them, and re-layouts: 23.9 us -> none  [the longest x2 14.1 us: body(): picked_col = jnp.take(row_whole, source_col - row_base, axis=0)]
    dot_general x4 -> x0, matrix products: 22.7 us -> none  [the longest x1 14.3 us: body(): jnp.einsum('fkab,fkbc->fac', picked, edge_row, preferred_element_type=jnp...]
  transfers between devices with their start and end apart: 4 -> 19, of which waited for: 4 -> 7; matrix products, arithmetic and copies ran while one was open for 0% -> 0% of each run, Pallas kernels for 0% -> 0%
where the time goes in v2:
time: 123 us
  blocking collectives  42.9 us (35%)
  waiting for transfers between devices  31 us (25%)
  starting transfers between devices  25.2 us (20%)
  Pallas kernels  21.4 us (17%)
    ppermute x18, waiting for transfers between devices, flip(): lax.ppermute(value, 'right', [(i, i ^ FLIPS[pairing]) for i in range(size)])  28.8 us
    ppermute x18, starting transfers between devices, flip(): lax.ppermute(value, 'right', [(i, i ^ FLIPS[pairing]) for i in range(size)])  23.2 us
    all_to_all x1, blocking collectives, body(): col_parts = lax.all_to_all(partial_cols, 'left', 0, 0, tiled=True)  22.4 us
    all_to_all x1, blocking collectives, body(): lax.all_to_all(jnp.broadcast_to(corner, (lefts // 2, SIZE, SIZE)), 'left'...  20.5 us
    pallas_call x1, Pallas kernels, row_partial(): pl.pallas_call(row_kernel, out_shape=tuple(outs), grid_spec=pltpu.Prefetc...  11.4 us
    pallas_call x1, Pallas kernels, col_partial(): pl.pallas_call(col_kernel, out_shape=jax.ShapeDtypeStruct((pieces, sector...  7.81 us
  transfers between devices with their start and end apart: 19, of which 7 were waited for; matrix products, arithmetic and copies ran while one was open for 0% of the time, Pallas kernels for 0%

profile of v2, /device:TPU:1, one launch (start us, length us, event | category | flops | bytes accessed | tf_op | source)
XLA Modules:
  0.0 122.6 jit_solution(107438060287355489)
XLA Ops:
  0.7 1.0 broadcast_in_dim.12
  1.6 20.5 %all_to_all.10 = bf16[8,256,256]{2,1,0:T(8,128)(2,1)S(1)} all-to-all(bf16[8,256,256]{2,1,0:T(8,128)(2,1)S(1)} %broadcast_in_dim.12), channel_id=1, replica_groups={{0,16,32,48,64,80,96,112},{8,24,40,56,72,88,104,120},{1,17,33,49,65,81,..., dimensions={0} | all-to-all | bytes 2097152 | tf_op jit(solution)/shard_map/all_to_all | solution.py:240
  22.1 2.0 %collective-permute-start = (bf16[8,256,256]{2,1,0:T(8,128)(2,1)S(1)}, bf16[8,256,256]{2,1,0:T(8,128)(2,1)S(1)}, u32[]{:S(2)}, u32[]{:S(2)}) collective-permute-start(bf16[8,256,256]{2,1,0:T(8,128)(2,1)S(1)} %all_to_all.10), channel_id=1, source_target_pairs={{0,8},{8,0},{16,24},{24,16},{32,40},{40,32},{48,56},{56,48},{64,72... | collective-permute-start | bytes 3145736 | tf_op jit(solution)/shard_map/ppermute | solution.py:243
  24.2 2.2 %collective-permute-done = bf16[8,256,256]{2,1,0:T(8,128)(2,1)S(1)} collective-permute-done((bf16[8,256,256]{2,1,0:T(8,128)(2,1)S(1)}, bf16[8,256,256]{2,1,0:T(8,128)(2,1)S(1)}, u32[]{:S(2)}, u32[]{:S(2)}) %collective-permute-start) | collective-permute-done | bytes 1048608 | tf_op jit(solution)/shard_map/ppermute | solution.py:243
  26.4 0.2 pad_maximum_fusion.held_ref
  26.6 11.4 %row_partial.1 = (bf16[4,176,256]{2,1,0:T(8,128)(2,1)S(1)}, f32[4,176,256]{2,1,0:T(8,128)S(1)}, bf16[4,176,256]{2,1,0:T(8,128)(2,1)S(1)}, f32[4,176,256]{2,1,0:T...) custom-call(s32[16,8]{1,0:T(8,128)S(1)} %fusion.1.slot_ref, s32[8]{0:T(128)S(1)} %broadcast_xor_fusion.peer_ref, ...), custom_call_target="tpu_custom_call" | custom-call | flops 4294967296 | bytes 16777216 | tf_op jit(solution)/shard_map/row_partial/pallas_call | solution.py:68
  38.0 1.3 %collective-permute-start.1 = (bf16[4,176,256]{2,1,0:T(8,128)(2,1)S(1)}, bf16[4,176,256]{2,1,0:T(8,128)(2,1)S(1)}, u32[]{:S(2)}, u32[]{:S(2)}) collective-permute-start(bf16[4,176,256]{2,1,0:T(8,128)(2,1)S(1)} %get-tuple-element.31), channel_id=1, source_target_pairs={{0,1},{1,0},{2,3},{3,2},{4,5},{5,4},{6,7},{7,6},{8,9},{9,8},{10,11... | collective-permute-start | bytes 1081352 | tf_op jit(solution)/shard_map/ppermute | solution.py:22
  39.3 1.8 %collective-permute-start.2 = (bf16[4,176,256]{2,1,0:T(8,128)(2,1)S(1)}, bf16[4,176,256]{2,1,0:T(8,128)(2,1)S(1)}, u32[]{:S(2)}, u32[]{:S(2)}) collective-permute-start(bf16[4,176,256]{2,1,0:T(8,128)(2,1)S(1)} %get-tuple-element.33), channel_id=1, source_target_pairs={{0,3},{1,2},{2,1},{3,0},{4,7},{5,6},{6,5},{7,4},{8,11},{9,10},{10,... | collective-permute-start | bytes 1081352 | tf_op jit(solution)/shard_map/ppermute | solution.py:22
  41.1 3.3 %collective-permute-start.3 = (bf16[4,160,256]{2,1,0:T(8,128)(2,1)S(1)}, bf16[4,160,256]{2,1,0:T(8,128)(2,1)S(1)}, u32[]{:S(2)}, u32[]{:S(2)}) collective-permute-start(bf16[4,160,256]{2,1,0:T(8,128)(2,1)S(1)} %get-tuple-element.35), channel_id=1, source_target_pairs={{0,4},{1,5},{2,6},{3,7},{4,0},{5,1},{6,2},{7,3},{8,12},{9,13},{10,... | collective-permute-start | bytes 983048 | tf_op jit(solution)/shard_map/ppermute | solution.py:22
  44.4 7.1 %collective-permute-done.3.refs_5_ = bf16[4,160,256]{2,1,0:T(8,128)(2,1)S(1)} collective-permute-done((bf16[4,160,256]{2,1,0:T(8,128)(2,1)S(1)}, bf16[4,160,256]{2,1,0:T(8,128)(2,1)S(1)}, u32[]{:S(2)}, u32[]{:S(2)}) %collective-permute-start.3) | collective-permute-done | bytes 327712 | tf_op jit(solution)/shard_map/ppermute | solution.py:22
  51.5 0.2 halve.2
  51.7 0.9 collective-permute-start.4
  52.7 2.6 %collective-permute-start.5 = (bf16[2,176,256]{2,1,0:T(8,128)(2,1)S(1)}, bf16[2,176,256]{2,1,0:T(8,128)(2,1)S(1)}, u32[]{:S(2)}, u32[]{:S(2)}) collective-permute-start(bf16[2,176,256]{2,1,0:T(8,128)(2,1)S(1)} %get-tuple-element.39), channel_id=1, source_target_pairs={{0,4},{1,5},{2,6},{3,7},{4,0},{5,1},{6,2},{7,3},{8,12},{9,13},{10,... | collective-permute-start | bytes 540680 | tf_op jit(solution)/shard_map/ppermute | solution.py:22
  55.3 4.5 %collective-permute-done.6.refs_5_ = bf16[2,160,256]{2,1,0:T(8,128)(2,1)S(1)} collective-permute-done((bf16[2,160,256]{2,1,0:T(8,128)(2,1)S(1)}, bf16[2,160,256]{2,1,0:T(8,128)(2,1)S(1)}, u32[]{:S(2)}, u32[]{:S(2)}) %collective-permute-start.6) | collective-permute-done | bytes 163872 | tf_op jit(solution)/shard_map/ppermute | solution.py:22
  59.9 1.8 %collective-permute-start.7 = (bf16[1,176,256]{2,1,0:T(8,128)(2,1)S(1)}, bf16[1,176,256]{2,1,0:T(8,128)(2,1)S(1)}, u32[]{:S(2)}, u32[]{:S(2)}) collective-permute-start(bf16[1,176,256]{2,1,0:T(8,128)(2,1)S(1)} %get-tuple-element.45), channel_id=1, source_target_pairs={{0,4},{1,5},{2,6},{3,7},{4,0},{5,1},{6,2},{7,3},{8,12},{9,13},{10,... | collective-permute-start | bytes 270344 | tf_op jit(solution)/shard_map/ppermute | solution.py:22
  61.6 1.8 %collective-permute-start.9 = (bf16[1,160,256]{2,1,0:T(8,128)(2,1)S(1)}, bf16[1,160,256]{2,1,0:T(8,128)(2,1)S(1)}, u32[]{:S(2)}, u32[]{:S(2)}) collective-permute-start(bf16[1,160,256]{2,1,0:T(8,128)(2,1)S(1)} %get-tuple-element.47), channel_id=1, source_target_pairs={{0,3},{1,2},{2,1},{3,0},{4,7},{5,6},{6,5},{7,4},{8,11},{9,10},{10,... | collective-permute-start | bytes 245768 | tf_op jit(solution)/shard_map/ppermute | solution.py:22
  63.4 2.7 %collective-permute-done.9.refs_6_ = bf16[1,160,256]{2,1,0:T(8,128)(2,1)S(1)} collective-permute-done((bf16[1,160,256]{2,1,0:T(8,128)(2,1)S(1)}, bf16[1,160,256]{2,1,0:T(8,128)(2,1)S(1)}, u32[]{:S(2)}, u32[]{:S(2)}) %collective-permute-start.9) | collective-permute-done | bytes 81952 | tf_op jit(solution)/shard_map/ppermute | solution.py:22
  66.1 1.0 absorb.1
  67.2 1.3 %collective-permute-start.10 = (bf16[1,176,256]{2,1,0:T(8,128)(2,1)S(1)}, bf16[1,176,256]{2,1,0:T(8,128)(2,1)S(1)}, u32[]{:S(2)}, u32[]{:S(2)}) collective-permute-start(bf16[1,176,256]{2,1,0:T(8,128)(2,1)S(1)} %get-tuple-element.49.refs_0_), channel_id=1, source_target_pairs={{0,4},{1,5},{2,6},{3,7},{4,0},{5,1},{6,2},{7,3},{8,12},{9,13},{10,... | collective-permute-start | bytes 270344 | tf_op jit(solution)/shard_map/ppermute | solution.py:22
  68.5 0.3 collective-permute-start.11
  68.7 1.8 %collective-permute-start.12 = (bf16[1,160,256]{2,1,0:T(8,128)(2,1)S(1)}, bf16[1,160,256]{2,1,0:T(8,128)(2,1)S(1)}, u32[]{:S(2)}, u32[]{:S(2)}) collective-permute-start(bf16[1,160,256]{2,1,0:T(8,128)(2,1)S(1)} %get-tuple-element.51.refs_4_), channel_id=1, source_target_pairs={{0,3},{1,2},{2,1},{3,0},{4,7},{5,6},{6,5},{7,4},{8,11},{9,10},{10,... | collective-permute-start | bytes 245768 | tf_op jit(solution)/shard_map/ppermute | solution.py:22
  70.5 2.7 %collective-permute-done.12.refs_5_ = bf16[1,160,256]{2,1,0:T(8,128)(2,1)S(1)} collective-permute-done((bf16[1,160,256]{2,1,0:T(8,128)(2,1)S(1)}, bf16[1,160,256]{2,1,0:T(8,128)(2,1)S(1)}, u32[]{:S(2)}, u32[]{:S(2)}) %collective-permute-start.12) | collective-permute-done | bytes 81952 | tf_op jit(solution)/shard_map/ppermute | solution.py:22
  73.3 1.9 %collective-permute-start.13 = (bf16[2,176,256]{2,1,0:T(8,128)(2,1)S(1)}, bf16[2,176,256]{2,1,0:T(8,128)(2,1)S(1)}, u32[]{:S(2)}, u32[]{:S(2)}) collective-permute-start(bf16[2,176,256]{2,1,0:T(8,128)(2,1)S(1)} %get-tuple-element.52.refs_0_), channel_id=1, source_target_pairs={{0,3},{1,2},{2,1},{3,0},{4,7},{5,6},{6,5},{7,4},{8,11},{9,10},{10,... | collective-permute-start | bytes 540680 | tf_op jit(solution)/shard_map/ppermute | solution.py:22
  75.2 1.7 %collective-permute-start.14 = (bf16[2,176,256]{2,1,0:T(8,128)(2,1)S(1)}, bf16[2,176,256]{2,1,0:T(8,128)(2,1)S(1)}, u32[]{:S(2)}, u32[]{:S(2)}) collective-permute-start(bf16[2,176,256]{2,1,0:T(8,128)(2,1)S(1)} %get-tuple-element.53.refs_2_), channel_id=1, source_target_pairs={{0,4},{1,5},{2,6},{3,7},{4,0},{5,1},{6,2},{7,3},{8,12},{9,13},{10,... | collective-permute-start | bytes 540680 | tf_op jit(solution)/shard_map/ppermute | solution.py:22
  76.8 4.2 %collective-permute-done.15.refs_5_ = bf16[2,160,256]{2,1,0:T(8,128)(2,1)S(1)} collective-permute-done((bf16[2,160,256]{2,1,0:T(8,128)(2,1)S(1)}, bf16[2,160,256]{2,1,0:T(8,128)(2,1)S(1)}, u32[]{:S(2)}, u32[]{:S(2)}) %collective-permute-start.15) | collective-permute-done | bytes 163872 | tf_op jit(solution)/shard_map/ppermute | solution.py:22
  81.1 0.1 collective-permute-start.16
  81.2 1.0 collective-permute-start.17
  82.1 1.7 %collective-permute-start.18 = (bf16[4,160,256]{2,1,0:T(8,128)(2,1)S(1)}, bf16[4,160,256]{2,1,0:T(8,128)(2,1)S(1)}, u32[]{:S(2)}, u32[]{:S(2)}) collective-permute-start(bf16[4,160,256]{2,1,0:T(8,128)(2,1)S(1)} %get-tuple-element.57.refs_4_), channel_id=1, source_target_pairs={{0,4},{1,5},{2,6},{3,7},{4,0},{5,1},{6,2},{7,3},{8,12},{9,13},{10,... | collective-permute-start | bytes 983048 | tf_op jit(solution)/shard_map/ppermute | solution.py:22
  83.8 7.6 %collective-permute-done.18.refs_5_ = bf16[4,160,256]{2,1,0:T(8,128)(2,1)S(1)} collective-permute-done((bf16[4,160,256]{2,1,0:T(8,128)(2,1)S(1)}, bf16[4,160,256]{2,1,0:T(8,128)(2,1)S(1)}, u32[]{:S(2)}, u32[]{:S(2)}) %collective-permute-start.18) | collective-permute-done | bytes 327712 | tf_op jit(solution)/shard_map/ppermute | solution.py:22
  91.5 7.8 %col_partial.1 = bf16[16,4,16,256]{3,2,1,0:T(8,128)(2,1)S(1)} custom-call(s32[4,10]{1,0:T(4,128)S(1)} %fusion.14.slot_ref, bf16[4,176,256]{2,1,0:T(8,128)(2,1)S(1)} %get-tuple-element.55.refs_0_, bf16[4,176,256]{2,1,0:T(8,128)(2,1)S(1)} %collective-permute-done.16.refs_1_, bf16[4,176,256]{2,1,0:T(8,128)(2,1)S(1)} %get-tuple-element.56.refs_2_, ...), custom_call_target="tpu_custom_call" | custom-call | flops 1342177280 | bytes 5242880 | tf_op jit(solution)/shard_map/col_partial/pallas_call | solution.py:202
  99.3 22.4 %all_to_all.11.part_ref = bf16[16,4,16,256]{3,2,1,0:T(8,128)(2,1)S(1)} all-to-all(bf16[16,4,16,256]{3,2,1,0:T(8,128)(2,1)S(1)} %col_partial.1), channel_id=1, replica_groups=mesh['left'=16,'right'=8] {'left'}, dimensions={0} | all-to-all | bytes 1048576 | tf_op jit(solution)/shard_map/all_to_all | solution.py:270
  121.7 0.9 finish.1
  (32 shorter events, 0.4 us)
Async XLA Ops:
  0.6 23.6 %copy-start.4 = (s32[8]{0:T(128)S(1)}, s32[8]{0:T(128)}, u32[]{:S(2)}) copy-start(s32[8]{0:T(128)} %constant.104.clone) | copy-start | bytes 100
  0.6 23.5 %copy-start.2 = (s32[16,8]{0,1:T(8,128)S(1)}, s32[16,8]{0,1:T(8,128)}, u32[]{:S(2)}) copy-start(s32[16,8]{0,1:T(8,128)} %param.10) | copy-start | bytes 1540
  22.1 4.3 %collective-permute-start = (bf16[8,256,256]{2,1,0:T(8,128)(2,1)S(1)}, bf16[8,256,256]{2,1,0:T(8,128)(2,1)S(1)}, u32[]{:S(2)}, u32[]{:S(2)}) collective-permute-start(bf16[8,256,256]{2,1,0:T(8,128)(2,1)S(1)} %all_to_all.10), channel_id=1, source_target_pairs={{0,8},{8,0},{16,24},{24,16},{32,40},{40,32},{48,56},{56,48},{64,72... | collective-permute-start | bytes 3145736 | tf_op jit(solution)/shard_map/ppermute | solution.py:243
  38.0 13.5 %collective-permute-start.1 = (bf16[4,176,256]{2,1,0:T(8,128)(2,1)S(1)}, bf16[4,176,256]{2,1,0:T(8,128)(2,1)S(1)}, u32[]{:S(2)}, u32[]{:S(2)}) collective-permute-start(bf16[4,176,256]{2,1,0:T(8,128)(2,1)S(1)} %get-tuple-element.31), channel_id=1, source_target_pairs={{0,1},{1,0},{2,3},{3,2},{4,5},{5,4},{6,7},{7,6},{8,9},{9,8},{10,11... | collective-permute-start | bytes 1081352 | tf_op jit(solution)/shard_map/ppermute | solution.py:22
  39.3 12.3 %collective-permute-start.2 = (bf16[4,176,256]{2,1,0:T(8,128)(2,1)S(1)}, bf16[4,176,256]{2,1,0:T(8,128)(2,1)S(1)}, u32[]{:S(2)}, u32[]{:S(2)}) collective-permute-start(bf16[4,176,256]{2,1,0:T(8,128)(2,1)S(1)} %get-tuple-element.33), channel_id=1, source_target_pairs={{0,3},{1,2},{2,1},{3,0},{4,7},{5,6},{6,5},{7,4},{8,11},{9,10},{10,... | collective-permute-start | bytes 1081352 | tf_op jit(solution)/shard_map/ppermute | solution.py:22
  41.1 10.4 %collective-permute-start.3 = (bf16[4,160,256]{2,1,0:T(8,128)(2,1)S(1)}, bf16[4,160,256]{2,1,0:T(8,128)(2,1)S(1)}, u32[]{:S(2)}, u32[]{:S(2)}) collective-permute-start(bf16[4,160,256]{2,1,0:T(8,128)(2,1)S(1)} %get-tuple-element.35), channel_id=1, source_target_pairs={{0,4},{1,5},{2,6},{3,7},{4,0},{5,1},{6,2},{7,3},{8,12},{9,13},{10,... | collective-permute-start | bytes 983048 | tf_op jit(solution)/shard_map/ppermute | solution.py:22
  51.5 14.6 %copy-start = (bf16[16,256,256]{2,1,0:T(8,128)(2,1)S(1)}, bf16[16,256,256]{2,1,0:T(8,128)(2,1)}, u32[]{:S(2)}) copy-start(bf16[16,256,256]{2,1,0:T(8,128)(2,1)} %refs_0_.1) | copy-start | bytes 6291460
  51.7 8.1 %collective-permute-start.4 = (bf16[2,176,256]{2,1,0:T(8,128)(2,1)S(1)}, bf16[2,176,256]{2,1,0:T(8,128)(2,1)S(1)}, u32[]{:S(2)}, u32[]{:S(2)}) collective-permute-start(bf16[2,176,256]{2,1,0:T(8,128)(2,1)S(1)} %get-tuple-element.37), channel_id=1, source_target_pairs={{0,3},{1,2},{2,1},{3,0},{4,7},{5,6},{6,5},{7,4},{8,11},{9,10},{10,... | collective-permute-start | bytes 540680 | tf_op jit(solution)/shard_map/ppermute | solution.py:22
  52.7 7.1 %collective-permute-start.5 = (bf16[2,176,256]{2,1,0:T(8,128)(2,1)S(1)}, bf16[2,176,256]{2,1,0:T(8,128)(2,1)S(1)}, u32[]{:S(2)}, u32[]{:S(2)}) collective-permute-start(bf16[2,176,256]{2,1,0:T(8,128)(2,1)S(1)} %get-tuple-element.39), channel_id=1, source_target_pairs={{0,4},{1,5},{2,6},{3,7},{4,0},{5,1},{6,2},{7,3},{8,12},{9,13},{10,... | collective-permute-start | bytes 540680 | tf_op jit(solution)/shard_map/ppermute | solution.py:22
  55.3 4.5 %collective-permute-start.6 = (bf16[2,160,256]{2,1,0:T(8,128)(2,1)S(1)}, bf16[2,160,256]{2,1,0:T(8,128)(2,1)S(1)}, u32[]{:S(2)}, u32[]{:S(2)}) collective-permute-start(bf16[2,160,256]{2,1,0:T(8,128)(2,1)S(1)} %get-tuple-element.41), channel_id=1, source_target_pairs={{0,1},{1,0},{2,3},{3,2},{4,5},{5,4},{6,7},{7,6},{8,9},{9,8},{10,11... | collective-permute-start | bytes 491528 | tf_op jit(solution)/shard_map/ppermute | solution.py:22
  59.9 6.3 %collective-permute-start.7 = (bf16[1,176,256]{2,1,0:T(8,128)(2,1)S(1)}, bf16[1,176,256]{2,1,0:T(8,128)(2,1)S(1)}, u32[]{:S(2)}, u32[]{:S(2)}) collective-permute-start(bf16[1,176,256]{2,1,0:T(8,128)(2,1)S(1)} %get-tuple-element.45), channel_id=1, source_target_pairs={{0,4},{1,5},{2,6},{3,7},{4,0},{5,1},{6,2},{7,3},{8,12},{9,13},{10,... | collective-permute-start | bytes 270344 | tf_op jit(solution)/shard_map/ppermute | solution.py:22
  61.6 4.5 %collective-permute-start.8 = (bf16[1,176,256]{2,1,0:T(8,128)(2,1)S(1)}, bf16[1,176,256]{2,1,0:T(8,128)(2,1)S(1)}, u32[]{:S(2)}, u32[]{:S(2)}) collective-permute-start(bf16[1,176,256]{2,1,0:T(8,128)(2,1)S(1)} %get-tuple-element.46), channel_id=1, source_target_pairs={{0,1},{1,0},{2,3},{3,2},{4,5},{5,4},{6,7},{7,6},{8,9},{9,8},{10,11... | collective-permute-start | bytes 270344 | tf_op jit(solution)/shard_map/ppermute | solution.py:22
  61.6 4.5 %collective-permute-start.9 = (bf16[1,160,256]{2,1,0:T(8,128)(2,1)S(1)}, bf16[1,160,256]{2,1,0:T(8,128)(2,1)S(1)}, u32[]{:S(2)}, u32[]{:S(2)}) collective-permute-start(bf16[1,160,256]{2,1,0:T(8,128)(2,1)S(1)} %get-tuple-element.47), channel_id=1, source_target_pairs={{0,3},{1,2},{2,1},{3,0},{4,7},{5,6},{6,5},{7,4},{8,11},{9,10},{10,... | collective-permute-start | bytes 245768 | tf_op jit(solution)/shard_map/ppermute | solution.py:22
  66.1 17.7 %copy-start.3 = (s32[4,10]{1,0:T(4,128)S(1)}, s32[4,10]{1,0:T(4,128)}, u32[]{:S(2)}) copy-start(s32[4,10]{1,0:T(4,128)} %param.13) | copy-start | bytes 484
  67.2 6.1 %collective-permute-start.10 = (bf16[1,176,256]{2,1,0:T(8,128)(2,1)S(1)}, bf16[1,176,256]{2,1,0:T(8,128)(2,1)S(1)}, u32[]{:S(2)}, u32[]{:S(2)}) collective-permute-start(bf16[1,176,256]{2,1,0:T(8,128)(2,1)S(1)} %get-tuple-element.49.refs_0_), channel_id=1, source_target_pairs={{0,4},{1,5},{2,6},{3,7},{4,0},{5,1},{6,2},{7,3},{8,12},{9,13},{10,... | collective-permute-start | bytes 270344 | tf_op jit(solution)/shard_map/ppermute | solution.py:22
  68.5 4.8 %collective-permute-start.11 = (bf16[1,176,256]{2,1,0:T(8,128)(2,1)S(1)}, bf16[1,176,256]{2,1,0:T(8,128)(2,1)S(1)}, u32[]{:S(2)}, u32[]{:S(2)}) collective-permute-start(bf16[1,176,256]{2,1,0:T(8,128)(2,1)S(1)} %get-tuple-element.50.refs_2_), channel_id=1, source_target_pairs={{0,1},{1,0},{2,3},{3,2},{4,5},{5,4},{6,7},{7,6},{8,9},{9,8},{10,11... | collective-permute-start | bytes 270344 | tf_op jit(solution)/shard_map/ppermute | solution.py:22
  68.7 4.5 %collective-permute-start.12 = (bf16[1,160,256]{2,1,0:T(8,128)(2,1)S(1)}, bf16[1,160,256]{2,1,0:T(8,128)(2,1)S(1)}, u32[]{:S(2)}, u32[]{:S(2)}) collective-permute-start(bf16[1,160,256]{2,1,0:T(8,128)(2,1)S(1)} %get-tuple-element.51.refs_4_), channel_id=1, source_target_pairs={{0,3},{1,2},{2,1},{3,0},{4,7},{5,6},{6,5},{7,4},{8,11},{9,10},{10,... | collective-permute-start | bytes 245768 | tf_op jit(solution)/shard_map/ppermute | solution.py:22
  73.3 7.7 %collective-permute-start.13 = (bf16[2,176,256]{2,1,0:T(8,128)(2,1)S(1)}, bf16[2,176,256]{2,1,0:T(8,128)(2,1)S(1)}, u32[]{:S(2)}, u32[]{:S(2)}) collective-permute-start(bf16[2,176,256]{2,1,0:T(8,128)(2,1)S(1)} %get-tuple-element.52.refs_0_), channel_id=1, source_target_pairs={{0,3},{1,2},{2,1},{3,0},{4,7},{5,6},{6,5},{7,4},{8,11},{9,10},{10,... | collective-permute-start | bytes 540680 | tf_op jit(solution)/shard_map/ppermute | solution.py:22
  75.2 5.8 %collective-permute-start.14 = (bf16[2,176,256]{2,1,0:T(8,128)(2,1)S(1)}, bf16[2,176,256]{2,1,0:T(8,128)(2,1)S(1)}, u32[]{:S(2)}, u32[]{:S(2)}) collective-permute-start(bf16[2,176,256]{2,1,0:T(8,128)(2,1)S(1)} %get-tuple-element.53.refs_2_), channel_id=1, source_target_pairs={{0,4},{1,5},{2,6},{3,7},{4,0},{5,1},{6,2},{7,3},{8,12},{9,13},{10,... | collective-permute-start | bytes 540680 | tf_op jit(solution)/shard_map/ppermute | solution.py:22
  76.8 4.2 %collective-permute-start.15 = (bf16[2,160,256]{2,1,0:T(8,128)(2,1)S(1)}, bf16[2,160,256]{2,1,0:T(8,128)(2,1)S(1)}, u32[]{:S(2)}, u32[]{:S(2)}) collective-permute-start(bf16[2,160,256]{2,1,0:T(8,128)(2,1)S(1)} %get-tuple-element.54.refs_4_), channel_id=1, source_target_pairs={{0,1},{1,0},{2,3},{3,2},{4,5},{5,4},{6,7},{7,6},{8,9},{9,8},{10,11... | collective-permute-start | bytes 491528 | tf_op jit(solution)/shard_map/ppermute | solution.py:22
  81.1 10.4 %collective-permute-start.16 = (bf16[4,176,256]{2,1,0:T(8,128)(2,1)S(1)}, bf16[4,176,256]{2,1,0:T(8,128)(2,1)S(1)}, u32[]{:S(2)}, u32[]{:S(2)}) collective-permute-start(bf16[4,176,256]{2,1,0:T(8,128)(2,1)S(1)} %get-tuple-element.55.refs_0_), channel_id=1, source_target_pairs={{0,1},{1,0},{2,3},{3,2},{4,5},{5,4},{6,7},{7,6},{8,9},{9,8},{10,11... | collective-permute-start | bytes 1081352 | tf_op jit(solution)/shard_map/ppermute | solution.py:22
  81.2 10.3 %collective-permute-start.17 = (bf16[4,176,256]{2,1,0:T(8,128)(2,1)S(1)}, bf16[4,176,256]{2,1,0:T(8,128)(2,1)S(1)}, u32[]{:S(2)}, u32[]{:S(2)}) collective-permute-start(bf16[4,176,256]{2,1,0:T(8,128)(2,1)S(1)} %get-tuple-element.56.refs_2_), channel_id=1, source_target_pairs={{0,3},{1,2},{2,1},{3,0},{4,7},{5,6},{6,5},{7,4},{8,11},{9,10},{10,... | collective-permute-start | bytes 1081352 | tf_op jit(solution)/shard_map/ppermute | solution.py:22
  82.1 9.4 %collective-permute-start.18 = (bf16[4,160,256]{2,1,0:T(8,128)(2,1)S(1)}, bf16[4,160,256]{2,1,0:T(8,128)(2,1)S(1)}, u32[]{:S(2)}, u32[]{:S(2)}) collective-permute-start(bf16[4,160,256]{2,1,0:T(8,128)(2,1)S(1)} %get-tuple-element.57.refs_4_), channel_id=1, source_target_pairs={{0,4},{1,5},{2,6},{3,7},{4,0},{5,1},{6,2},{7,3},{8,12},{9,13},{10,... | collective-permute-start | bytes 983048 | tf_op jit(solution)/shard_map/ppermute | solution.py:22
  83.8 37.9 %copy-start.1 = (bf16[4,256,256]{2,1,0:T(8,128)(2,1)S(1)}, bf16[4,256,256]{2,1,0:T(8,128)(2,1)}, u32[]{:S(2)}) copy-start(bf16[4,256,256]{2,1,0:T(8,128)(2,1)} %proj_ref.1) | copy-start | bytes 1572868

commit v3 on v2

--- a/solution.py
+++ b/solution.py
@@ -10,6 +10,7 @@
 SIZE = 256
 COUNT = 2
 FLAT = COUNT * SIZE
+DEPTH = 4
 FLIPS = (1, 3, 4)
 ORDERS = ((0, 1, 2), (1, 2, 0), (2, 0, 1))
 CUTS = (0, 176, 352, FLAT)
@@ -31,10 +32,33 @@
     return pl.CostEstimate(flops=flops, bytes_accessed=2 * elements, transcendentals=0)
 
 
-def row_kernel(slot_ref, peer_ref, held_ref, edge_ref, *out_refs):
-    step = pl.program_id(0)
-    place = pl.num_programs(0) - 1 - step
+def row_kernel(slot_ref, peer_ref, held_ref, edge_hbm, *refs):
+    *out_refs, ring, sems = refs
+    step, steps, depth = pl.program_id(0), pl.num_programs(0), ring.shape[0]
+    place = steps - 1 - step
     first = peer_ref[step] * COUNT
+
+    def fetch(later):
+        slot = later % depth
+        return [
+            pltpu.make_async_copy(edge_hbm.at[peer_ref[later] * COUNT + i], ring.at[slot, i], sems.at[slot, i])
+            for i in range(COUNT)
+        ]
+
+    @pl.when(step == 0)
+    def _():
+        for later in range(depth - 1):
+            for copy in fetch(later):
+                copy.start()
+
+    @pl.when(step + depth - 1 < steps)
+    def _():
+        for copy in fetch(step + depth - 1):
+            copy.start()
+
+    for copy in fetch(step):
+        copy.wait()
+    edge_ref = ring.at[step % depth]
     values = []
     for sector in range(COUNT):
         total = jnp.dot(held_ref[slot_ref[first + sector, 0]], edge_ref[sector, 0], preferred_element_type=F32)
@@ -42,7 +66,7 @@
             total += jnp.dot(
                 held_ref[slot_ref[first + sector, entry]], edge_ref[sector, entry], preferred_element_type=F32
             )
-        values.append(total)
+        values.append(total.T)
     flat = jnp.concatenate(values, axis=0)
     for part, order in enumerate(ORDERS):
         index = place_of(place, order)
@@ -71,11 +95,12 @@
         grid_spec=pltpu.PrefetchScalarGridSpec(
             num_scalar_prefetch=2,
             grid=(steps,),
-            in_specs=[
-                VMEM,
-                pl.BlockSpec((COUNT, entries, SIZE, SIZE), lambda s, slots, peers: (peers[s], 0, 0, 0)),
+            in_specs=[VMEM, pl.BlockSpec(memory_space=pl.ANY)],
+            out_specs=tuple(VMEM for _ in outs),
+            scratch_shapes=[
+                pltpu.VMEM((DEPTH, COUNT, entries, SIZE, SIZE), BF16),
+                pltpu.SemaphoreType.DMA((DEPTH, COUNT)),
             ],
-            out_specs=tuple(VMEM for _ in outs),
         ),
         compiler_params=pltpu.CompilerParams(vmem_limit_bytes=24 * 2**20),
         cost_estimate=cost(2 * steps * COUNT * entries * SIZE**3, steps * COUNT * entries * SIZE**2),
@@ -110,41 +135,61 @@
     )(*args)
 
 
-def absorb_kernel(proj_ref, *refs):
-    keep_refs, came_refs, out_ref, part_refs = refs[:3], refs[3:6], refs[6], refs[7:]
-    pieces = [keep[0] + came[0].astype(F32) for keep, came in zip(keep_refs, came_refs)]
-    total = jnp.concatenate(pieces, axis=0).astype(BF16)
-    values = []
+def meet_kernel(*refs):
+    for part in range(3):
+        keep_ref, came_ref, out_ref = refs[2 * part], refs[2 * part + 1], refs[6 + part]
+        out_ref[...] = (keep_ref[...] + came_ref[...].astype(F32)).astype(BF16)
+
+
+def meet(keeps, came):
+    args = [value for pair in zip(keeps, came) for value in pair]
+    return pl.pallas_call(
+        meet_kernel,
+        out_shape=tuple(jax.ShapeDtypeStruct(value.shape, BF16) for value in keeps),
+        in_specs=[VMEM] * 6,
+        out_specs=tuple(VMEM for _ in range(3)),
+        compiler_params=SMALL,
+        cost_estimate=cost(2 * FLAT * SIZE, 8 * FLAT * SIZE),
+        name="meet",
+    )(*args)
+
+
+def absorb_kernel(index_ref, proj_ref, *refs):
+    ours_refs, came_refs, out_ref, part_refs = refs[:3], refs[3:6], refs[6], refs[7:]
+    mine = []
+    for part, order in enumerate(ORDERS):
+        low, high = CUTS[part], CUTS[part + 1]
+        for place in range(2):
+            first = (index_ref[0] ^ (place * FLIPS[order[2]])) * COUNT
+            total = (ours_refs[part][place].astype(F32) + came_refs[part][1 - place].astype(F32)).astype(BF16)
+            pieces = []
+            for sector in range(COUNT):
+                start, stop = max(low, sector * SIZE), min(high, (sector + 1) * SIZE)
+                if start < stop:
+                    pieces.append(
+                        jnp.dot(total[start - low : stop - low], proj_ref[first + sector], preferred_element_type=F32)
+                    )
+            value = jnp.concatenate(pieces, axis=0).astype(BF16)
+            part_refs[part][place] = value
+            if place == 0:
+                mine.append(value)
+    flat = jnp.concatenate(mine, axis=0)
     for sector in range(COUNT):
-        value = lax.dot_general(
-            proj_ref[sector],
-            total[sector * SIZE : (sector + 1) * SIZE],
-            (((0,), (0,)), ((), ())),
-            preferred_element_type=F32,
-        ).astype(BF16)
-        out_ref[sector] = value
-        values.append(value)
-    flat = jnp.concatenate(values, axis=0)
-    for part, part_ref in enumerate(part_refs):
-        part_ref[0] = flat[CUTS[part] : CUTS[part + 1]]
-
-
-def absorb(index, keeps, came, proj_row):
+        out_ref[sector] = flat[sector * SIZE : (sector + 1) * SIZE].T
+
+
+def absorb(index, ours, came, proj_row):
     outs = [jax.ShapeDtypeStruct((COUNT, SIZE, SIZE), BF16)]
-    outs += [jax.ShapeDtypeStruct((1, length, SIZE), BF16) for length in LENGTHS]
-    return pl.pallas_call(
-        lambda index_ref, *refs: absorb_kernel(*refs),
+    outs += [jax.ShapeDtypeStruct((2, length, SIZE), BF16) for length in LENGTHS]
+    return pl.pallas_call(
+        absorb_kernel,
         out_shape=tuple(outs),
-        grid_spec=pltpu.PrefetchScalarGridSpec(
-            num_scalar_prefetch=1,
-            grid=(1,),
-            in_specs=[pl.BlockSpec((COUNT, SIZE, SIZE), lambda s, index: (index[0], 0, 0))] + [VMEM] * 6,
-            out_specs=tuple(VMEM for _ in outs),
-        ),
-        compiler_params=SMALL,
-        cost_estimate=cost(2 * COUNT * SIZE**3, 6 * FLAT * SIZE),
+        in_specs=[pl.BlockSpec(memory_space=pltpu.SMEM)] + [VMEM] * 7,
+        out_specs=tuple(VMEM for _ in outs),
+        compiler_params=SMALL,
+        cost_estimate=cost(4 * COUNT * SIZE**3, 10 * FLAT * SIZE),
         name="absorb",
-    )(index, proj_row, *keeps, *came)
+    )(index, proj_row, *ours, *came)
 
 
 def double_kernel(*refs):
@@ -170,29 +215,35 @@
 
 
 def col_kernel(slot_ref, *refs):
-    piece_refs, (edge_ref, out_ref, held, sems) = refs[:6], refs[6:]
+    piece_refs, (edge_hbm, out_ref, held, edge_ref, edge_sems) = refs[:6], refs[6:]
     step = pl.program_id(0)
+
+    def fetch(later):
+        return pltpu.make_async_copy(edge_hbm.at[later], edge_ref.at[later], edge_sems.at[later])
 
     @pl.when(step == 0)
     def _():
-        copies = []
+        for later in range(edge_ref.shape[0]):
+            fetch(later).start()
         for part, order in enumerate(ORDERS):
             for place in range(8):
                 index = place_of(place, order)
-                source = piece_refs[2 * part + index // 4].at[index % 4]
-                target = held.at[pl.ds(place * FLAT + CUTS[part], LENGTHS[part])]
-                copies.append(pltpu.make_async_copy(source, target, sems.at[part * 8 + place]))
-        for copy in copies:
-            copy.start()
-        for copy in copies:
-            copy.wait()
+                start = place * FLAT + CUTS[part]
+                held[start : start + LENGTHS[part]] = piece_refs[2 * part + index // 4][index % 4]
+
+    fetch(step).wait()
 
     def block(entry):
         return held[pl.ds(pl.multiple_of(slot_ref[step, entry] * SIZE, SIZE), SIZE)]
 
-    total = jnp.dot(edge_ref[0, 0], block(0), preferred_element_type=F32)
+    def term(entry):
+        return lax.dot_general(
+            edge_ref[step, entry], block(entry), (((1,), (1,)), ((), ())), preferred_element_type=F32
+        )
+
+    total = term(0)
     for entry in range(1, edge_ref.shape[1]):
-        total += jnp.dot(edge_ref[0, entry], block(entry), preferred_element_type=F32)
+        total += term(entry)
     out_ref[:, 0] = total.astype(BF16).reshape(out_ref.shape[0], out_ref.shape[2], SIZE)
 
 
@@ -205,9 +256,13 @@
         grid_spec=pltpu.PrefetchScalarGridSpec(
             num_scalar_prefetch=1,
             grid=(sectors,),
-            in_specs=[VMEM] * 6 + [pl.BlockSpec((1, entries, SIZE, SIZE), lambda g, s: (g, 0, 0, 0))],
+            in_specs=[VMEM] * 6 + [pl.BlockSpec(memory_space=pl.ANY)],
             out_specs=pl.BlockSpec((pieces, 1, piece, SIZE), lambda g, s: (0, g, 0, 0)),
-            scratch_shapes=[pltpu.VMEM((8 * FLAT, SIZE), BF16), pltpu.SemaphoreType.DMA((24,))],
+            scratch_shapes=[
+                pltpu.VMEM((8 * FLAT, SIZE), BF16),
+                pltpu.VMEM(edge_col.shape, BF16),
+                pltpu.SemaphoreType.DMA((sectors,)),
+            ],
         ),
         compiler_params=pltpu.CompilerParams(vmem_limit_bytes=24 * 2**20),
         cost_estimate=cost(2 * sectors * entries * SIZE**3, sectors * entries * SIZE**2),
@@ -248,14 +303,13 @@
     offsets = [p * FLIPS[0] ^ q * FLIPS[1] ^ z * FLIPS[2] for p in range(2) for q in range(2) for z in range(2)]
     peers = jnp.bitwise_xor(right, jnp.array(offsets[::-1], jnp.int32))
     outs = row_partial(slots, peers, held, edge_row)
-    for phase in range(3):
+    for phase in range(2):
         came = [flip(outs[2 * part], ORDERS[part][phase], rights) for part in range(3)]
-        keeps = outs[1::2]
-        if phase < 2:
-            outs = halve(keeps, came)
-    absorbed, *parts = absorb(jnp.reshape(right, (1,)).astype(jnp.int32), keeps, came, proj_row)
-
-    for phase in range(3):
+        outs = halve(outs[1::2], came) if phase == 0 else meet(outs[1::2], came)
+    came = [flip(outs[part], ORDERS[part][2], rights) for part in range(3)]
+    absorbed, *parts = absorb(jnp.reshape(right, (1,)).astype(jnp.int32), outs, came, proj_row)
+
+    for phase in range(1, 3):
         came = [flip(parts[part], ORDERS[part][2 - phase], rights) for part in range(3)]
         if phase < 2:
             parts = double(parts, came)

time: 123 us -> 110 us (0.89)
  Pallas kernels: 21.4 us -> 16.3 us
  starting transfers between devices: 25.2 us -> 21 us
  waiting for transfers between devices: 31 us -> 28.1 us
    ppermute x18 -> x15, starting transfers between devices: 23.2 us -> 19 us  [flip(): lax.ppermute(value, 'right', [(i, i ^ FLIPS[pairing]) for i in range(size)])]
    pallas_call x1, Pallas kernels: 7.81 us -> 4.18 us  [col_partial(): pl.pallas_call(col_kernel, out_shape=jax.ShapeDtypeStruct((pieces, sector...]
    ppermute x18 -> x15, waiting for transfers between devices: 28.8 us -> 25.9 us  [flip(): lax.ppermute(value, 'right', [(i, i ^ FLIPS[pairing]) for i in range(size)])]
    pallas_call x1, Pallas kernels: 11.4 us -> 9.83 us  [row_partial(): pl.pallas_call(row_kernel, out_shape=tuple(outs), grid_spec=pltpu.Prefetc...]
  transfers between devices with their start and end apart: 19 -> 16, of which waited for: 7 -> 7; matrix products, arithmetic and copies ran while one was open for 0% -> 0% of each run, Pallas kernels for 0% -> 0%
where the time goes in v3:
time: 110 us
  blocking collectives  42.5 us (39%)
  waiting for transfers between devices  28.1 us (26%)
  starting transfers between devices  21 us (19%)
  Pallas kernels  16.3 us (15%)
    ppermute x15, waiting for transfers between devices, flip(): lax.ppermute(value, 'right', [(i, i ^ FLIPS[pairing]) for i in range(size)])  25.9 us
    all_to_all x1, blocking collectives, body(): col_parts = lax.all_to_all(partial_cols, 'left', 0, 0, tiled=True)  22 us
    all_to_all x1, blocking collectives, body(): lax.all_to_all(jnp.broadcast_to(corner, (lefts // 2, SIZE, SIZE)), 'left'...  20.5 us
    ppermute x15, starting transfers between devices, flip(): lax.ppermute(value, 'right', [(i, i ^ FLIPS[pairing]) for i in range(size)])  19 us
    pallas_call x1, Pallas kernels, row_partial(): pl.pallas_call(row_kernel, out_shape=tuple(outs), grid_spec=pltpu.Prefetc...  9.83 us
    pallas_call x1, Pallas kernels, col_partial(): pl.pallas_call(col_kernel, out_shape=jax.ShapeDtypeStruct((pieces, sector...  4.18 us
  transfers between devices with their start and end apart: 16, of which 7 were waited for; matrix products, arithmetic and copies ran while one was open for 0% of the time, Pallas kernels for 0%

profile of v3, /device:TPU:1, one launch (start us, length us, event | category | flops | bytes accessed | tf_op | source)
XLA Modules:
  0.0 109.9 jit_solution(3633626175481554950)
XLA Ops:
  0.7 1.0 broadcast_in_dim.12
  1.6 20.5 %all_to_all.10 = bf16[8,256,256]{2,1,0:T(8,128)(2,1)S(1)} all-to-all(bf16[8,256,256]{2,1,0:T(8,128)(2,1)S(1)} %broadcast_in_dim.12), channel_id=1, replica_groups={{0,16,32,48,64,80,96,112},{8,24,40,56,72,88,104,120},{1,17,33,49,65,81,..., dimensions={0} | all-to-all | bytes 2097152 | tf_op jit(solution)/shard_map/all_to_all | solution.py:295
  22.1 2.0 %collective-permute-start = (bf16[8,256,256]{2,1,0:T(8,128)(2,1)S(1)}, bf16[8,256,256]{2,1,0:T(8,128)(2,1)S(1)}, u32[]{:S(2)}, u32[]{:S(2)}) collective-permute-start(bf16[8,256,256]{2,1,0:T(8,128)(2,1)S(1)} %all_to_all.10), channel_id=1, source_target_pairs={{0,8},{8,0},{16,24},{24,16},{32,40},{40,32},{48,56},{56,48},{64,72... | collective-permute-start | bytes 3145736 | tf_op jit(solution)/shard_map/ppermute | solution.py:298
  24.1 0.1 copy.10
  24.2 2.2 %collective-permute-done = bf16[8,256,256]{2,1,0:T(8,128)(2,1)S(1)} collective-permute-done((bf16[8,256,256]{2,1,0:T(8,128)(2,1)S(1)}, bf16[8,256,256]{2,1,0:T(8,128)(2,1)S(1)}, u32[]{:S(2)}, u32[]{:S(2)}) %collective-permute-start) | collective-permute-done | bytes 1048608 | tf_op jit(solution)/shard_map/ppermute | solution.py:298
  26.4 0.2 pad_maximum_fusion.held_ref
  26.6 9.8 %row_partial.1 = (bf16[4,176,256]{2,1,0:T(8,128)(2,1)S(1)}, f32[4,176,256]{2,1,0:T(8,128)S(1)}, bf16[4,176,256]{2,1,0:T(8,128)(2,1)S(1)}, f32[4,176,256]{2,1,0:T...) custom-call(s32[16,8]{1,0:T(8,128)S(1)} %fusion.1.slot_ref, s32[8]{0:T(128)S(1)} %broadcast_xor_fusion.peer_ref, ...), custom_call_target="tpu_custom_call" | custom-call | flops 4294967296 | bytes 16777216 | tf_op jit(solution)/shard_map/row_partial/pallas_call | solution.py:92
  36.4 1.3 %collective-permute-start.1 = (bf16[4,176,256]{2,1,0:T(8,128)(2,1)S(1)}, bf16[4,176,256]{2,1,0:T(8,128)(2,1)S(1)}, u32[]{:S(2)}, u32[]{:S(2)}) collective-permute-start(bf16[4,176,256]{2,1,0:T(8,128)(2,1)S(1)} %get-tuple-element.25), channel_id=1, source_target_pairs={{0,1},{1,0},{2,3},{3,2},{4,5},{5,4},{6,7},{7,6},{8,9},{9,8},{10,11... | collective-permute-start | bytes 1081352 | tf_op jit(solution)/shard_map/ppermute | solution.py:23
  37.7 1.8 %collective-permute-start.2 = (bf16[4,176,256]{2,1,0:T(8,128)(2,1)S(1)}, bf16[4,176,256]{2,1,0:T(8,128)(2,1)S(1)}, u32[]{:S(2)}, u32[]{:S(2)}) collective-permute-start(bf16[4,176,256]{2,1,0:T(8,128)(2,1)S(1)} %get-tuple-element.27), channel_id=1, source_target_pairs={{0,3},{1,2},{2,1},{3,0},{4,7},{5,6},{6,5},{7,4},{8,11},{9,10},{10,... | collective-permute-start | bytes 1081352 | tf_op jit(solution)/shard_map/ppermute | solution.py:23
  39.5 3.3 %collective-permute-start.3 = (bf16[4,160,256]{2,1,0:T(8,128)(2,1)S(1)}, bf16[4,160,256]{2,1,0:T(8,128)(2,1)S(1)}, u32[]{:S(2)}, u32[]{:S(2)}) collective-permute-start(bf16[4,160,256]{2,1,0:T(8,128)(2,1)S(1)} %get-tuple-element.29), channel_id=1, source_target_pairs={{0,4},{1,5},{2,6},{3,7},{4,0},{5,1},{6,2},{7,3},{8,12},{9,13},{10,... | collective-permute-start | bytes 983048 | tf_op jit(solution)/shard_map/ppermute | solution.py:23
  42.8 7.2 %collective-permute-done.3.refs_5_ = bf16[4,160,256]{2,1,0:T(8,128)(2,1)S(1)} collective-permute-done((bf16[4,160,256]{2,1,0:T(8,128)(2,1)S(1)}, bf16[4,160,256]{2,1,0:T(8,128)(2,1)S(1)}, u32[]{:S(2)}, u32[]{:S(2)}) %collective-permute-start.3) | collective-permute-done | bytes 327712 | tf_op jit(solution)/shard_map/ppermute | solution.py:23
  50.0 0.2 halve.1
  50.2 0.9 collective-permute-start.4
  51.1 2.6 %collective-permute-start.5 = (bf16[2,176,256]{2,1,0:T(8,128)(2,1)S(1)}, bf16[2,176,256]{2,1,0:T(8,128)(2,1)S(1)}, u32[]{:S(2)}, u32[]{:S(2)}) collective-permute-start(bf16[2,176,256]{2,1,0:T(8,128)(2,1)S(1)} %get-tuple-element.33), channel_id=1, source_target_pairs={{0,4},{1,5},{2,6},{3,7},{4,0},{5,1},{6,2},{7,3},{8,12},{9,13},{10,... | collective-permute-start | bytes 540680 | tf_op jit(solution)/shard_map/ppermute | solution.py:23
  53.8 4.5 %collective-permute-done.6.refs_5_ = bf16[2,160,256]{2,1,0:T(8,128)(2,1)S(1)} collective-permute-done((bf16[2,160,256]{2,1,0:T(8,128)(2,1)S(1)}, bf16[2,160,256]{2,1,0:T(8,128)(2,1)S(1)}, u32[]{:S(2)}, u32[]{:S(2)}) %collective-permute-start.6) | collective-permute-done | bytes 163872 | tf_op jit(solution)/shard_map/ppermute | solution.py:23
  58.2 0.1 meet.1
  58.3 1.8 %collective-permute-start.7 = (bf16[2,176,256]{2,1,0:T(8,128)(2,1)S(1)}, bf16[2,176,256]{2,1,0:T(8,128)(2,1)S(1)}, u32[]{:S(2)}, u32[]{:S(2)}) collective-permute-start(bf16[2,176,256]{2,1,0:T(8,128)(2,1)S(1)} %get-tuple-element.36.refs_0_), channel_id=1, source_target_pairs={{0,4},{1,5},{2,6},{3,7},{4,0},{5,1},{6,2},{7,3},{8,12},{9,13},{10,... | collective-permute-start | bytes 540680 | tf_op jit(solution)/shard_map/ppermute | solution.py:23
  60.1 1.8 %collective-permute-start.9 = (bf16[2,160,256]{2,1,0:T(8,128)(2,1)S(1)}, bf16[2,160,256]{2,1,0:T(8,128)(2,1)S(1)}, u32[]{:S(2)}, u32[]{:S(2)}) collective-permute-start(bf16[2,160,256]{2,1,0:T(8,128)(2,1)S(1)} %get-tuple-element.38.refs_2_), channel_id=1, source_target_pairs={{0,3},{1,2},{2,1},{3,0},{4,7},{5,6},{6,5},{7,4},{8,11},{9,10},{10,... | collective-permute-start | bytes 491528 | tf_op jit(solution)/shard_map/ppermute | solution.py:23
  61.9 3.5 %collective-permute-done.9.refs_5_ = bf16[2,160,256]{2,1,0:T(8,128)(2,1)S(1)} collective-permute-done((bf16[2,160,256]{2,1,0:T(8,128)(2,1)S(1)}, bf16[2,160,256]{2,1,0:T(8,128)(2,1)S(1)}, u32[]{:S(2)}, u32[]{:S(2)}) %collective-permute-start.9) | collective-permute-done | bytes 163872 | tf_op jit(solution)/shard_map/ppermute | solution.py:23
  65.5 1.1 absorb.1
  66.6 1.8 %collective-permute-start.10 = (bf16[2,176,256]{2,1,0:T(8,128)(2,1)S(1)}, bf16[2,176,256]{2,1,0:T(8,128)(2,1)S(1)}, u32[]{:S(2)}, u32[]{:S(2)}) collective-permute-start(bf16[2,176,256]{2,1,0:T(8,128)(2,1)S(1)} %get-tuple-element.40.refs_0_), channel_id=1, source_target_pairs={{0,3},{1,2},{2,1},{3,0},{4,7},{5,6},{6,5},{7,4},{8,11},{9,10},{10,... | collective-permute-start | bytes 540680 | tf_op jit(solution)/shard_map/ppermute | solution.py:23
  68.4 1.3 %collective-permute-start.11 = (bf16[2,176,256]{2,1,0:T(8,128)(2,1)S(1)}, bf16[2,176,256]{2,1,0:T(8,128)(2,1)S(1)}, u32[]{:S(2)}, u32[]{:S(2)}) collective-permute-start(bf16[2,176,256]{2,1,0:T(8,128)(2,1)S(1)} %get-tuple-element.41.refs_2_), channel_id=1, source_target_pairs={{0,4},{1,5},{2,6},{3,7},{4,0},{5,1},{6,2},{7,3},{8,12},{9,13},{10,... | collective-permute-start | bytes 540680 | tf_op jit(solution)/shard_map/ppermute | solution.py:23
  69.7 4.2 %collective-permute-done.12.refs_5_ = bf16[2,160,256]{2,1,0:T(8,128)(2,1)S(1)} collective-permute-done((bf16[2,160,256]{2,1,0:T(8,128)(2,1)S(1)}, bf16[2,160,256]{2,1,0:T(8,128)(2,1)S(1)}, u32[]{:S(2)}, u32[]{:S(2)}) %collective-permute-start.12) | collective-permute-done | bytes 163872 | tf_op jit(solution)/shard_map/ppermute | solution.py:23
  73.9 0.4 collective-permute-done.11.refs_3_
  74.3 0.1 double.1
  74.3 0.1 collective-permute-start.13
  74.4 0.9 collective-permute-start.14
  75.3 1.3 %collective-permute-start.15 = (bf16[4,160,256]{2,1,0:T(8,128)(2,1)S(1)}, bf16[4,160,256]{2,1,0:T(8,128)(2,1)S(1)}, u32[]{:S(2)}, u32[]{:S(2)}) collective-permute-start(bf16[4,160,256]{2,1,0:T(8,128)(2,1)S(1)} %get-tuple-element.45.refs_4_), channel_id=1, source_target_pairs={{0,4},{1,5},{2,6},{3,7},{4,0},{5,1},{6,2},{7,3},{8,12},{9,13},{10,... | collective-permute-start | bytes 983048 | tf_op jit(solution)/shard_map/ppermute | solution.py:23
  76.7 6.2 %collective-permute-done.15.refs_5_ = bf16[4,160,256]{2,1,0:T(8,128)(2,1)S(1)} collective-permute-done((bf16[4,160,256]{2,1,0:T(8,128)(2,1)S(1)}, bf16[4,160,256]{2,1,0:T(8,128)(2,1)S(1)}, u32[]{:S(2)}, u32[]{:S(2)}) %collective-permute-start.15) | collective-permute-done | bytes 327712 | tf_op jit(solution)/shard_map/ppermute | solution.py:23
  82.9 4.2 %col_partial.1 = bf16[16,4,16,256]{3,2,1,0:T(8,128)(2,1)S(1)} custom-call(s32[4,10]{1,0:T(4,128)S(1)} %fusion.14.slot_ref, bf16[4,176,256]{2,1,0:T(8,128)(2,1)S(1)} %get-tuple-element.43.refs_0_, bf16[4,176,256]{2,1,0:T(8,128)(2,1)S(1)} %collective-permute-done.13.refs_1_, bf16[4,176,256]{2,1,0:T(8,128)(2,1)S(1)} %get-tuple-element.44.refs_2_, ...), custom_call_target="tpu_custom_call" | custom-call | flops 1342177280 | bytes 5242880 | tf_op jit(solution)/shard_map/col_partial/pallas_call | solution.py:253
  87.1 22.0 %all_to_all.11.part_ref = bf16[16,4,16,256]{3,2,1,0:T(8,128)(2,1)S(1)} all-to-all(bf16[16,4,16,256]{3,2,1,0:T(8,128)(2,1)S(1)} %col_partial.1), channel_id=1, replica_groups=mesh['left'=16,'right'=8] {'left'}, dimensions={0} | all-to-all | bytes 1048576 | tf_op jit(solution)/shard_map/all_to_all | solution.py:324
  109.1 0.9 finish.1
  (25 shorter events, 0.1 us)
Async XLA Ops:
  0.6 23.6 %copy-start.4 = (s32[8]{0:T(128)S(1)}, s32[8]{0:T(128)}, u32[]{:S(2)}) copy-start(s32[8]{0:T(128)} %constant.104.clone) | copy-start | bytes 100
  0.6 23.5 %copy-start.2 = (s32[16,8]{0,1:T(8,128)S(1)}, s32[16,8]{0,1:T(8,128)}, u32[]{:S(2)}) copy-start(s32[16,8]{0,1:T(8,128)} %param.10) | copy-start | bytes 1540
  22.1 4.3 %collective-permute-start = (bf16[8,256,256]{2,1,0:T(8,128)(2,1)S(1)}, bf16[8,256,256]{2,1,0:T(8,128)(2,1)S(1)}, u32[]{:S(2)}, u32[]{:S(2)}) collective-permute-start(bf16[8,256,256]{2,1,0:T(8,128)(2,1)S(1)} %all_to_all.10), channel_id=1, source_target_pairs={{0,8},{8,0},{16,24},{24,16},{32,40},{40,32},{48,56},{56,48},{64,72... | collective-permute-start | bytes 3145736 | tf_op jit(solution)/shard_map/ppermute | solution.py:298
  36.4 13.6 %collective-permute-start.1 = (bf16[4,176,256]{2,1,0:T(8,128)(2,1)S(1)}, bf16[4,176,256]{2,1,0:T(8,128)(2,1)S(1)}, u32[]{:S(2)}, u32[]{:S(2)}) collective-permute-start(bf16[4,176,256]{2,1,0:T(8,128)(2,1)S(1)} %get-tuple-element.25), channel_id=1, source_target_pairs={{0,1},{1,0},{2,3},{3,2},{4,5},{5,4},{6,7},{7,6},{8,9},{9,8},{10,11... | collective-permute-start | bytes 1081352 | tf_op jit(solution)/shard_map/ppermute | solution.py:23
  37.7 12.3 %collective-permute-start.2 = (bf16[4,176,256]{2,1,0:T(8,128)(2,1)S(1)}, bf16[4,176,256]{2,1,0:T(8,128)(2,1)S(1)}, u32[]{:S(2)}, u32[]{:S(2)}) collective-permute-start(bf16[4,176,256]{2,1,0:T(8,128)(2,1)S(1)} %get-tuple-element.27), channel_id=1, source_target_pairs={{0,3},{1,2},{2,1},{3,0},{4,7},{5,6},{6,5},{7,4},{8,11},{9,10},{10,... | collective-permute-start | bytes 1081352 | tf_op jit(solution)/shard_map/ppermute | solution.py:23
  39.5 10.5 %collective-permute-start.3 = (bf16[4,160,256]{2,1,0:T(8,128)(2,1)S(1)}, bf16[4,160,256]{2,1,0:T(8,128)(2,1)S(1)}, u32[]{:S(2)}, u32[]{:S(2)}) collective-permute-start(bf16[4,160,256]{2,1,0:T(8,128)(2,1)S(1)} %get-tuple-element.29), channel_id=1, source_target_pairs={{0,4},{1,5},{2,6},{3,7},{4,0},{5,1},{6,2},{7,3},{8,12},{9,13},{10,... | collective-permute-start | bytes 983048 | tf_op jit(solution)/shard_map/ppermute | solution.py:23
  50.0 15.5 %copy-start = (bf16[16,256,256]{2,1,0:T(8,128)(2,1)S(1)}, bf16[16,256,256]{2,1,0:T(8,128)(2,1)}, u32[]{:S(2)}) copy-start(bf16[16,256,256]{2,1,0:T(8,128)(2,1)} %proj_ref.2) | copy-start | bytes 6291460
  50.2 8.0 %collective-permute-start.4 = (bf16[2,176,256]{2,1,0:T(8,128)(2,1)S(1)}, bf16[2,176,256]{2,1,0:T(8,128)(2,1)S(1)}, u32[]{:S(2)}, u32[]{:S(2)}) collective-permute-start(bf16[2,176,256]{2,1,0:T(8,128)(2,1)S(1)} %get-tuple-element.31), channel_id=1, source_target_pairs={{0,3},{1,2},{2,1},{3,0},{4,7},{5,6},{6,5},{7,4},{8,11},{9,10},{10,... | collective-permute-start | bytes 540680 | tf_op jit(solution)/shard_map/ppermute | solution.py:23
  51.1 7.1 %collective-permute-start.5 = (bf16[2,176,256]{2,1,0:T(8,128)(2,1)S(1)}, bf16[2,176,256]{2,1,0:T(8,128)(2,1)S(1)}, u32[]{:S(2)}, u32[]{:S(2)}) collective-permute-start(bf16[2,176,256]{2,1,0:T(8,128)(2,1)S(1)} %get-tuple-element.33), channel_id=1, source_target_pairs={{0,4},{1,5},{2,6},{3,7},{4,0},{5,1},{6,2},{7,3},{8,12},{9,13},{10,... | collective-permute-start | bytes 540680 | tf_op jit(solution)/shard_map/ppermute | solution.py:23
  53.7 4.5 %collective-permute-start.6 = (bf16[2,160,256]{2,1,0:T(8,128)(2,1)S(1)}, bf16[2,160,256]{2,1,0:T(8,128)(2,1)S(1)}, u32[]{:S(2)}, u32[]{:S(2)}) collective-permute-start(bf16[2,160,256]{2,1,0:T(8,128)(2,1)S(1)} %get-tuple-element.35), channel_id=1, source_target_pairs={{0,1},{1,0},{2,3},{3,2},{4,5},{5,4},{6,7},{7,6},{8,9},{9,8},{10,11... | collective-permute-start | bytes 491528 | tf_op jit(solution)/shard_map/ppermute | solution.py:23
  58.3 7.1 %collective-permute-start.7 = (bf16[2,176,256]{2,1,0:T(8,128)(2,1)S(1)}, bf16[2,176,256]{2,1,0:T(8,128)(2,1)S(1)}, u32[]{:S(2)}, u32[]{:S(2)}) collective-permute-start(bf16[2,176,256]{2,1,0:T(8,128)(2,1)S(1)} %get-tuple-element.36.refs_0_), channel_id=1, source_target_pairs={{0,4},{1,5},{2,6},{3,7},{4,0},{5,1},{6,2},{7,3},{8,12},{9,13},{10,... | collective-permute-start | bytes 540680 | tf_op jit(solution)/shard_map/ppermute | solution.py:23
  60.1 5.4 %collective-permute-start.8 = (bf16[2,176,256]{2,1,0:T(8,128)(2,1)S(1)}, bf16[2,176,256]{2,1,0:T(8,128)(2,1)S(1)}, u32[]{:S(2)}, u32[]{:S(2)}) collective-permute-start(bf16[2,176,256]{2,1,0:T(8,128)(2,1)S(1)} %get-tuple-element.37.refs_1_), channel_id=1, source_target_pairs={{0,1},{1,0},{2,3},{3,2},{4,5},{5,4},{6,7},{7,6},{8,9},{9,8},{10,11... | collective-permute-start | bytes 540680 | tf_op jit(solution)/shard_map/ppermute | solution.py:23
  60.1 5.4 %collective-permute-start.9 = (bf16[2,160,256]{2,1,0:T(8,128)(2,1)S(1)}, bf16[2,160,256]{2,1,0:T(8,128)(2,1)S(1)}, u32[]{:S(2)}, u32[]{:S(2)}) collective-permute-start(bf16[2,160,256]{2,1,0:T(8,128)(2,1)S(1)} %get-tuple-element.38.refs_2_), channel_id=1, source_target_pairs={{0,3},{1,2},{2,1},{3,0},{4,7},{5,6},{6,5},{7,4},{8,11},{9,10},{10,... | collective-permute-start | bytes 491528 | tf_op jit(solution)/shard_map/ppermute | solution.py:23
  65.5 11.2 %copy-start.3 = (s32[4,10]{1,0:T(4,128)S(1)}, s32[4,10]{1,0:T(4,128)}, u32[]{:S(2)}) copy-start(s32[4,10]{1,0:T(4,128)} %param.13) | copy-start | bytes 484
  66.6 7.3 %collective-permute-start.10 = (bf16[2,176,256]{2,1,0:T(8,128)(2,1)S(1)}, bf16[2,176,256]{2,1,0:T(8,128)(2,1)S(1)}, u32[]{:S(2)}, u32[]{:S(2)}) collective-permute-start(bf16[2,176,256]{2,1,0:T(8,128)(2,1)S(1)} %get-tuple-element.40.refs_0_), channel_id=1, source_target_pairs={{0,3},{1,2},{2,1},{3,0},{4,7},{5,6},{6,5},{7,4},{8,11},{9,10},{10,... | collective-permute-start | bytes 540680 | tf_op jit(solution)/shard_map/ppermute | solution.py:23
  68.4 5.8 %collective-permute-start.11 = (bf16[2,176,256]{2,1,0:T(8,128)(2,1)S(1)}, bf16[2,176,256]{2,1,0:T(8,128)(2,1)S(1)}, u32[]{:S(2)}, u32[]{:S(2)}) collective-permute-start(bf16[2,176,256]{2,1,0:T(8,128)(2,1)S(1)} %get-tuple-element.41.refs_2_), channel_id=1, source_target_pairs={{0,4},{1,5},{2,6},{3,7},{4,0},{5,1},{6,2},{7,3},{8,12},{9,13},{10,... | collective-permute-start | bytes 540680 | tf_op jit(solution)/shard_map/ppermute | solution.py:23
  69.7 4.2 %collective-permute-start.12 = (bf16[2,160,256]{2,1,0:T(8,128)(2,1)S(1)}, bf16[2,160,256]{2,1,0:T(8,128)(2,1)S(1)}, u32[]{:S(2)}, u32[]{:S(2)}) collective-permute-start(bf16[2,160,256]{2,1,0:T(8,128)(2,1)S(1)} %get-tuple-element.42.refs_4_), channel_id=1, source_target_pairs={{0,1},{1,0},{2,3},{3,2},{4,5},{5,4},{6,7},{7,6},{8,9},{9,8},{10,11... | collective-permute-start | bytes 491528 | tf_op jit(solution)/shard_map/ppermute | solution.py:23
  74.3 8.6 %collective-permute-start.13 = (bf16[4,176,256]{2,1,0:T(8,128)(2,1)S(1)}, bf16[4,176,256]{2,1,0:T(8,128)(2,1)S(1)}, u32[]{:S(2)}, u32[]{:S(2)}) collective-permute-start(bf16[4,176,256]{2,1,0:T(8,128)(2,1)S(1)} %get-tuple-element.43.refs_0_), channel_id=1, source_target_pairs={{0,1},{1,0},{2,3},{3,2},{4,5},{5,4},{6,7},{7,6},{8,9},{9,8},{10,11... | collective-permute-start | bytes 1081352 | tf_op jit(solution)/shard_map/ppermute | solution.py:23
  74.4 8.5 %collective-permute-start.14 = (bf16[4,176,256]{2,1,0:T(8,128)(2,1)S(1)}, bf16[4,176,256]{2,1,0:T(8,128)(2,1)S(1)}, u32[]{:S(2)}, u32[]{:S(2)}) collective-permute-start(bf16[4,176,256]{2,1,0:T(8,128)(2,1)S(1)} %get-tuple-element.44.refs_2_), channel_id=1, source_target_pairs={{0,3},{1,2},{2,1},{3,0},{4,7},{5,6},{6,5},{7,4},{8,11},{9,10},{10,... | collective-permute-start | bytes 1081352 | tf_op jit(solution)/shard_map/ppermute | solution.py:23
  75.3 7.6 %collective-permute-start.15 = (bf16[4,160,256]{2,1,0:T(8,128)(2,1)S(1)}, bf16[4,160,256]{2,1,0:T(8,128)(2,1)S(1)}, u32[]{:S(2)}, u32[]{:S(2)}) collective-permute-start(bf16[4,160,256]{2,1,0:T(8,128)(2,1)S(1)} %get-tuple-element.45.refs_4_), channel_id=1, source_target_pairs={{0,4},{1,5},{2,6},{3,7},{4,0},{5,1},{6,2},{7,3},{8,12},{9,13},{10,... | collective-permute-start | bytes 983048 | tf_op jit(solution)/shard_map/ppermute | solution.py:23
  76.7 32.4 %copy-start.1 = (bf16[4,256,256]{2,1,0:T(8,128)(2,1)S(1)}, bf16[4,256,256]{2,1,0:T(8,128)(2,1)}, u32[]{:S(2)}) copy-start(bf16[4,256,256]{2,1,0:T(8,128)(2,1)} %proj_ref.3) | copy-start | bytes 1572868

commit v4 on v3

--- a/solution.py
+++ b/solution.py
@@ -1,3 +1,5 @@
+import functools
+
 import jax
 import jax.numpy as jnp
 from jax import lax
@@ -13,7 +15,7 @@
 DEPTH = 4
 FLIPS = (1, 3, 4)
 ORDERS = ((0, 1, 2), (1, 2, 0), (2, 0, 1))
-CUTS = (0, 176, 352, FLAT)
+CUTS = (0, 208, 384, FLAT)
 LENGTHS = tuple(CUTS[i + 1] - CUTS[i] for i in range(3))
 VMEM = pl.BlockSpec(memory_space=pltpu.VMEM)
 SMALL = pltpu.CompilerParams(vmem_limit_bytes=8 * 2**20)
@@ -108,48 +110,22 @@
     )(slots, peers, held, pltpu.with_memory_space_constraint(edge_row, pltpu.HBM))
 
 
-def halve_kernel(*refs):
-    for part in range(3):
-        keep_ref, came_ref = refs[2 * part], refs[2 * part + 1]
-        send_ref, rest_ref = refs[6 + 2 * part], refs[7 + 2 * part]
-        half = send_ref.shape[0]
-        send_ref[...] = (keep_ref[half:] + came_ref[half:].astype(F32)).astype(BF16)
-        rest_ref[...] = keep_ref[:half] + came_ref[:half].astype(F32)
-
-
-def halve(keeps, came):
-    half = keeps[0].shape[0] // 2
-    outs = []
-    for length in LENGTHS:
-        outs.append(jax.ShapeDtypeStruct((half, length, SIZE), BF16))
-        outs.append(jax.ShapeDtypeStruct((half, length, SIZE), F32))
-    args = [value for pair in zip(keeps, came) for value in pair]
-    return pl.pallas_call(
-        halve_kernel,
-        out_shape=tuple(outs),
-        in_specs=[VMEM] * 6,
-        out_specs=tuple(VMEM for _ in outs),
-        compiler_params=SMALL,
-        cost_estimate=cost(4 * half * FLAT * SIZE, 6 * half * FLAT * SIZE),
-        name="halve",
-    )(*args)
-
-
-def meet_kernel(*refs):
+def meet_kernel(turn, *refs):
     for part in range(3):
         keep_ref, came_ref, out_ref = refs[2 * part], refs[2 * part + 1], refs[6 + part]
-        out_ref[...] = (keep_ref[...] + came_ref[...].astype(F32)).astype(BF16)
-
-
-def meet(keeps, came):
+        for place in range(4):
+            out_ref[place] = (keep_ref[place].astype(F32) + came_ref[place ^ turn].astype(F32)).astype(BF16)
+
+
+def meet(keeps, came, turn):
     args = [value for pair in zip(keeps, came) for value in pair]
     return pl.pallas_call(
-        meet_kernel,
+        functools.partial(meet_kernel, turn),
         out_shape=tuple(jax.ShapeDtypeStruct(value.shape, BF16) for value in keeps),
         in_specs=[VMEM] * 6,
         out_specs=tuple(VMEM for _ in range(3)),
         compiler_params=SMALL,
-        cost_estimate=cost(2 * FLAT * SIZE, 8 * FLAT * SIZE),
+        cost_estimate=cost(4 * FLAT * SIZE, 16 * FLAT * SIZE),
         name="meet",
     )(*args)
 
@@ -159,9 +135,10 @@
     mine = []
     for part, order in enumerate(ORDERS):
         low, high = CUTS[part], CUTS[part + 1]
-        for place in range(2):
-            first = (index_ref[0] ^ (place * FLIPS[order[2]])) * COUNT
-            total = (ours_refs[part][place].astype(F32) + came_refs[part][1 - place].astype(F32)).astype(BF16)
+        for place in range(4):
+            offset = place // 2 * FLIPS[order[1]] ^ place % 2 * FLIPS[order[2]]
+            first = (index_ref[0] ^ offset) * COUNT
+            total = (ours_refs[part][place].astype(F32) + came_refs[part][place ^ 1].astype(F32)).astype(BF16)
             pieces = []
             for sector in range(COUNT):
                 start, stop = max(low, sector * SIZE), min(high, (sector + 1) * SIZE)
@@ -180,38 +157,16 @@
 
 def absorb(index, ours, came, proj_row):
     outs = [jax.ShapeDtypeStruct((COUNT, SIZE, SIZE), BF16)]
-    outs += [jax.ShapeDtypeStruct((2, length, SIZE), BF16) for length in LENGTHS]
+    outs += [jax.ShapeDtypeStruct((4, length, SIZE), BF16) for length in LENGTHS]
     return pl.pallas_call(
         absorb_kernel,
         out_shape=tuple(outs),
         in_specs=[pl.BlockSpec(memory_space=pltpu.SMEM)] + [VMEM] * 7,
         out_specs=tuple(VMEM for _ in outs),
         compiler_params=SMALL,
-        cost_estimate=cost(4 * COUNT * SIZE**3, 10 * FLAT * SIZE),
+        cost_estimate=cost(8 * COUNT * SIZE**3, 20 * FLAT * SIZE),
         name="absorb",
     )(index, proj_row, *ours, *came)
-
-
-def double_kernel(*refs):
-    for part in range(3):
-        held_ref, came_ref, out_ref = refs[2 * part], refs[2 * part + 1], refs[6 + part]
-        half = held_ref.shape[0]
-        out_ref[:half] = held_ref[...]
-        out_ref[half:] = came_ref[...]
-
-
-def double(held, came):
-    half = held[0].shape[0]
-    args = [value for pair in zip(held, came) for value in pair]
-    return pl.pallas_call(
-        double_kernel,
-        out_shape=tuple(jax.ShapeDtypeStruct((2 * half, length, SIZE), BF16) for length in LENGTHS),
-        in_specs=[VMEM] * 6,
-        out_specs=tuple(VMEM for _ in range(3)),
-        compiler_params=SMALL,
-        cost_estimate=cost(0, 4 * half * FLAT * SIZE),
-        name="double",
-    )(*args)
 
 
 def col_kernel(slot_ref, *refs):
@@ -303,16 +258,13 @@
     offsets = [p * FLIPS[0] ^ q * FLIPS[1] ^ z * FLIPS[2] for p in range(2) for q in range(2) for z in range(2)]
     peers = jnp.bitwise_xor(right, jnp.array(offsets[::-1], jnp.int32))
     outs = row_partial(slots, peers, held, edge_row)
-    for phase in range(2):
-        came = [flip(outs[2 * part], ORDERS[part][phase], rights) for part in range(3)]
-        outs = halve(outs[1::2], came) if phase == 0 else meet(outs[1::2], came)
-    came = [flip(outs[part], ORDERS[part][2], rights) for part in range(3)]
-    absorbed, *parts = absorb(jnp.reshape(right, (1,)).astype(jnp.int32), outs, came, proj_row)
-
-    for phase in range(1, 3):
-        came = [flip(parts[part], ORDERS[part][2 - phase], rights) for part in range(3)]
-        if phase < 2:
-            parts = double(parts, came)
+    came = [flip(outs[2 * part], ORDERS[part][0], rights) for part in range(3)]
+    ours = meet(outs[1::2], came, 0)
+    came = [flip(ours[part], ORDERS[part][1], rights) for part in range(3)]
+    ours = meet(ours, came, 2)
+    came = [flip(ours[part], ORDERS[part][2], rights) for part in range(3)]
+    absorbed, *parts = absorb(jnp.reshape(right, (1,)).astype(jnp.int32), ours, came, proj_row)
+    came = [flip(parts[part], ORDERS[part][0], rights) for part in range(3)]
     pieces = [value for pair in zip(parts, came) for value in pair]
 
     inner = source_col - left * (rights * COUNT)

time: 110 us -> 103 us (0.936)
  blocking collectives: 42.5 us -> 37.5 us
  waiting for transfers between devices: 28.1 us -> 25.4 us
    all_to_all x1, blocking collectives: 22 us -> 17 us  [body(): col_parts = lax.all_to_all(partial_cols, 'left', 0, 0, tiled=True)]
    ppermute x15 -> x12, waiting for transfers between devices: 25.9 us -> 23.2 us  [flip(): lax.ppermute(value, 'right', [(i, i ^ FLIPS[pairing]) for i in range(size)])]
    ppermute x15 -> x12, starting transfers between devices: 19 us -> 19.5 us  [flip(): lax.ppermute(value, 'right', [(i, i ^ FLIPS[pairing]) for i in range(size)])]
  transfers between devices with their start and end apart: 16 -> 13, of which waited for: 7 -> 8; matrix products, arithmetic and copies ran while one was open for 0% -> 0% of each run, Pallas kernels for 0% -> 0%
where the time goes in v4:
time: 103 us
  blocking collectives  37.5 us (36%)
  waiting for transfers between devices  25.4 us (25%)
  starting transfers between devices  21.5 us (21%)
  Pallas kernels  16.5 us (16%)
  local copies, waits for them, and re-layouts  1.08 us (1%)
    ppermute x12, waiting for transfers between devices, flip(): lax.ppermute(value, 'right', [(i, i ^ FLIPS[pairing]) for i in range(size)])  23.2 us
    all_to_all x1, blocking collectives, body(): lax.all_to_all(jnp.broadcast_to(corner, (lefts // 2, SIZE, SIZE)), 'left'...  20.5 us
    ppermute x12, starting transfers between devices, flip(): lax.ppermute(value, 'right', [(i, i ^ FLIPS[pairing]) for i in range(size)])  19.5 us
    all_to_all x1, blocking collectives, body(): col_parts = lax.all_to_all(partial_cols, 'left', 0, 0, tiled=True)  17 us
    pallas_call x1, Pallas kernels, row_partial(): pl.pallas_call(row_kernel, out_shape=tuple(outs), grid_spec=pltpu.Prefetc...  9.8 us
    pallas_call x1, Pallas kernels, col_partial(): pl.pallas_call(col_kernel, out_shape=jax.ShapeDtypeStruct((pieces, sector...  4.18 us
    ppermute x1, waiting for transfers between devices, body(): other = lax.ppermute(own, 'left', [(i, i ^ 1) for i in range(lefts)])  2.18 us
  transfers between devices with their start and end apart: 13, of which 8 were waited for; matrix products, arithmetic and copies ran while one was open for 0% of the time, Pallas kernels for 0%

profile of v4, /device:TPU:1, one launch (start us, length us, event | category | flops | bytes accessed | tf_op | source)
XLA Modules:
  0.0 102.9 jit_solution(3580464022372754340)
XLA Ops:
  0.6 0.0 copy-start.4
  0.7 1.0 broadcast_in_dim.12
  1.6 20.5 %all_to_all.10 = bf16[8,256,256]{2,1,0:T(8,128)(2,1)S(1)} all-to-all(bf16[8,256,256]{2,1,0:T(8,128)(2,1)S(1)} %broadcast_in_dim.12), channel_id=1, replica_groups={{0,16,32,48,64,80,96,112},{8,24,40,56,72,88,104,120},{1,17,33,49,65,81,..., dimensions={0} | all-to-all | bytes 2097152 | tf_op jit(solution)/shard_map/all_to_all | solution.py:250
  22.1 2.0 %collective-permute-start = (bf16[8,256,256]{2,1,0:T(8,128)(2,1)S(1)}, bf16[8,256,256]{2,1,0:T(8,128)(2,1)S(1)}, u32[]{:S(2)}, u32[]{:S(2)}) collective-permute-start(bf16[8,256,256]{2,1,0:T(8,128)(2,1)S(1)} %all_to_all.10), channel_id=1, source_target_pairs={{0,8},{8,0},{16,24},{24,16},{32,40},{40,32},{48,56},{56,48},{64,72... | collective-permute-start | bytes 3145736 | tf_op jit(solution)/shard_map/ppermute | solution.py:253
  24.1 0.1 copy.10
  24.2 2.2 %collective-permute-done = bf16[8,256,256]{2,1,0:T(8,128)(2,1)S(1)} collective-permute-done((bf16[8,256,256]{2,1,0:T(8,128)(2,1)S(1)}, bf16[8,256,256]{2,1,0:T(8,128)(2,1)S(1)}, u32[]{:S(2)}, u32[]{:S(2)}) %collective-permute-start) | collective-permute-done | bytes 1048608 | tf_op jit(solution)/shard_map/ppermute | solution.py:253
  26.4 0.2 pad_maximum_fusion.held_ref
  26.6 9.8 %row_partial.1 = (bf16[4,208,256]{2,1,0:T(8,128)(2,1)S(1)}, f32[4,208,256]{2,1,0:T(8,128)S(1)}, bf16[4,176,256]{2,1,0:T(8,128)(2,1)S(1)}, f32[4,176,256]{2,1,0:T...) custom-call(s32[16,8]{1,0:T(8,128)S(1)} %fusion.1.slot_ref, s32[8]{0:T(128)S(1)} %broadcast_xor_fusion.peer_ref, ...), custom_call_target="tpu_custom_call" | custom-call | flops 4294967296 | bytes 16777216 | tf_op jit(solution)/shard_map/row_partial/pallas_call | solution.py:94
  36.4 1.3 %collective-permute-start.1 = (bf16[4,208,256]{2,1,0:T(8,128)(2,1)S(1)}, bf16[4,208,256]{2,1,0:T(8,128)(2,1)S(1)}, u32[]{:S(2)}, u32[]{:S(2)}) collective-permute-start(bf16[4,208,256]{2,1,0:T(8,128)(2,1)S(1)} %get-tuple-element.19), channel_id=1, source_target_pairs={{0,1},{1,0},{2,3},{3,2},{4,5},{5,4},{6,7},{7,6},{8,9},{9,8},{10,11... | collective-permute-start | bytes 1277960 | tf_op jit(solution)/shard_map/ppermute | solution.py:25
  37.7 1.8 %collective-permute-start.2 = (bf16[4,176,256]{2,1,0:T(8,128)(2,1)S(1)}, bf16[4,176,256]{2,1,0:T(8,128)(2,1)S(1)}, u32[]{:S(2)}, u32[]{:S(2)}) collective-permute-start(bf16[4,176,256]{2,1,0:T(8,128)(2,1)S(1)} %get-tuple-element.21), channel_id=1, source_target_pairs={{0,3},{1,2},{2,1},{3,0},{4,7},{5,6},{6,5},{7,4},{8,11},{9,10},{10,... | collective-permute-start | bytes 1081352 | tf_op jit(solution)/shard_map/ppermute | solution.py:25
  39.5 3.3 %collective-permute-start.3 = (bf16[4,128,256]{2,1,0:T(8,128)(2,1)S(1)}, bf16[4,128,256]{2,1,0:T(8,128)(2,1)S(1)}, u32[]{:S(2)}, u32[]{:S(2)}) collective-permute-start(bf16[4,128,256]{2,1,0:T(8,128)(2,1)S(1)} %get-tuple-element.23), channel_id=1, source_target_pairs={{0,4},{1,5},{2,6},{3,7},{4,0},{5,1},{6,2},{7,3},{8,12},{9,13},{10,... | collective-permute-start | bytes 786440 | tf_op jit(solution)/shard_map/ppermute | solution.py:25
  42.8 5.7 %collective-permute-done.3.refs_5_ = bf16[4,128,256]{2,1,0:T(8,128)(2,1)S(1)} collective-permute-done((bf16[4,128,256]{2,1,0:T(8,128)(2,1)S(1)}, bf16[4,128,256]{2,1,0:T(8,128)(2,1)S(1)}, u32[]{:S(2)}, u32[]{:S(2)}) %collective-permute-start.3) | collective-permute-done | bytes 262176 | tf_op jit(solution)/shard_map/ppermute | solution.py:25
  48.6 0.2 meet.2
  48.8 1.6 %collective-permute-start.4 = (bf16[4,208,256]{2,1,0:T(8,128)(2,1)S(1)}, bf16[4,208,256]{2,1,0:T(8,128)(2,1)S(1)}, u32[]{:S(2)}, u32[]{:S(2)}) collective-permute-start(bf16[4,208,256]{2,1,0:T(8,128)(2,1)S(1)} %get-tuple-element.24.refs_0_), channel_id=1, source_target_pairs={{0,3},{1,2},{2,1},{3,0},{4,7},{5,6},{6,5},{7,4},{8,11},{9,10},{10,... | collective-permute-start | bytes 1277960 | tf_op jit(solution)/shard_map/ppermute | solution.py:25
  50.4 3.3 %collective-permute-start.5 = (bf16[4,176,256]{2,1,0:T(8,128)(2,1)S(1)}, bf16[4,176,256]{2,1,0:T(8,128)(2,1)S(1)}, u32[]{:S(2)}, u32[]{:S(2)}) collective-permute-start(bf16[4,176,256]{2,1,0:T(8,128)(2,1)S(1)} %get-tuple-element.25.refs_2_), channel_id=1, source_target_pairs={{0,4},{1,5},{2,6},{3,7},{4,0},{5,1},{6,2},{7,3},{8,12},{9,13},{10,... | collective-permute-start | bytes 1081352 | tf_op jit(solution)/shard_map/ppermute | solution.py:25
  53.7 5.7 %collective-permute-done.6.refs_5_ = bf16[4,128,256]{2,1,0:T(8,128)(2,1)S(1)} collective-permute-done((bf16[4,128,256]{2,1,0:T(8,128)(2,1)S(1)}, bf16[4,128,256]{2,1,0:T(8,128)(2,1)S(1)}, u32[]{:S(2)}, u32[]{:S(2)}) %collective-permute-start.6) | collective-permute-done | bytes 262176 | tf_op jit(solution)/shard_map/ppermute | solution.py:25
  59.4 1.2 %collective-permute-done.5.refs_3_ = bf16[4,176,256]{2,1,0:T(8,128)(2,1)S(1)} collective-permute-done((bf16[4,176,256]{2,1,0:T(8,128)(2,1)S(1)}, bf16[4,176,256]{2,1,0:T(8,128)(2,1)S(1)}, u32[]{:S(2)}, u32[]{:S(2)}) %collective-permute-start.5) | collective-permute-done | bytes 360480 | tf_op jit(solution)/shard_map/ppermute | solution.py:25
  60.6 0.2 meet.3
  60.8 2.8 %collective-permute-start.7 = (bf16[4,208,256]{2,1,0:T(8,128)(2,1)S(1)}, bf16[4,208,256]{2,1,0:T(8,128)(2,1)S(1)}, u32[]{:S(2)}, u32[]{:S(2)}) collective-permute-start(bf16[4,208,256]{2,1,0:T(8,128)(2,1)S(1)} %get-tuple-element.27.refs_0_), channel_id=1, source_target_pairs={{0,4},{1,5},{2,6},{3,7},{4,0},{5,1},{6,2},{7,3},{8,12},{9,13},{10,... | collective-permute-start | bytes 1277960 | tf_op jit(solution)/shard_map/ppermute | solution.py:25
  63.6 0.2 collective-permute-start.8
  63.8 1.2 %collective-permute-start.9 = (bf16[4,128,256]{2,1,0:T(8,128)(2,1)S(1)}, bf16[4,128,256]{2,1,0:T(8,128)(2,1)S(1)}, u32[]{:S(2)}, u32[]{:S(2)}) collective-permute-start(bf16[4,128,256]{2,1,0:T(8,128)(2,1)S(1)} %get-tuple-element.29.refs_2_), channel_id=1, source_target_pairs={{0,3},{1,2},{2,1},{3,0},{4,7},{5,6},{6,5},{7,4},{8,11},{9,10},{10,... | collective-permute-start | bytes 786440 | tf_op jit(solution)/shard_map/ppermute | solution.py:25
  65.0 5.6 %collective-permute-done.9.refs_5_ = bf16[4,128,256]{2,1,0:T(8,128)(2,1)S(1)} collective-permute-done((bf16[4,128,256]{2,1,0:T(8,128)(2,1)S(1)}, bf16[4,128,256]{2,1,0:T(8,128)(2,1)S(1)}, u32[]{:S(2)}, u32[]{:S(2)}) %collective-permute-start.9) | collective-permute-done | bytes 262176 | tf_op jit(solution)/shard_map/ppermute | solution.py:25
  70.6 0.7 collective-permute-done.7.refs_3_
  71.3 1.3 %absorb.1 = (bf16[2,256,256]{2,1,0:T(8,128)(2,1)}, bf16[4,208,256]{2,1,0:T(8,128)(2,1)S(1)}, bf16[4,176,256]{2,1,0:T(8,128)(2,1)S(1)}, bf16[4,128,256]{2,1,0:T(8,128)(2,1)S(1)}) custom-call(s32[1]{0:T(128)} %bitcast.index_ref, bf16[16,256,256]{2,1,0:T(8,128)(2,1)S(1)} %copy-done, bf16[4,208,256]{2,1,0:T(8,128)(2,1)S(1)} %get-tuple-element.27.refs_0_, ...), custom_call_target="tpu_custom_call" | custom-call | flops 268435456 | bytes 5242880 | tf_op jit(solution)/shard_map/absorb/pallas_call | solution.py:161
  72.6 0.5 collective-permute-start.10
  73.1 0.8 collective-permute-start.11
  73.9 2.7 %collective-permute-start.12 = (bf16[4,128,256]{2,1,0:T(8,128)(2,1)S(1)}, bf16[4,128,256]{2,1,0:T(8,128)(2,1)S(1)}, u32[]{:S(2)}, u32[]{:S(2)}) collective-permute-start(bf16[4,128,256]{2,1,0:T(8,128)(2,1)S(1)} %get-tuple-element.33.refs_4_), channel_id=1, source_target_pairs={{0,4},{1,5},{2,6},{3,7},{4,0},{5,1},{6,2},{7,3},{8,12},{9,13},{10,... | collective-permute-start | bytes 786440 | tf_op jit(solution)/shard_map/ppermute | solution.py:25
  76.7 3.9 %collective-permute-done.12.refs_5_ = bf16[4,128,256]{2,1,0:T(8,128)(2,1)S(1)} collective-permute-done((bf16[4,128,256]{2,1,0:T(8,128)(2,1)S(1)}, bf16[4,128,256]{2,1,0:T(8,128)(2,1)S(1)}, u32[]{:S(2)}, u32[]{:S(2)}) %collective-permute-start.12) | collective-permute-done | bytes 262176 | tf_op jit(solution)/shard_map/ppermute | solution.py:25
  80.6 0.3 collective-permute-done.11.refs_3_
  80.9 4.2 %col_partial.1 = bf16[16,4,16,256]{3,2,1,0:T(8,128)(2,1)S(1)} custom-call(s32[4,10]{1,0:T(4,128)S(1)} %fusion.14.slot_ref, bf16[4,208,256]{2,1,0:T(8,128)(2,1)S(1)} %get-tuple-element.31.refs_0_, bf16[4,208,256]{2,1,0:T(8,128)(2,1)S(1)} %collective-permute-done.10.refs_1_, bf16[4,176,256]{2,1,0:T(8,128)(2,1)S(1)} %get-tuple-element.32.refs_2_, ...), custom_call_target="tpu_custom_call" | custom-call | flops 1342177280 | bytes 5242880 | tf_op jit(solution)/shard_map/col_partial/pallas_call | solution.py:208
  85.1 17.0 %all_to_all.11.part_ref = bf16[16,4,16,256]{3,2,1,0:T(8,128)(2,1)S(1)} all-to-all(bf16[16,4,16,256]{3,2,1,0:T(8,128)(2,1)S(1)} %col_partial.1), channel_id=1, replica_groups=mesh['left'=16,'right'=8] {'left'}, dimensions={0} | all-to-all | bytes 1048576 | tf_op jit(solution)/shard_map/all_to_all | solution.py:276
  102.1 0.9 finish.1
  (18 shorter events, 0.1 us)
Async XLA Ops:
  0.6 23.6 %copy-start.4 = (s32[8]{0:T(128)S(1)}, s32[8]{0:T(128)}, u32[]{:S(2)}) copy-start(s32[8]{0:T(128)} %constant.104.clone) | copy-start | bytes 100
  0.6 23.5 %copy-start.2 = (s32[16,8]{0,1:T(8,128)S(1)}, s32[16,8]{0,1:T(8,128)}, u32[]{:S(2)}) copy-start(s32[16,8]{0,1:T(8,128)} %param.10) | copy-start | bytes 1540
  22.1 4.3 %collective-permute-start = (bf16[8,256,256]{2,1,0:T(8,128)(2,1)S(1)}, bf16[8,256,256]{2,1,0:T(8,128)(2,1)S(1)}, u32[]{:S(2)}, u32[]{:S(2)}) collective-permute-start(bf16[8,256,256]{2,1,0:T(8,128)(2,1)S(1)} %all_to_all.10), channel_id=1, source_target_pairs={{0,8},{8,0},{16,24},{24,16},{32,40},{40,32},{48,56},{56,48},{64,72... | collective-permute-start | bytes 3145736 | tf_op jit(solution)/shard_map/ppermute | solution.py:253
  36.4 12.2 %collective-permute-start.1 = (bf16[4,208,256]{2,1,0:T(8,128)(2,1)S(1)}, bf16[4,208,256]{2,1,0:T(8,128)(2,1)S(1)}, u32[]{:S(2)}, u32[]{:S(2)}) collective-permute-start(bf16[4,208,256]{2,1,0:T(8,128)(2,1)S(1)} %get-tuple-element.19), channel_id=1, source_target_pairs={{0,1},{1,0},{2,3},{3,2},{4,5},{5,4},{6,7},{7,6},{8,9},{9,8},{10,11... | collective-permute-start | bytes 1277960 | tf_op jit(solution)/shard_map/ppermute | solution.py:25
  37.7 10.8 %collective-permute-start.2 = (bf16[4,176,256]{2,1,0:T(8,128)(2,1)S(1)}, bf16[4,176,256]{2,1,0:T(8,128)(2,1)S(1)}, u32[]{:S(2)}, u32[]{:S(2)}) collective-permute-start(bf16[4,176,256]{2,1,0:T(8,128)(2,1)S(1)} %get-tuple-element.21), channel_id=1, source_target_pairs={{0,3},{1,2},{2,1},{3,0},{4,7},{5,6},{6,5},{7,4},{8,11},{9,10},{10,... | collective-permute-start | bytes 1081352 | tf_op jit(solution)/shard_map/ppermute | solution.py:25
  39.5 9.0 %collective-permute-start.3 = (bf16[4,128,256]{2,1,0:T(8,128)(2,1)S(1)}, bf16[4,128,256]{2,1,0:T(8,128)(2,1)S(1)}, u32[]{:S(2)}, u32[]{:S(2)}) collective-permute-start(bf16[4,128,256]{2,1,0:T(8,128)(2,1)S(1)} %get-tuple-element.23), channel_id=1, source_target_pairs={{0,4},{1,5},{2,6},{3,7},{4,0},{5,1},{6,2},{7,3},{8,12},{9,13},{10,... | collective-permute-start | bytes 786440 | tf_op jit(solution)/shard_map/ppermute | solution.py:25
  48.6 22.7 %copy-start = (bf16[16,256,256]{2,1,0:T(8,128)(2,1)S(1)}, bf16[16,256,256]{2,1,0:T(8,128)(2,1)}, u32[]{:S(2)}) copy-start(bf16[16,256,256]{2,1,0:T(8,128)(2,1)} %proj_ref.2) | copy-start | bytes 6291460
  48.8 11.8 %collective-permute-start.4 = (bf16[4,208,256]{2,1,0:T(8,128)(2,1)S(1)}, bf16[4,208,256]{2,1,0:T(8,128)(2,1)S(1)}, u32[]{:S(2)}, u32[]{:S(2)}) collective-permute-start(bf16[4,208,256]{2,1,0:T(8,128)(2,1)S(1)} %get-tuple-element.24.refs_0_), channel_id=1, source_target_pairs={{0,3},{1,2},{2,1},{3,0},{4,7},{5,6},{6,5},{7,4},{8,11},{9,10},{10,... | collective-permute-start | bytes 1277960 | tf_op jit(solution)/shard_map/ppermute | solution.py:25
  50.4 10.2 %collective-permute-start.5 = (bf16[4,176,256]{2,1,0:T(8,128)(2,1)S(1)}, bf16[4,176,256]{2,1,0:T(8,128)(2,1)S(1)}, u32[]{:S(2)}, u32[]{:S(2)}) collective-permute-start(bf16[4,176,256]{2,1,0:T(8,128)(2,1)S(1)} %get-tuple-element.25.refs_2_), channel_id=1, source_target_pairs={{0,4},{1,5},{2,6},{3,7},{4,0},{5,1},{6,2},{7,3},{8,12},{9,13},{10,... | collective-permute-start | bytes 1081352 | tf_op jit(solution)/shard_map/ppermute | solution.py:25
  53.6 5.7 %collective-permute-start.6 = (bf16[4,128,256]{2,1,0:T(8,128)(2,1)S(1)}, bf16[4,128,256]{2,1,0:T(8,128)(2,1)S(1)}, u32[]{:S(2)}, u32[]{:S(2)}) collective-permute-start(bf16[4,128,256]{2,1,0:T(8,128)(2,1)S(1)} %get-tuple-element.26.refs_4_), channel_id=1, source_target_pairs={{0,1},{1,0},{2,3},{3,2},{4,5},{5,4},{6,7},{7,6},{8,9},{9,8},{10,11... | collective-permute-start | bytes 786440 | tf_op jit(solution)/shard_map/ppermute | solution.py:25
  60.8 10.5 %collective-permute-start.7 = (bf16[4,208,256]{2,1,0:T(8,128)(2,1)S(1)}, bf16[4,208,256]{2,1,0:T(8,128)(2,1)S(1)}, u32[]{:S(2)}, u32[]{:S(2)}) collective-permute-start(bf16[4,208,256]{2,1,0:T(8,128)(2,1)S(1)} %get-tuple-element.27.refs_0_), channel_id=1, source_target_pairs={{0,4},{1,5},{2,6},{3,7},{4,0},{5,1},{6,2},{7,3},{8,12},{9,13},{10,... | collective-permute-start | bytes 1277960 | tf_op jit(solution)/shard_map/ppermute | solution.py:25
  63.6 7.0 %collective-permute-start.8 = (bf16[4,176,256]{2,1,0:T(8,128)(2,1)S(1)}, bf16[4,176,256]{2,1,0:T(8,128)(2,1)S(1)}, u32[]{:S(2)}, u32[]{:S(2)}) collective-permute-start(bf16[4,176,256]{2,1,0:T(8,128)(2,1)S(1)} %get-tuple-element.28.refs_1_), channel_id=1, source_target_pairs={{0,1},{1,0},{2,3},{3,2},{4,5},{5,4},{6,7},{7,6},{8,9},{9,8},{10,11... | collective-permute-start | bytes 1081352 | tf_op jit(solution)/shard_map/ppermute | solution.py:25
  63.8 6.7 %collective-permute-start.9 = (bf16[4,128,256]{2,1,0:T(8,128)(2,1)S(1)}, bf16[4,128,256]{2,1,0:T(8,128)(2,1)S(1)}, u32[]{:S(2)}, u32[]{:S(2)}) collective-permute-start(bf16[4,128,256]{2,1,0:T(8,128)(2,1)S(1)} %get-tuple-element.29.refs_2_), channel_id=1, source_target_pairs={{0,3},{1,2},{2,1},{3,0},{4,7},{5,6},{6,5},{7,4},{8,11},{9,10},{10,... | collective-permute-start | bytes 786440 | tf_op jit(solution)/shard_map/ppermute | solution.py:25
  71.3 5.3 %copy-start.3 = (s32[4,10]{1,0:T(4,128)S(1)}, s32[4,10]{1,0:T(4,128)}, u32[]{:S(2)}) copy-start(s32[4,10]{1,0:T(4,128)} %param.13) | copy-start | bytes 484
  72.6 8.3 %collective-permute-start.10 = (bf16[4,208,256]{2,1,0:T(8,128)(2,1)S(1)}, bf16[4,208,256]{2,1,0:T(8,128)(2,1)S(1)}, u32[]{:S(2)}, u32[]{:S(2)}) collective-permute-start(bf16[4,208,256]{2,1,0:T(8,128)(2,1)S(1)} %get-tuple-element.31.refs_0_), channel_id=1, source_target_pairs={{0,1},{1,0},{2,3},{3,2},{4,5},{5,4},{6,7},{7,6},{8,9},{9,8},{10,11... | collective-permute-start | bytes 1277960 | tf_op jit(solution)/shard_map/ppermute | solution.py:25
  73.1 7.8 %collective-permute-start.11 = (bf16[4,176,256]{2,1,0:T(8,128)(2,1)S(1)}, bf16[4,176,256]{2,1,0:T(8,128)(2,1)S(1)}, u32[]{:S(2)}, u32[]{:S(2)}) collective-permute-start(bf16[4,176,256]{2,1,0:T(8,128)(2,1)S(1)} %get-tuple-element.32.refs_2_), channel_id=1, source_target_pairs={{0,3},{1,2},{2,1},{3,0},{4,7},{5,6},{6,5},{7,4},{8,11},{9,10},{10,... | collective-permute-start | bytes 1081352 | tf_op jit(solution)/shard_map/ppermute | solution.py:25
  73.9 6.7 %collective-permute-start.12 = (bf16[4,128,256]{2,1,0:T(8,128)(2,1)S(1)}, bf16[4,128,256]{2,1,0:T(8,128)(2,1)S(1)}, u32[]{:S(2)}, u32[]{:S(2)}) collective-permute-start(bf16[4,128,256]{2,1,0:T(8,128)(2,1)S(1)} %get-tuple-element.33.refs_4_), channel_id=1, source_target_pairs={{0,4},{1,5},{2,6},{3,7},{4,0},{5,1},{6,2},{7,3},{8,12},{9,13},{10,... | collective-permute-start | bytes 786440 | tf_op jit(solution)/shard_map/ppermute | solution.py:25
  76.7 25.4 %copy-start.1 = (bf16[4,256,256]{2,1,0:T(8,128)(2,1)S(1)}, bf16[4,256,256]{2,1,0:T(8,128)(2,1)}, u32[]{:S(2)}) copy-start(bf16[4,256,256]{2,1,0:T(8,128)(2,1)} %proj_ref.3) | copy-start | bytes 1572868

commit v5 on v4

--- a/solution.py
+++ b/solution.py
@@ -12,6 +12,7 @@
 SIZE = 256
 COUNT = 2
 FLAT = COUNT * SIZE
+HOPS = ((2, 1), (1, 1), (3, 1), (0, 1), (1, 0), (3, 0), (2, 0))
 DEPTH = 4
 FLIPS = (1, 3, 4)
 ORDERS = ((0, 1, 2), (1, 2, 0), (2, 0, 1))
@@ -34,39 +35,58 @@
     return pl.CostEstimate(flops=flops, bytes_accessed=2 * elements, transcendentals=0)
 
 
-def row_kernel(slot_ref, peer_ref, held_ref, edge_hbm, *refs):
-    *out_refs, ring, sems = refs
-    step, steps, depth = pl.program_id(0), pl.num_programs(0), ring.shape[0]
-    place = steps - 1 - step
+def join_kernel(*refs):
+    *block_refs, out_ref = refs
+    for place, block_ref in enumerate(block_refs):
+        out_ref[place] = block_ref[0]
+
+
+def join(blocks):
+    return pl.pallas_call(
+        join_kernel,
+        out_shape=jax.ShapeDtypeStruct((len(blocks), SIZE, SIZE), BF16),
+        in_specs=[VMEM for _ in blocks],
+        out_specs=VMEM,
+        compiler_params=SMALL,
+        cost_estimate=cost(0, 2 * len(blocks) * SIZE**2),
+        name="join",
+    )(*blocks)
+
+
+def load_kernel(edge_ref, out_ref, sems):
+    copies = [
+        pltpu.make_async_copy(edge_ref.at[i], out_ref.at[i], sems.at[i]) for i in range(edge_ref.shape[0])
+    ]
+    for copy in copies:
+        copy.start()
+    for copy in copies:
+        copy.wait()
+
+
+def load(edge):
+    return pl.pallas_call(
+        load_kernel,
+        out_shape=pltpu.VMEM(edge.shape, edge.dtype),
+        in_specs=[pl.BlockSpec(memory_space=pl.ANY)],
+        out_specs=VMEM,
+        scratch_shapes=[pltpu.SemaphoreType.DMA((edge.shape[0],))],
+        compiler_params=SMALL,
+        cost_estimate=cost(0, 2 * edge.size),
+        name="load",
+    )(pltpu.with_memory_space_constraint(edge, pltpu.HBM))
+
+
+def row_kernel(slot_ref, peer_ref, held_ref, edge_ref, *out_refs):
+    step = pl.program_id(0)
+    place = pl.num_programs(0) - 1 - step
     first = peer_ref[step] * COUNT
 
-    def fetch(later):
-        slot = later % depth
-        return [
-            pltpu.make_async_copy(edge_hbm.at[peer_ref[later] * COUNT + i], ring.at[slot, i], sems.at[slot, i])
-            for i in range(COUNT)
-        ]
-
-    @pl.when(step == 0)
-    def _():
-        for later in range(depth - 1):
-            for copy in fetch(later):
-                copy.start()
-
-    @pl.when(step + depth - 1 < steps)
-    def _():
-        for copy in fetch(step + depth - 1):
-            copy.start()
-
-    for copy in fetch(step):
-        copy.wait()
-    edge_ref = ring.at[step % depth]
     values = []
     for sector in range(COUNT):
-        total = jnp.dot(held_ref[slot_ref[first + sector, 0]], edge_ref[sector, 0], preferred_element_type=F32)
+        total = jnp.dot(held_ref[slot_ref[0, first + sector]], edge_ref[first + sector, 0], preferred_element_type=F32)
         for entry in range(1, edge_ref.shape[1]):
             total += jnp.dot(
-                held_ref[slot_ref[first + sector, entry]], edge_ref[sector, entry], preferred_element_type=F32
+                held_ref[slot_ref[entry, first + sector]], edge_ref[first + sector, entry], preferred_element_type=F32
             )
         values.append(total.T)
     flat = jnp.concatenate(values, axis=0)
@@ -97,17 +117,13 @@
         grid_spec=pltpu.PrefetchScalarGridSpec(
             num_scalar_prefetch=2,
             grid=(steps,),
-            in_specs=[VMEM, pl.BlockSpec(memory_space=pl.ANY)],
+            in_specs=[VMEM, VMEM],
             out_specs=tuple(VMEM for _ in outs),
-            scratch_shapes=[
-                pltpu.VMEM((DEPTH, COUNT, entries, SIZE, SIZE), BF16),
-                pltpu.SemaphoreType.DMA((DEPTH, COUNT)),
-            ],
         ),
-        compiler_params=pltpu.CompilerParams(vmem_limit_bytes=24 * 2**20),
+        compiler_params=SMALL,
         cost_estimate=cost(2 * steps * COUNT * entries * SIZE**3, steps * COUNT * entries * SIZE**2),
         name="row_partial",
-    )(slots, peers, held, pltpu.with_memory_space_constraint(edge_row, pltpu.HBM))
+    )(slots, peers, held, edge_row)
 
 
 def meet_kernel(turn, *refs):
@@ -170,24 +186,17 @@
 
 
 def col_kernel(slot_ref, *refs):
-    piece_refs, (edge_hbm, out_ref, held, edge_ref, edge_sems) = refs[:6], refs[6:]
+    piece_refs, (edge_ref, out_ref, held) = refs[:6], refs[6:]
     step = pl.program_id(0)
-
-    def fetch(later):
-        return pltpu.make_async_copy(edge_hbm.at[later], edge_ref.at[later], edge_sems.at[later])
 
     @pl.when(step == 0)
     def _():
-        for later in range(edge_ref.shape[0]):
-            fetch(later).start()
         for part, order in enumerate(ORDERS):
             for place in range(8):
                 index = place_of(place, order)
                 start = place * FLAT + CUTS[part]
                 held[start : start + LENGTHS[part]] = piece_refs[2 * part + index // 4][index % 4]
 
-    fetch(step).wait()
-
     def block(entry):
         return held[pl.ds(pl.multiple_of(slot_ref[step, entry] * SIZE, SIZE), SIZE)]
 
@@ -211,18 +220,14 @@
         grid_spec=pltpu.PrefetchScalarGridSpec(
             num_scalar_prefetch=1,
             grid=(sectors,),
-            in_specs=[VMEM] * 6 + [pl.BlockSpec(memory_space=pl.ANY)],
+            in_specs=[VMEM] * 7,
             out_specs=pl.BlockSpec((pieces, 1, piece, SIZE), lambda g, s: (0, g, 0, 0)),
-            scratch_shapes=[
-                pltpu.VMEM((8 * FLAT, SIZE), BF16),
-                pltpu.VMEM(edge_col.shape, BF16),
-                pltpu.SemaphoreType.DMA((sectors,)),
-            ],
+            scratch_shapes=[pltpu.VMEM((8 * FLAT, SIZE), BF16)],
         ),
-        compiler_params=pltpu.CompilerParams(vmem_limit_bytes=24 * 2**20),
+        compiler_params=SMALL,
         cost_estimate=cost(2 * sectors * entries * SIZE**3, sectors * entries * SIZE**2),
         name="col_partial",
-    )(slots, *pieces_in, pltpu.with_memory_space_constraint(edge_col, pltpu.HBM))
+    )(slots, *pieces_in, edge_col)
 
 
 def finish_kernel(part_ref, proj_ref, out_ref):
@@ -245,34 +250,49 @@
 def body(corner, edge_row, source_row, proj_row, edge_col, source_col, proj_col):
     lefts, rights = lax.axis_size("left"), lax.axis_size("right")
     left, right = lax.axis_index("left"), lax.axis_index("right")
-
-    parity = [list(range(start, lefts, 2)) for start in range(2)]
-    own = lax.all_to_all(
-        jnp.broadcast_to(corner, (lefts // 2, SIZE, SIZE)), "left", 0, 0, axis_index_groups=parity, tiled=True
-    )
+    rings, chips = lefts // 4, lefts // 2
+
+    source = source_row.T // rights
+    turn = (left // 4 - source // 4) % rings
+    swap = (left // 2 + source // 2) % 2
+    slots = swap * rings + turn + jnp.where(source % 2 == left % 2, 0, chips)
+    offsets = [p * FLIPS[0] ^ q * FLIPS[1] ^ z * FLIPS[2] for p in range(2) for q in range(2) for z in range(2)]
+    peers = jnp.bitwise_xor(right, jnp.array(offsets[::-1], jnp.int32))
+    mine = jnp.reshape(right, (1,)).astype(jnp.int32)
+    inner = source_col - left * (rights * COUNT)
+    offset = jnp.bitwise_xor(inner // COUNT, right)
+    z = offset // 4
+    q = offset // 2 % 2
+    p = (offset + q) % 2
+    col_slots = (p * 4 + q * 2 + z) * COUNT + inner % COUNT
+
+    def bring(turn, swap):
+        pairs = []
+        for ring in range(rings):
+            for low in range(4):
+                pairs.append((ring * 4 + low, (ring + turn) % rings * 4 + (low ^ (2 * swap))))
+        return lax.ppermute(corner, "left", pairs)
+
+    came = {hop: bring(*hop) for hop in HOPS}
+    edge_row, slots, peers, mine, col_slots = lax.optimization_barrier((edge_row, slots, peers, mine, col_slots))
+    edge_row = load(edge_row)
+    came[HOPS[-1]], edge_row = lax.optimization_barrier((came[HOPS[-1]], edge_row))
+    own = join([came[place % rings, place // rings] if place else corner for place in range(chips)])
     other = lax.ppermute(own, "left", [(i, i ^ 1) for i in range(lefts)])
     held = jnp.concatenate([own, other], axis=0)
-    source = source_row // rights
-    slots = source // 2 + jnp.where(source % 2 == left % 2, 0, lefts // 2)
-
-    offsets = [p * FLIPS[0] ^ q * FLIPS[1] ^ z * FLIPS[2] for p in range(2) for q in range(2) for z in range(2)]
-    peers = jnp.bitwise_xor(right, jnp.array(offsets[::-1], jnp.int32))
+
     outs = row_partial(slots, peers, held, edge_row)
     came = [flip(outs[2 * part], ORDERS[part][0], rights) for part in range(3)]
     ours = meet(outs[1::2], came, 0)
     came = [flip(ours[part], ORDERS[part][1], rights) for part in range(3)]
     ours = meet(ours, came, 2)
     came = [flip(ours[part], ORDERS[part][2], rights) for part in range(3)]
-    absorbed, *parts = absorb(jnp.reshape(right, (1,)).astype(jnp.int32), ours, came, proj_row)
+    absorbed, *parts = absorb(mine, ours, came, proj_row)
+
     came = [flip(parts[part], ORDERS[part][0], rights) for part in range(3)]
+    edge_col = load(edge_col)
     pieces = [value for pair in zip(parts, came) for value in pair]
-
-    inner = source_col - left * (rights * COUNT)
-    offset = jnp.bitwise_xor(inner // COUNT, right)
-    z = offset // 4
-    q = offset // 2 % 2
-    p = (offset + q) % 2
-    partial_cols = col_partial((p * 4 + q * 2 + z) * COUNT + inner % COUNT, pieces, edge_col, lefts)
+    partial_cols = col_partial(col_slots, pieces, edge_col, lefts)
     col_parts = lax.all_to_all(partial_cols, "left", 0, 0, tiled=True)
     return absorbed, finish(col_parts, proj_col)
 

time: 103 us -> 100 us (0.971)
  blocking collectives: 37.5 us -> 18.3 us
  starting transfers between devices: 21.5 us -> 34 us
  Pallas kernels: 16.5 us -> 21.9 us
  waiting for transfers between devices: 25.4 us -> 23 us
  other arithmetic: 0.25 us -> 2.28 us
  local copies, waits for them, and re-layouts: 1.08 us -> 0.01 us
    all_to_all x1 -> x0, blocking collectives: 20.5 us -> none  [body(): lax.all_to_all(jnp.broadcast_to(corner, (lefts // 2, SIZE, SIZE)), 'left'...]
    ppermute x0 -> x7, starting transfers between devices: none -> 11.9 us  [bring(): return lax.ppermute(corner, 'left', pairs)]
    pallas_call x0 -> x3, Pallas kernels: none -> 8.56 us  [the longest x2 8.49 us: load(): pl.pallas_call(load_kernel, out_shape=pltpu.VMEM(edge.shape, edge.dtype),...]
    ppermute x12, waiting for transfers between devices: 23.2 us -> 20.7 us  [flip(): lax.ppermute(value, 'right', [(i, i ^ FLIPS[pairing]) for i in range(size)])]
    pallas_call x1, Pallas kernels: 9.8 us -> 7.82 us  [row_partial(): pl.pallas_call(row_kernel, out_shape=tuple(outs), grid_spec=pltpu.Prefetc...]
    add x2, other arithmetic: 0.06 us -> 1.44 us  [the longest x1 0.73 us: body(): col_slots = (p * 4 + q * 2 + z) * COUNT + inner % COUNT]
    all_to_all x1, blocking collectives: 17 us -> 18.3 us  [body(): col_parts = lax.all_to_all(partial_cols, 'left', 0, 0, tiled=True)]
    pallas_call x1, Pallas kernels: 4.18 us -> 2.96 us  [col_partial(): pl.pallas_call(col_kernel, out_shape=jax.ShapeDtypeStruct((pieces, sector...]
  transfers between devices with their start and end apart: 13 -> 20, of which waited for: 8 -> 8; matrix products, arithmetic and copies ran while one was open for 0% -> 2% of each run, Pallas kernels for 0% -> 8%
where the time goes in v5:
time: 100 us
  starting transfers between devices  34 us (34%)
  waiting for transfers between devices  23 us (23%)
  Pallas kernels  21.9 us (22%)
  blocking collectives  18.3 us (18%)
  other arithmetic  2.28 us (2%)
    ppermute x12, waiting for transfers between devices, flip(): lax.ppermute(value, 'right', [(i, i ^ FLIPS[pairing]) for i in range(size)])  20.7 us
    ppermute x12, starting transfers between devices, flip(): lax.ppermute(value, 'right', [(i, i ^ FLIPS[pairing]) for i in range(size)])  19.5 us
    all_to_all x1, blocking collectives, body(): col_parts = lax.all_to_all(partial_cols, 'left', 0, 0, tiled=True)  18.3 us
    ppermute x7, starting transfers between devices, bring(): return lax.ppermute(corner, 'left', pairs)  11.9 us
    pallas_call x2, Pallas kernels, load(): pl.pallas_call(load_kernel, out_shape=pltpu.VMEM(edge.shape, edge.dtype),...  8.49 us
    pallas_call x1, Pallas kernels, row_partial(): pl.pallas_call(row_kernel, out_shape=tuple(outs), grid_spec=pltpu.Prefetc...  7.82 us
    pallas_call x1, Pallas kernels, col_partial(): pl.pallas_call(col_kernel, out_shape=jax.ShapeDtypeStruct((pieces, sector...  2.96 us
    ppermute x1, starting transfers between devices, body(): other = lax.ppermute(own, 'left', [(i, i ^ 1) for i in range(lefts)])  2.58 us
  transfers between devices with their start and end apart: 20, of which 8 were waited for; matrix products, arithmetic and copies ran while one was open for 2% of the time, Pallas kernels for 8%

profile of v5, /device:TPU:1, one launch (start us, length us, event | category | flops | bytes accessed | tf_op | source)
XLA Modules:
  0.0 100.2 jit_solution(5923435238006414131)
XLA Ops:
  0.6 3.8 %collective-permute-start.1 = (bf16[1,256,256]{2,1,0:T(8,128)(2,1)}, bf16[1,256,256]{2,1,0:T(8,128)(2,1)S(1)}, u32[]{:S(2)}, u32[]{:S(2)}) collective-permute-start(bf16[1,256,256]{2,1,0:T(8,128)(2,1)} %refs_0_.1), channel_id=1, source_target_pairs={{0,64},{8,72},{16,80},{24,88},{32,96},{40,104},{48,112},{56,120},{... | collective-permute-start | bytes 393224 | tf_op jit(solution)/shard_map/ppermute | solution.py:274
  4.9 2.3 %collective-permute-start.2 = (bf16[1,256,256]{2,1,0:T(8,128)(2,1)}, bf16[1,256,256]{2,1,0:T(8,128)(2,1)S(1)}, u32[]{:S(2)}, u32[]{:S(2)}) collective-permute-start(bf16[1,256,256]{2,1,0:T(8,128)(2,1)} %refs_0_.1), channel_id=1, source_target_pairs={{0,96},{8,104},{16,112},{24,120},{32,0},{40,8},{48,16},{56,24},{64... | collective-permute-start | bytes 393224 | tf_op jit(solution)/shard_map/ppermute | solution.py:274
  7.1 1.6 %collective-permute-start.3 = (bf16[1,256,256]{2,1,0:T(8,128)(2,1)}, bf16[1,256,256]{2,1,0:T(8,128)(2,1)S(1)}, u32[]{:S(2)}, u32[]{:S(2)}) collective-permute-start(bf16[1,256,256]{2,1,0:T(8,128)(2,1)} %refs_0_.1), channel_id=1, source_target_pairs={{0,16},{8,24},{16,0},{24,8},{32,48},{40,56},{48,32},{56,40},{64,80... | collective-permute-start | bytes 393224 | tf_op jit(solution)/shard_map/ppermute | solution.py:274
  8.8 0.7 fusion.5.slot_ref
  9.5 0.7 fusion.22.slot_ref
  10.2 2.2 %collective-permute-start.5 = (bf16[1,256,256]{2,1,0:T(8,128)(2,1)}, bf16[1,256,256]{2,1,0:T(8,128)(2,1)S(1)}, u32[]{:S(2)}, u32[]{:S(2)}) collective-permute-start(bf16[1,256,256]{2,1,0:T(8,128)(2,1)} %refs_0_.1), channel_id=1, source_target_pairs={{0,80},{8,88},{16,64},{24,72},{32,112},{40,120},{48,96},{56,104},{... | collective-permute-start | bytes 393224 | tf_op jit(solution)/shard_map/ppermute | solution.py:274
  12.4 1.6 %collective-permute-start.6 = (bf16[1,256,256]{2,1,0:T(8,128)(2,1)}, bf16[1,256,256]{2,1,0:T(8,128)(2,1)S(1)}, u32[]{:S(2)}, u32[]{:S(2)}) collective-permute-start(bf16[1,256,256]{2,1,0:T(8,128)(2,1)} %refs_0_.1), channel_id=1, source_target_pairs={{0,112},{8,120},{16,96},{24,104},{32,16},{40,24},{48,0},{56,8},{64... | collective-permute-start | bytes 393224 | tf_op jit(solution)/shard_map/ppermute | solution.py:274
  14.0 0.7 broadcast_xor_fusion.peer_ref
  14.6 6.0 %load.2.edge_ref = bf16[16,8,256,256]{3,2,1,0:T(8,128)(2,1)S(1)} custom-call(bf16[16,8,256,256]{3,2,1,0:T(8,128)(2,1)} %edge_ref.1), custom_call_target="tpu_custom_call" | custom-call | bytes 33554432 | tf_op jit(solution)/shard_map/load/pallas_call | solution.py:67
  20.7 2.6 %collective-permute-start.7 = (bf16[8,256,256]{2,1,0:T(8,128)(2,1)S(1)}, bf16[8,256,256]{2,1,0:T(8,128)(2,1)S(1)}, u32[]{:S(2)}, u32[]{:S(2)}) collective-permute-start(bf16[8,256,256]{2,1,0:T(8,128)(2,1)S(1)} %join.1), channel_id=1, source_target_pairs={{0,8},{8,0},{16,24},{24,16},{32,40},{40,32},{48,56},{56,48},{64,72... | collective-permute-start | bytes 3145736 | tf_op jit(solution)/shard_map/ppermute | solution.py:281
  23.3 2.3 %collective-permute-done.7 = bf16[8,256,256]{2,1,0:T(8,128)(2,1)S(1)} collective-permute-done((bf16[8,256,256]{2,1,0:T(8,128)(2,1)S(1)}, bf16[8,256,256]{2,1,0:T(8,128)(2,1)S(1)}, u32[]{:S(2)}, u32[]{:S(2)}) %collective-permute-start.7) | collective-permute-done | bytes 1048608 | tf_op jit(solution)/shard_map/ppermute | solution.py:281
  25.8 7.8 %row_partial.1 = (bf16[4,208,256]{2,1,0:T(8,128)(2,1)S(1)}, f32[4,208,256]{2,1,0:T(8,128)S(1)}, bf16[4,176,256]{2,1,0:T(8,128)(2,1)S(1)}, f32[4,176,256]{2,1,0:T...) custom-call(s32[8,16]{1,0:T(8,128)S(1)} %fusion.5.slot_ref, s32[8]{0:T(128)S(1)} %broadcast_xor_fusion.peer_ref, ...), custom_call_target="tpu_custom_call" | custom-call | flops 4294967296 | bytes 16777216 | tf_op jit(solution)/shard_map/row_partial/pallas_call | solution.py:114
  33.6 1.3 %collective-permute-start.8 = (bf16[4,208,256]{2,1,0:T(8,128)(2,1)S(1)}, bf16[4,208,256]{2,1,0:T(8,128)(2,1)S(1)}, u32[]{:S(2)}, u32[]{:S(2)}) collective-permute-start(bf16[4,208,256]{2,1,0:T(8,128)(2,1)S(1)} %get-tuple-element.32), channel_id=1, source_target_pairs={{0,1},{1,0},{2,3},{3,2},{4,5},{5,4},{6,7},{7,6},{8,9},{9,8},{10,11... | collective-permute-start | bytes 1277960 | tf_op jit(solution)/shard_map/ppermute | solution.py:26
  34.9 1.8 %collective-permute-start.9 = (bf16[4,176,256]{2,1,0:T(8,128)(2,1)S(1)}, bf16[4,176,256]{2,1,0:T(8,128)(2,1)S(1)}, u32[]{:S(2)}, u32[]{:S(2)}) collective-permute-start(bf16[4,176,256]{2,1,0:T(8,128)(2,1)S(1)} %get-tuple-element.34), channel_id=1, source_target_pairs={{0,3},{1,2},{2,1},{3,0},{4,7},{5,6},{6,5},{7,4},{8,11},{9,10},{10,... | collective-permute-start | bytes 1081352 | tf_op jit(solution)/shard_map/ppermute | solution.py:26
  36.7 3.4 %collective-permute-start.10 = (bf16[4,128,256]{2,1,0:T(8,128)(2,1)S(1)}, bf16[4,128,256]{2,1,0:T(8,128)(2,1)S(1)}, u32[]{:S(2)}, u32[]{:S(2)}) collective-permute-start(bf16[4,128,256]{2,1,0:T(8,128)(2,1)S(1)} %get-tuple-element.36), channel_id=1, source_target_pairs={{0,4},{1,5},{2,6},{3,7},{4,0},{5,1},{6,2},{7,3},{8,12},{9,13},{10,... | collective-permute-start | bytes 786440 | tf_op jit(solution)/shard_map/ppermute | solution.py:26
  40.1 5.7 %collective-permute-done.10.refs_5_ = bf16[4,128,256]{2,1,0:T(8,128)(2,1)S(1)} collective-permute-done((bf16[4,128,256]{2,1,0:T(8,128)(2,1)S(1)}, bf16[4,128,256]{2,1,0:T(8,128)(2,1)S(1)}, u32[]{:S(2)}, u32[]{:S(2)}) %collective-permute-start.10) | collective-permute-done | bytes 262176 | tf_op jit(solution)/shard_map/ppermute | solution.py:26
  46.0 1.5 %collective-permute-start.11 = (bf16[4,208,256]{2,1,0:T(8,128)(2,1)S(1)}, bf16[4,208,256]{2,1,0:T(8,128)(2,1)S(1)}, u32[]{:S(2)}, u32[]{:S(2)}) collective-permute-start(bf16[4,208,256]{2,1,0:T(8,128)(2,1)S(1)} %get-tuple-element.37.refs_0_), channel_id=1, source_target_pairs={{0,3},{1,2},{2,1},{3,0},{4,7},{5,6},{6,5},{7,4},{8,11},{9,10},{10,... | collective-permute-start | bytes 1277960 | tf_op jit(solution)/shard_map/ppermute | solution.py:26
  47.5 3.4 %collective-permute-start.12 = (bf16[4,176,256]{2,1,0:T(8,128)(2,1)S(1)}, bf16[4,176,256]{2,1,0:T(8,128)(2,1)S(1)}, u32[]{:S(2)}, u32[]{:S(2)}) collective-permute-start(bf16[4,176,256]{2,1,0:T(8,128)(2,1)S(1)} %get-tuple-element.38.refs_2_), channel_id=1, source_target_pairs={{0,4},{1,5},{2,6},{3,7},{4,0},{5,1},{6,2},{7,3},{8,12},{9,13},{10,... | collective-permute-start | bytes 1081352 | tf_op jit(solution)/shard_map/ppermute | solution.py:26
  50.9 5.7 %collective-permute-done.13.refs_5_ = bf16[4,128,256]{2,1,0:T(8,128)(2,1)S(1)} collective-permute-done((bf16[4,128,256]{2,1,0:T(8,128)(2,1)S(1)}, bf16[4,128,256]{2,1,0:T(8,128)(2,1)S(1)}, u32[]{:S(2)}, u32[]{:S(2)}) %collective-permute-start.13) | collective-permute-done | bytes 262176 | tf_op jit(solution)/shard_map/ppermute | solution.py:26
  56.6 1.2 %collective-permute-done.12.refs_3_ = bf16[4,176,256]{2,1,0:T(8,128)(2,1)S(1)} collective-permute-done((bf16[4,176,256]{2,1,0:T(8,128)(2,1)S(1)}, bf16[4,176,256]{2,1,0:T(8,128)(2,1)S(1)}, u32[]{:S(2)}, u32[]{:S(2)}) %collective-permute-start.12) | collective-permute-done | bytes 360480 | tf_op jit(solution)/shard_map/ppermute | solution.py:26
  58.0 2.8 %collective-permute-start.14 = (bf16[4,208,256]{2,1,0:T(8,128)(2,1)S(1)}, bf16[4,208,256]{2,1,0:T(8,128)(2,1)S(1)}, u32[]{:S(2)}, u32[]{:S(2)}) collective-permute-start(bf16[4,208,256]{2,1,0:T(8,128)(2,1)S(1)} %get-tuple-element.40.refs_0_), channel_id=1, source_target_pairs={{0,4},{1,5},{2,6},{3,7},{4,0},{5,1},{6,2},{7,3},{8,12},{9,13},{10,... | collective-permute-start | bytes 1277960 | tf_op jit(solution)/shard_map/ppermute | solution.py:26
  61.0 1.2 %collective-permute-start.16 = (bf16[4,128,256]{2,1,0:T(8,128)(2,1)S(1)}, bf16[4,128,256]{2,1,0:T(8,128)(2,1)S(1)}, u32[]{:S(2)}, u32[]{:S(2)}) collective-permute-start(bf16[4,128,256]{2,1,0:T(8,128)(2,1)S(1)} %get-tuple-element.42.refs_2_), channel_id=1, source_target_pairs={{0,3},{1,2},{2,1},{3,0},{4,7},{5,6},{6,5},{7,4},{8,11},{9,10},{10,... | collective-permute-start | bytes 786440 | tf_op jit(solution)/shard_map/ppermute | solution.py:26
  62.2 5.6 %collective-permute-done.16.refs_5_ = bf16[4,128,256]{2,1,0:T(8,128)(2,1)S(1)} collective-permute-done((bf16[4,128,256]{2,1,0:T(8,128)(2,1)S(1)}, bf16[4,128,256]{2,1,0:T(8,128)(2,1)S(1)}, u32[]{:S(2)}, u32[]{:S(2)}) %collective-permute-start.16) | collective-permute-done | bytes 262176 | tf_op jit(solution)/shard_map/ppermute | solution.py:26
  67.7 0.7 collective-permute-done.14.refs_3_
  68.5 1.2 %absorb.1 = (bf16[2,256,256]{2,1,0:T(8,128)(2,1)}, bf16[4,208,256]{2,1,0:T(8,128)(2,1)S(1)}, bf16[4,176,256]{2,1,0:T(8,128)(2,1)S(1)}, bf16[4,128,256]{2,1,0:T(8,128)(2,1)S(1)}) custom-call(s32[1]{0:T(128)} %bitcast.1.index_ref, bf16[16,256,256]{2,1,0:T(8,128)(2,1)S(1)} %copy-done, bf16[4,208,256]{2,1,0:T(8,128)(2,1)S(1)} %get-tuple-element.40.refs_0_, ...), custom_call_target="tpu_custom_call" | custom-call | flops 268435456 | bytes 5242880 | tf_op jit(solution)/shard_map/absorb/pallas_call | solution.py:177
  70.3 0.8 collective-permute-start.18
  71.1 2.7 %collective-permute-start.19 = (bf16[4,128,256]{2,1,0:T(8,128)(2,1)S(1)}, bf16[4,128,256]{2,1,0:T(8,128)(2,1)S(1)}, u32[]{:S(2)}, u32[]{:S(2)}) collective-permute-start(bf16[4,128,256]{2,1,0:T(8,128)(2,1)S(1)} %get-tuple-element.47.refs_4_), channel_id=1, source_target_pairs={{0,4},{1,5},{2,6},{3,7},{4,0},{5,1},{6,2},{7,3},{8,12},{9,13},{10,... | collective-permute-start | bytes 786440 | tf_op jit(solution)/shard_map/ppermute | solution.py:26
  73.8 2.5 %load.3.refs_6_ = bf16[4,10,256,256]{3,2,1,0:T(8,128)(2,1)S(1)} custom-call(bf16[4,10,256,256]{3,2,1,0:T(8,128)(2,1)} %edge_ref.2), custom_call_target="tpu_custom_call" | custom-call | bytes 10485760 | tf_op jit(solution)/shard_map/load/pallas_call | solution.py:67
  76.4 1.4 %collective-permute-done.19.refs_5_ = bf16[4,128,256]{2,1,0:T(8,128)(2,1)S(1)} collective-permute-done((bf16[4,128,256]{2,1,0:T(8,128)(2,1)S(1)}, bf16[4,128,256]{2,1,0:T(8,128)(2,1)S(1)}, u32[]{:S(2)}, u32[]{:S(2)}) %collective-permute-start.19) | collective-permute-done | bytes 262176 | tf_op jit(solution)/shard_map/ppermute | solution.py:26
  78.1 3.0 %col_partial.1 = bf16[16,4,16,256]{3,2,1,0:T(8,128)(2,1)S(1)} custom-call(s32[4,10]{1,0:T(4,128)S(1)} %fusion.22.slot_ref, bf16[4,208,256]{2,1,0:T(8,128)(2,1)S(1)} %get-tuple-element.45.refs_0_, bf16[4,208,256]{2,1,0:T(8,128)(2,1)S(1)} %collective-permute-done.17.refs_1_, bf16[4,176,256]{2,1,0:T(8,128)(2,1)S(1)} %get-tuple-element.46.refs_2_, ...), custom_call_target="tpu_custom_call" | custom-call | flops 1342177280 | bytes 5242880 | tf_op jit(solution)/shard_map/col_partial/pallas_call | solution.py:217
  81.0 18.3 %all_to_all.5.part_ref = bf16[16,4,16,256]{3,2,1,0:T(8,128)(2,1)S(1)} all-to-all(bf16[16,4,16,256]{3,2,1,0:T(8,128)(2,1)S(1)} %col_partial.1), channel_id=1, replica_groups=mesh['left'=16,'right'=8] {'left'}, dimensions={0} | all-to-all | bytes 1048576 | tf_op jit(solution)/shard_map/all_to_all | solution.py:296
  99.3 0.9 finish.1
  (28 shorter events, 2.1 us)
Async XLA Ops:
  0.6 9.6 %collective-permute-start.1 = (bf16[1,256,256]{2,1,0:T(8,128)(2,1)}, bf16[1,256,256]{2,1,0:T(8,128)(2,1)S(1)}, u32[]{:S(2)}, u32[]{:S(2)}) collective-permute-start(bf16[1,256,256]{2,1,0:T(8,128)(2,1)} %refs_0_.1), channel_id=1, source_target_pairs={{0,64},{8,72},{16,80},{24,88},{32,96},{40,104},{48,112},{56,120},{... | collective-permute-start | bytes 393224 | tf_op jit(solution)/shard_map/ppermute | solution.py:274
  4.5 7.9 %collective-permute-start = (bf16[1,256,256]{2,1,0:T(8,128)(2,1)}, bf16[1,256,256]{2,1,0:T(8,128)(2,1)S(1)}, u32[]{:S(2)}, u32[]{:S(2)}) collective-permute-start(bf16[1,256,256]{2,1,0:T(8,128)(2,1)} %refs_0_.1), channel_id=1, source_target_pairs={{0,32},{8,40},{16,48},{24,56},{32,64},{40,72},{48,80},{56,88},{64,... | collective-permute-start | bytes 393224 | tf_op jit(solution)/shard_map/ppermute | solution.py:274
  4.9 15.7 %collective-permute-start.2 = (bf16[1,256,256]{2,1,0:T(8,128)(2,1)}, bf16[1,256,256]{2,1,0:T(8,128)(2,1)S(1)}, u32[]{:S(2)}, u32[]{:S(2)}) collective-permute-start(bf16[1,256,256]{2,1,0:T(8,128)(2,1)} %refs_0_.1), channel_id=1, source_target_pairs={{0,96},{8,104},{16,112},{24,120},{32,0},{40,8},{48,16},{56,24},{64... | collective-permute-start | bytes 393224 | tf_op jit(solution)/shard_map/ppermute | solution.py:274
  7.1 13.5 %collective-permute-start.3 = (bf16[1,256,256]{2,1,0:T(8,128)(2,1)}, bf16[1,256,256]{2,1,0:T(8,128)(2,1)S(1)}, u32[]{:S(2)}, u32[]{:S(2)}) collective-permute-start(bf16[1,256,256]{2,1,0:T(8,128)(2,1)} %refs_0_.1), channel_id=1, source_target_pairs={{0,16},{8,24},{16,0},{24,8},{32,48},{40,56},{48,32},{56,40},{64,80... | collective-permute-start | bytes 393224 | tf_op jit(solution)/shard_map/ppermute | solution.py:274
  8.8 11.8 %collective-permute-start.4 = (bf16[1,256,256]{2,1,0:T(8,128)(2,1)}, bf16[1,256,256]{2,1,0:T(8,128)(2,1)S(1)}, u32[]{:S(2)}, u32[]{:S(2)}) collective-permute-start(bf16[1,256,256]{2,1,0:T(8,128)(2,1)} %refs_0_.1), channel_id=1, source_target_pairs={{0,48},{8,56},{16,32},{24,40},{32,80},{40,88},{48,64},{56,72},{64,... | collective-permute-start | bytes 393224 | tf_op jit(solution)/shard_map/ppermute | solution.py:274
  10.2 10.4 %collective-permute-start.5 = (bf16[1,256,256]{2,1,0:T(8,128)(2,1)}, bf16[1,256,256]{2,1,0:T(8,128)(2,1)S(1)}, u32[]{:S(2)}, u32[]{:S(2)}) collective-permute-start(bf16[1,256,256]{2,1,0:T(8,128)(2,1)} %refs_0_.1), channel_id=1, source_target_pairs={{0,80},{8,88},{16,64},{24,72},{32,112},{40,120},{48,96},{56,104},{... | collective-permute-start | bytes 393224 | tf_op jit(solution)/shard_map/ppermute | solution.py:274
  12.4 8.3 %collective-permute-start.6 = (bf16[1,256,256]{2,1,0:T(8,128)(2,1)}, bf16[1,256,256]{2,1,0:T(8,128)(2,1)S(1)}, u32[]{:S(2)}, u32[]{:S(2)}) collective-permute-start(bf16[1,256,256]{2,1,0:T(8,128)(2,1)} %refs_0_.1), channel_id=1, source_target_pairs={{0,112},{8,120},{16,96},{24,104},{32,16},{40,24},{48,0},{56,8},{64... | collective-permute-start | bytes 393224 | tf_op jit(solution)/shard_map/ppermute | solution.py:274
  14.6 6.0 %copy-start.2 = (bf16[1,256,256]{2,1,0:T(8,128)(2,1)S(1)}, bf16[1,256,256]{2,1,0:T(8,128)(2,1)}, u32[]{:S(2)}) copy-start(bf16[1,256,256]{2,1,0:T(8,128)(2,1)} %refs_0_.1) | copy-start | bytes 393220
  20.7 4.9 %collective-permute-start.7 = (bf16[8,256,256]{2,1,0:T(8,128)(2,1)S(1)}, bf16[8,256,256]{2,1,0:T(8,128)(2,1)S(1)}, u32[]{:S(2)}, u32[]{:S(2)}) collective-permute-start(bf16[8,256,256]{2,1,0:T(8,128)(2,1)S(1)} %join.1), channel_id=1, source_target_pairs={{0,8},{8,0},{16,24},{24,16},{32,40},{40,32},{48,56},{56,48},{64,72... | collective-permute-start | bytes 3145736 | tf_op jit(solution)/shard_map/ppermute | solution.py:281
  33.6 12.2 %collective-permute-start.8 = (bf16[4,208,256]{2,1,0:T(8,128)(2,1)S(1)}, bf16[4,208,256]{2,1,0:T(8,128)(2,1)S(1)}, u32[]{:S(2)}, u32[]{:S(2)}) collective-permute-start(bf16[4,208,256]{2,1,0:T(8,128)(2,1)S(1)} %get-tuple-element.32), channel_id=1, source_target_pairs={{0,1},{1,0},{2,3},{3,2},{4,5},{5,4},{6,7},{7,6},{8,9},{9,8},{10,11... | collective-permute-start | bytes 1277960 | tf_op jit(solution)/shard_map/ppermute | solution.py:26
  34.9 10.9 %collective-permute-start.9 = (bf16[4,176,256]{2,1,0:T(8,128)(2,1)S(1)}, bf16[4,176,256]{2,1,0:T(8,128)(2,1)S(1)}, u32[]{:S(2)}, u32[]{:S(2)}) collective-permute-start(bf16[4,176,256]{2,1,0:T(8,128)(2,1)S(1)} %get-tuple-element.34), channel_id=1, source_target_pairs={{0,3},{1,2},{2,1},{3,0},{4,7},{5,6},{6,5},{7,4},{8,11},{9,10},{10,... | collective-permute-start | bytes 1081352 | tf_op jit(solution)/shard_map/ppermute | solution.py:26
  36.7 9.1 %collective-permute-start.10 = (bf16[4,128,256]{2,1,0:T(8,128)(2,1)S(1)}, bf16[4,128,256]{2,1,0:T(8,128)(2,1)S(1)}, u32[]{:S(2)}, u32[]{:S(2)}) collective-permute-start(bf16[4,128,256]{2,1,0:T(8,128)(2,1)S(1)} %get-tuple-element.36), channel_id=1, source_target_pairs={{0,4},{1,5},{2,6},{3,7},{4,0},{5,1},{6,2},{7,3},{8,12},{9,13},{10,... | collective-permute-start | bytes 786440 | tf_op jit(solution)/shard_map/ppermute | solution.py:26
  45.8 22.7 %copy-start = (bf16[16,256,256]{2,1,0:T(8,128)(2,1)S(1)}, bf16[16,256,256]{2,1,0:T(8,128)(2,1)}, u32[]{:S(2)}) copy-start(bf16[16,256,256]{2,1,0:T(8,128)(2,1)} %proj_ref.2) | copy-start | bytes 6291460
  46.0 11.8 %collective-permute-start.11 = (bf16[4,208,256]{2,1,0:T(8,128)(2,1)S(1)}, bf16[4,208,256]{2,1,0:T(8,128)(2,1)S(1)}, u32[]{:S(2)}, u32[]{:S(2)}) collective-permute-start(bf16[4,208,256]{2,1,0:T(8,128)(2,1)S(1)} %get-tuple-element.37.refs_0_), channel_id=1, source_target_pairs={{0,3},{1,2},{2,1},{3,0},{4,7},{5,6},{6,5},{7,4},{8,11},{9,10},{10,... | collective-permute-start | bytes 1277960 | tf_op jit(solution)/shard_map/ppermute | solution.py:26
  47.5 10.3 %collective-permute-start.12 = (bf16[4,176,256]{2,1,0:T(8,128)(2,1)S(1)}, bf16[4,176,256]{2,1,0:T(8,128)(2,1)S(1)}, u32[]{:S(2)}, u32[]{:S(2)}) collective-permute-start(bf16[4,176,256]{2,1,0:T(8,128)(2,1)S(1)} %get-tuple-element.38.refs_2_), channel_id=1, source_target_pairs={{0,4},{1,5},{2,6},{3,7},{4,0},{5,1},{6,2},{7,3},{8,12},{9,13},{10,... | collective-permute-start | bytes 1081352 | tf_op jit(solution)/shard_map/ppermute | solution.py:26
  50.9 5.7 %collective-permute-start.13 = (bf16[4,128,256]{2,1,0:T(8,128)(2,1)S(1)}, bf16[4,128,256]{2,1,0:T(8,128)(2,1)S(1)}, u32[]{:S(2)}, u32[]{:S(2)}) collective-permute-start(bf16[4,128,256]{2,1,0:T(8,128)(2,1)S(1)} %get-tuple-element.39.refs_4_), channel_id=1, source_target_pairs={{0,1},{1,0},{2,3},{3,2},{4,5},{5,4},{6,7},{7,6},{8,9},{9,8},{10,11... | collective-permute-start | bytes 786440 | tf_op jit(solution)/shard_map/ppermute | solution.py:26
  58.0 10.5 %collective-permute-start.14 = (bf16[4,208,256]{2,1,0:T(8,128)(2,1)S(1)}, bf16[4,208,256]{2,1,0:T(8,128)(2,1)S(1)}, u32[]{:S(2)}, u32[]{:S(2)}) collective-permute-start(bf16[4,208,256]{2,1,0:T(8,128)(2,1)S(1)} %get-tuple-element.40.refs_0_), channel_id=1, source_target_pairs={{0,4},{1,5},{2,6},{3,7},{4,0},{5,1},{6,2},{7,3},{8,12},{9,13},{10,... | collective-permute-start | bytes 1277960 | tf_op jit(solution)/shard_map/ppermute | solution.py:26
  60.8 7.0 %collective-permute-start.15 = (bf16[4,176,256]{2,1,0:T(8,128)(2,1)S(1)}, bf16[4,176,256]{2,1,0:T(8,128)(2,1)S(1)}, u32[]{:S(2)}, u32[]{:S(2)}) collective-permute-start(bf16[4,176,256]{2,1,0:T(8,128)(2,1)S(1)} %get-tuple-element.41.refs_1_), channel_id=1, source_target_pairs={{0,1},{1,0},{2,3},{3,2},{4,5},{5,4},{6,7},{7,6},{8,9},{9,8},{10,11... | collective-permute-start | bytes 1081352 | tf_op jit(solution)/shard_map/ppermute | solution.py:26
  61.0 6.7 %collective-permute-start.16 = (bf16[4,128,256]{2,1,0:T(8,128)(2,1)S(1)}, bf16[4,128,256]{2,1,0:T(8,128)(2,1)S(1)}, u32[]{:S(2)}, u32[]{:S(2)}) collective-permute-start(bf16[4,128,256]{2,1,0:T(8,128)(2,1)S(1)} %get-tuple-element.42.refs_2_), channel_id=1, source_target_pairs={{0,3},{1,2},{2,1},{3,0},{4,7},{5,6},{6,5},{7,4},{8,11},{9,10},{10,... | collective-permute-start | bytes 786440 | tf_op jit(solution)/shard_map/ppermute | solution.py:26
  69.7 8.3 %collective-permute-start.17 = (bf16[4,208,256]{2,1,0:T(8,128)(2,1)S(1)}, bf16[4,208,256]{2,1,0:T(8,128)(2,1)S(1)}, u32[]{:S(2)}, u32[]{:S(2)}) collective-permute-start(bf16[4,208,256]{2,1,0:T(8,128)(2,1)S(1)} %get-tuple-element.45.refs_0_), channel_id=1, source_target_pairs={{0,1},{1,0},{2,3},{3,2},{4,5},{5,4},{6,7},{7,6},{8,9},{9,8},{10,11... | collective-permute-start | bytes 1277960 | tf_op jit(solution)/shard_map/ppermute | solution.py:26
  70.3 7.8 %collective-permute-start.18 = (bf16[4,176,256]{2,1,0:T(8,128)(2,1)S(1)}, bf16[4,176,256]{2,1,0:T(8,128)(2,1)S(1)}, u32[]{:S(2)}, u32[]{:S(2)}) collective-permute-start(bf16[4,176,256]{2,1,0:T(8,128)(2,1)S(1)} %get-tuple-element.46.refs_2_), channel_id=1, source_target_pairs={{0,3},{1,2},{2,1},{3,0},{4,7},{5,6},{6,5},{7,4},{8,11},{9,10},{10,... | collective-permute-start | bytes 1081352 | tf_op jit(solution)/shard_map/ppermute | solution.py:26
  71.1 6.7 %collective-permute-start.19 = (bf16[4,128,256]{2,1,0:T(8,128)(2,1)S(1)}, bf16[4,128,256]{2,1,0:T(8,128)(2,1)S(1)}, u32[]{:S(2)}, u32[]{:S(2)}) collective-permute-start(bf16[4,128,256]{2,1,0:T(8,128)(2,1)S(1)} %get-tuple-element.47.refs_4_), channel_id=1, source_target_pairs={{0,4},{1,5},{2,6},{3,7},{4,0},{5,1},{6,2},{7,3},{8,12},{9,13},{10,... | collective-permute-start | bytes 786440 | tf_op jit(solution)/shard_map/ppermute | solution.py:26
  76.4 23.0 %copy-start.1 = (bf16[4,256,256]{2,1,0:T(8,128)(2,1)S(1)}, bf16[4,256,256]{2,1,0:T(8,128)(2,1)}, u32[]{:S(2)}) copy-start(bf16[4,256,256]{2,1,0:T(8,128)(2,1)} %proj_ref.3) | copy-start | bytes 1572868

commit v6 on v5

--- a/solution.py
+++ b/solution.py
@@ -12,7 +12,7 @@
 SIZE = 256
 COUNT = 2
 FLAT = COUNT * SIZE
-HOPS = ((2, 1), (1, 1), (3, 1), (0, 1), (1, 0), (3, 0), (2, 0))
+HOPS = ((2, 1), (1, 1), (3, 1), (0, 1), (2, 0), (1, 0), (3, 0))
 DEPTH = 4
 FLIPS = (1, 3, 4)
 ORDERS = ((0, 1, 2), (1, 2, 0), (2, 0, 1))
@@ -76,54 +76,72 @@
     )(pltpu.with_memory_space_constraint(edge, pltpu.HBM))
 
 
-def row_kernel(slot_ref, peer_ref, held_ref, edge_ref, *out_refs):
+def row_kernel(source_ref, held_ref, edge_ref, *out_refs):
+    rights, rings = lax.axis_size("right"), lax.axis_size("left") // 4
+    left, right = lax.axis_index("left"), lax.axis_index("right")
+
+    def slot(entry, sector):
+        source = source_ref[entry, sector] // rights
+        turn = (left // 4 - source // 4 + rings) % rings
+        swap = (left // 2 + source // 2) % 2
+        return ((source + left) % 2 * 2 + swap) * rings + turn
+
+    def sums(place):
+        offset = place // 4 * FLIPS[0] ^ place // 2 % 2 * FLIPS[1] ^ place % 2 * FLIPS[2]
+        first = (right ^ offset) * COUNT
+        values = []
+        for sector in range(COUNT):
+            here = first + sector
+            total = jnp.dot(held_ref[slot(0, here)], edge_ref[here, 0], preferred_element_type=F32)
+            for entry in range(1, edge_ref.shape[1]):
+                total += jnp.dot(held_ref[slot(entry, here)], edge_ref[here, entry], preferred_element_type=F32)
+            values.append(total.T)
+        return jnp.concatenate(values, axis=0)
+
     step = pl.program_id(0)
-    place = pl.num_programs(0) - 1 - step
-    first = peer_ref[step] * COUNT
-
-    values = []
-    for sector in range(COUNT):
-        total = jnp.dot(held_ref[slot_ref[0, first + sector]], edge_ref[first + sector, 0], preferred_element_type=F32)
-        for entry in range(1, edge_ref.shape[1]):
-            total += jnp.dot(
-                held_ref[slot_ref[entry, first + sector]], edge_ref[first + sector, entry], preferred_element_type=F32
-            )
-        values.append(total.T)
-    flat = jnp.concatenate(values, axis=0)
-    for part, order in enumerate(ORDERS):
-        index = place_of(place, order)
-        send_ref, keep_ref = out_refs[2 * part], out_refs[2 * part + 1]
-        value = flat[CUTS[part] : CUTS[part + 1]]
-
-        @pl.when(index >= 4)
-        def _():
-            send_ref[index - 4] = value.astype(BF16)
-
-        @pl.when(index < 4)
-        def _():
-            keep_ref[index] = value
-
-
-def row_partial(slots, peers, held, edge_row):
+    for last in range(2):
+        place = (pl.num_programs(0) - 1 - step) * 2 + last
+        flat = sums(place)
+        for part, order in enumerate(ORDERS):
+            index = place_of(place, order)
+            send_ref, keep_ref = out_refs[2 * part], out_refs[2 * part + 1]
+            value = flat[CUTS[part] : CUTS[part + 1]]
+            if order[0] == 2:
+                if last:
+                    send_ref[index - 4] = value.astype(BF16)
+                else:
+                    keep_ref[index] = value
+                continue
+
+            @pl.when(index >= 4)
+            def _():
+                send_ref[index - 4] = value.astype(BF16)
+
+            @pl.when(index < 4)
+            def _():
+                keep_ref[index] = value
+
+
+def row_partial(source, held, edge_row):
     entries = edge_row.shape[1]
-    steps = peers.shape[0]
+    steps = edge_row.shape[0] // (2 * COUNT)
     outs = []
     for length in LENGTHS:
-        outs.append(jax.ShapeDtypeStruct((steps // 2, length, SIZE), BF16))
-        outs.append(jax.ShapeDtypeStruct((steps // 2, length, SIZE), F32))
+        outs.append(jax.ShapeDtypeStruct((4, length, SIZE), BF16))
+        outs.append(jax.ShapeDtypeStruct((4, length, SIZE), F32))
     return pl.pallas_call(
         row_kernel,
         out_shape=tuple(outs),
         grid_spec=pltpu.PrefetchScalarGridSpec(
-            num_scalar_prefetch=2,
+            num_scalar_prefetch=1,
             grid=(steps,),
             in_specs=[VMEM, VMEM],
             out_specs=tuple(VMEM for _ in outs),
         ),
         compiler_params=SMALL,
-        cost_estimate=cost(2 * steps * COUNT * entries * SIZE**3, steps * COUNT * entries * SIZE**2),
+        cost_estimate=cost(4 * steps * COUNT * entries * SIZE**3, steps * COUNT * entries * SIZE**2),
         name="row_partial",
-    )(slots, peers, held, edge_row)
+    )(source, held, edge_row)
 
 
 def meet_kernel(turn, *refs):
@@ -146,14 +164,15 @@
     )(*args)
 
 
-def absorb_kernel(index_ref, proj_ref, *refs):
+def absorb_kernel(proj_ref, *refs):
+    right = lax.axis_index("right")
     ours_refs, came_refs, out_ref, part_refs = refs[:3], refs[3:6], refs[6], refs[7:]
     mine = []
     for part, order in enumerate(ORDERS):
         low, high = CUTS[part], CUTS[part + 1]
         for place in range(4):
             offset = place // 2 * FLIPS[order[1]] ^ place % 2 * FLIPS[order[2]]
-            first = (index_ref[0] ^ offset) * COUNT
+            first = (right ^ offset) * COUNT
             total = (ours_refs[part][place].astype(F32) + came_refs[part][place ^ 1].astype(F32)).astype(BF16)
             pieces = []
             for sector in range(COUNT):
@@ -171,21 +190,21 @@
         out_ref[sector] = flat[sector * SIZE : (sector + 1) * SIZE].T
 
 
-def absorb(index, ours, came, proj_row):
+def absorb(ours, came, proj_row):
     outs = [jax.ShapeDtypeStruct((COUNT, SIZE, SIZE), BF16)]
     outs += [jax.ShapeDtypeStruct((4, length, SIZE), BF16) for length in LENGTHS]
     return pl.pallas_call(
         absorb_kernel,
         out_shape=tuple(outs),
-        in_specs=[pl.BlockSpec(memory_space=pltpu.SMEM)] + [VMEM] * 7,
+        in_specs=[VMEM] * 7,
         out_specs=tuple(VMEM for _ in outs),
         compiler_params=SMALL,
         cost_estimate=cost(8 * COUNT * SIZE**3, 20 * FLAT * SIZE),
         name="absorb",
-    )(index, proj_row, *ours, *came)
-
-
-def col_kernel(slot_ref, *refs):
+    )(proj_row, *ours, *came)
+
+
+def col_kernel(source_ref, *refs):
     piece_refs, (edge_ref, out_ref, held) = refs[:6], refs[6:]
     step = pl.program_id(0)
 
@@ -197,8 +216,16 @@
                 start = place * FLAT + CUTS[part]
                 held[start : start + LENGTHS[part]] = piece_refs[2 * part + index // 4][index % 4]
 
+    rights, left, right = lax.axis_size("right"), lax.axis_index("left"), lax.axis_index("right")
+
     def block(entry):
-        return held[pl.ds(pl.multiple_of(slot_ref[step, entry] * SIZE, SIZE), SIZE)]
+        inner = source_ref[step, entry] - left * (rights * COUNT)
+        offset = inner // COUNT ^ right
+        z = offset // 4
+        q = offset // 2 % 2
+        p = (offset + q) % 2
+        slot = (p * 4 + q * 2 + z) * COUNT + inner % COUNT
+        return held[pl.ds(pl.multiple_of(slot * SIZE, SIZE), SIZE)]
 
     def term(entry):
         return lax.dot_general(
@@ -249,22 +276,7 @@
 
 def body(corner, edge_row, source_row, proj_row, edge_col, source_col, proj_col):
     lefts, rights = lax.axis_size("left"), lax.axis_size("right")
-    left, right = lax.axis_index("left"), lax.axis_index("right")
-    rings, chips = lefts // 4, lefts // 2
-
-    source = source_row.T // rights
-    turn = (left // 4 - source // 4) % rings
-    swap = (left // 2 + source // 2) % 2
-    slots = swap * rings + turn + jnp.where(source % 2 == left % 2, 0, chips)
-    offsets = [p * FLIPS[0] ^ q * FLIPS[1] ^ z * FLIPS[2] for p in range(2) for q in range(2) for z in range(2)]
-    peers = jnp.bitwise_xor(right, jnp.array(offsets[::-1], jnp.int32))
-    mine = jnp.reshape(right, (1,)).astype(jnp.int32)
-    inner = source_col - left * (rights * COUNT)
-    offset = jnp.bitwise_xor(inner // COUNT, right)
-    z = offset // 4
-    q = offset // 2 % 2
-    p = (offset + q) % 2
-    col_slots = (p * 4 + q * 2 + z) * COUNT + inner % COUNT
+    rings = lefts // 4
 
     def bring(turn, swap):
         pairs = []
@@ -274,25 +286,27 @@
         return lax.ppermute(corner, "left", pairs)
 
     came = {hop: bring(*hop) for hop in HOPS}
-    edge_row, slots, peers, mine, col_slots = lax.optimization_barrier((edge_row, slots, peers, mine, col_slots))
     edge_row = load(edge_row)
     came[HOPS[-1]], edge_row = lax.optimization_barrier((came[HOPS[-1]], edge_row))
-    own = join([came[place % rings, place // rings] if place else corner for place in range(chips)])
-    other = lax.ppermute(own, "left", [(i, i ^ 1) for i in range(lefts)])
-    held = jnp.concatenate([own, other], axis=0)
-
-    outs = row_partial(slots, peers, held, edge_row)
+    owns, others = [], []
+    for far in (1, 0):
+        blocks = [came[turn, far] if turn or far else corner for turn in range(rings)]
+        owns.insert(0, join(blocks))
+        others.insert(0, lax.ppermute(owns[0], "left", [(i, i ^ 1) for i in range(lefts)]))
+    held = jnp.concatenate(owns + others, axis=0)
+
+    outs = row_partial(source_row.T, held, edge_row)
     came = [flip(outs[2 * part], ORDERS[part][0], rights) for part in range(3)]
     ours = meet(outs[1::2], came, 0)
     came = [flip(ours[part], ORDERS[part][1], rights) for part in range(3)]
     ours = meet(ours, came, 2)
     came = [flip(ours[part], ORDERS[part][2], rights) for part in range(3)]
-    absorbed, *parts = absorb(mine, ours, came, proj_row)
+    absorbed, *parts = absorb(ours, came, proj_row)
 
     came = [flip(parts[part], ORDERS[part][0], rights) for part in range(3)]
     edge_col = load(edge_col)
     pieces = [value for pair in zip(parts, came) for value in pair]
-    partial_cols = col_partial(col_slots, pieces, edge_col, lefts)
+    partial_cols = col_partial(source_col, pieces, edge_col, lefts)
     col_parts = lax.all_to_all(partial_cols, "left", 0, 0, tiled=True)
     return absorbed, finish(col_parts, proj_col)
 

time: 100 us -> 99.7 us (level)
  other arithmetic: 2.28 us -> 0.26 us
  starting transfers between devices: 34 us -> 35.8 us
    ppermute x1 -> x2, starting transfers between devices: 2.58 us -> 5.38 us  [body(): lax.ppermute(owns[0], 'left', [(i, i ^ 1) for i in range(lefts)])]
    add x2 -> x0, other arithmetic: 1.44 us -> none  [the longest x1 0.73 us: body(): col_slots = (p * 4 + q * 2 + z) * COUNT + inner % COUNT]
    ppermute x7, starting transfers between devices: 11.9 us -> 10.8 us  [bring(): return lax.ppermute(corner, 'left', pairs)]
    ppermute x7, waiting for transfers between devices: 0.02 us -> 1.07 us  [bring(): return lax.ppermute(corner, 'left', pairs)]
    ppermute x1 -> x2, waiting for transfers between devices: 2.29 us -> 1.54 us  [body(): lax.ppermute(owns[0], 'left', [(i, i ^ 1) for i in range(lefts)])]
  transfers between devices with their start and end apart: 20 -> 21, of which waited for: 8 -> 10; matrix products, arithmetic and copies ran while one was open for 2% -> 0% of each run, Pallas kernels for 8% -> 9%
where the time goes in v6:
time: 99.7 us; the launch traced here: 99.6 us
  starting transfers between devices  35.8 us (36%)
  waiting for transfers between devices  23.3 us (23%)
  Pallas kernels  22 us (22%)
  blocking collectives  17.5 us (18%)
    ppermute x12, waiting for transfers between devices, flip(): lax.ppermute(value, 'right', [(i, i ^ FLIPS[pairing]) for i in range(size)])  20.7 us
    ppermute x12, starting transfers between devices, flip(): lax.ppermute(value, 'right', [(i, i ^ FLIPS[pairing]) for i in range(size)])  19.6 us
    all_to_all x1, blocking collectives, body(): col_parts = lax.all_to_all(partial_cols, 'left', 0, 0, tiled=True)  17.5 us
    ppermute x7, starting transfers between devices, bring(): return lax.ppermute(corner, 'left', pairs)  10.8 us
    pallas_call x2, Pallas kernels, load(): pl.pallas_call(load_kernel, out_shape=pltpu.VMEM(edge.shape, edge.dtype),...  8.46 us
    pallas_call x1, Pallas kernels, row_partial(): pl.pallas_call(row_kernel, out_shape=tuple(outs), grid_spec=pltpu.Prefetc...  7.81 us
    ppermute x2, starting transfers between devices, body(): lax.ppermute(owns[0], 'left', [(i, i ^ 1) for i in range(lefts)])  5.38 us
    pallas_call x1, Pallas kernels, col_partial(): pl.pallas_call(col_kernel, out_shape=jax.ShapeDtypeStruct((pieces, sector...  3.14 us
  transfers between devices with their start and end apart: 21, of which 10 were waited for; matrix products, arithmetic and copies ran while one was open for 0% of the time, Pallas kernels for 9%

profile of v6, /device:TPU:1, one launch (start us, length us, event | category | flops | bytes accessed | tf_op | source)
XLA Modules:
  0.0 99.6 jit_solution(12868912721688631711)
XLA Ops:
  0.6 3.6 %collective-permute-start.2 = (bf16[1,256,256]{2,1,0:T(8,128)(2,1)}, bf16[1,256,256]{2,1,0:T(8,128)(2,1)S(1)}, u32[]{:S(2)}, u32[]{:S(2)}) collective-permute-start(bf16[1,256,256]{2,1,0:T(8,128)(2,1)} %refs_0_.1), channel_id=1, source_target_pairs={{0,96},{8,104},{16,112},{24,120},{32,0},{40,8},{48,16},{56,24},{64... | collective-permute-start | bytes 393224 | tf_op jit(solution)/shard_map/ppermute | solution.py:286
  4.3 1.6 %collective-permute-start.1 = (bf16[1,256,256]{2,1,0:T(8,128)(2,1)}, bf16[1,256,256]{2,1,0:T(8,128)(2,1)S(1)}, u32[]{:S(2)}, u32[]{:S(2)}) collective-permute-start(bf16[1,256,256]{2,1,0:T(8,128)(2,1)} %refs_0_.1), channel_id=1, source_target_pairs={{0,64},{8,72},{16,80},{24,88},{32,96},{40,104},{48,112},{56,120},{... | collective-permute-start | bytes 393224 | tf_op jit(solution)/shard_map/ppermute | solution.py:286
  5.9 1.6 %collective-permute-start.3 = (bf16[1,256,256]{2,1,0:T(8,128)(2,1)}, bf16[1,256,256]{2,1,0:T(8,128)(2,1)S(1)}, u32[]{:S(2)}, u32[]{:S(2)}) collective-permute-start(bf16[1,256,256]{2,1,0:T(8,128)(2,1)} %refs_0_.1), channel_id=1, source_target_pairs={{0,16},{8,24},{16,0},{24,8},{32,48},{40,56},{48,32},{56,40},{64,80... | collective-permute-start | bytes 393224 | tf_op jit(solution)/shard_map/ppermute | solution.py:286
  7.6 1.3 %collective-permute-start.4 = (bf16[1,256,256]{2,1,0:T(8,128)(2,1)}, bf16[1,256,256]{2,1,0:T(8,128)(2,1)S(1)}, u32[]{:S(2)}, u32[]{:S(2)}) collective-permute-start(bf16[1,256,256]{2,1,0:T(8,128)(2,1)} %refs_0_.1), channel_id=1, source_target_pairs={{0,48},{8,56},{16,32},{24,40},{32,80},{40,88},{48,64},{56,72},{64,... | collective-permute-start | bytes 393224 | tf_op jit(solution)/shard_map/ppermute | solution.py:286
  8.9 1.8 %collective-permute-start.5 = (bf16[1,256,256]{2,1,0:T(8,128)(2,1)}, bf16[1,256,256]{2,1,0:T(8,128)(2,1)S(1)}, u32[]{:S(2)}, u32[]{:S(2)}) collective-permute-start(bf16[1,256,256]{2,1,0:T(8,128)(2,1)} %refs_0_.1), channel_id=1, source_target_pairs={{0,80},{8,88},{16,64},{24,72},{32,112},{40,120},{48,96},{56,104},{... | collective-permute-start | bytes 393224 | tf_op jit(solution)/shard_map/ppermute | solution.py:286
  10.7 1.1 %collective-permute-done.refs_1_ = bf16[1,256,256]{2,1,0:T(8,128)(2,1)S(1)} collective-permute-done((bf16[1,256,256]{2,1,0:T(8,128)(2,1)}, bf16[1,256,256]{2,1,0:T(8,128)(2,1)S(1)}, u32[]{:S(2)}, u32[]{:S(2)}) %collective-permute-start) | collective-permute-done | bytes 131104 | tf_op jit(solution)/shard_map/ppermute | solution.py:286
  11.7 0.7 collective-permute-start.6
  12.5 5.9 %load.2.edge_ref = bf16[16,8,256,256]{3,2,1,0:T(8,128)(2,1)S(1)} custom-call(bf16[16,8,256,256]{3,2,1,0:T(8,128)(2,1)} %edge_ref.2), custom_call_target="tpu_custom_call" | custom-call | bytes 33554432 | tf_op jit(solution)/shard_map/load/pallas_call | solution.py:67
  18.5 4.1 %collective-permute-start.7 = (bf16[4,256,256]{2,1,0:T(8,128)(2,1)S(1)}, bf16[4,256,256]{2,1,0:T(8,128)(2,1)S(1)}, u32[]{:S(2)}, u32[]{:S(2)}) collective-permute-start(bf16[4,256,256]{2,1,0:T(8,128)(2,1)S(1)} %join.2), channel_id=1, source_target_pairs={{0,8},{8,0},{16,24},{24,16},{32,40},{40,32},{48,56},{56,48},{64,72... | collective-permute-start | bytes 1572872 | tf_op jit(solution)/shard_map/ppermute | solution.py:295
  22.6 1.3 %collective-permute-start.8 = (bf16[4,256,256]{2,1,0:T(8,128)(2,1)S(1)}, bf16[4,256,256]{2,1,0:T(8,128)(2,1)S(1)}, u32[]{:S(2)}, u32[]{:S(2)}) collective-permute-start(bf16[4,256,256]{2,1,0:T(8,128)(2,1)S(1)} %join.3), channel_id=1, source_target_pairs={{0,8},{8,0},{16,24},{24,16},{32,40},{40,32},{48,56},{56,48},{64,72... | collective-permute-start | bytes 1572872 | tf_op jit(solution)/shard_map/ppermute | solution.py:295
  24.1 1.4 %collective-permute-done.8 = bf16[4,256,256]{2,1,0:T(8,128)(2,1)S(1)} collective-permute-done((bf16[4,256,256]{2,1,0:T(8,128)(2,1)S(1)}, bf16[4,256,256]{2,1,0:T(8,128)(2,1)S(1)}, u32[]{:S(2)}, u32[]{:S(2)}) %collective-permute-start.8) | collective-permute-done | bytes 524320 | tf_op jit(solution)/shard_map/ppermute | solution.py:295
  25.7 7.8 %row_partial.1 = (bf16[4,208,256]{2,1,0:T(8,128)(2,1)S(1)}, f32[4,208,256]{2,1,0:T(8,128)S(1)}, bf16[4,176,256]{2,1,0:T(8,128)(2,1)S(1)}, f32[4,176,256]{2,1,0:T...) custom-call(s32[8,16]{1,0:T(8,128)S(1)} %bitcast.1, ...), custom_call_target="tpu_custom_call" | custom-call | flops 4294967296 | bytes 8388608 | tf_op jit(solution)/shard_map/row_partial/pallas_call | solution.py:132
  33.6 1.3 %collective-permute-start.9 = (bf16[4,208,256]{2,1,0:T(8,128)(2,1)S(1)}, bf16[4,208,256]{2,1,0:T(8,128)(2,1)S(1)}, u32[]{:S(2)}, u32[]{:S(2)}) collective-permute-start(bf16[4,208,256]{2,1,0:T(8,128)(2,1)S(1)} %get-tuple-element.23), channel_id=1, source_target_pairs={{0,1},{1,0},{2,3},{3,2},{4,5},{5,4},{6,7},{7,6},{8,9},{9,8},{10,11... | collective-permute-start | bytes 1277960 | tf_op jit(solution)/shard_map/ppermute | solution.py:26
  34.9 1.8 %collective-permute-start.10 = (bf16[4,176,256]{2,1,0:T(8,128)(2,1)S(1)}, bf16[4,176,256]{2,1,0:T(8,128)(2,1)S(1)}, u32[]{:S(2)}, u32[]{:S(2)}) collective-permute-start(bf16[4,176,256]{2,1,0:T(8,128)(2,1)S(1)} %get-tuple-element.25), channel_id=1, source_target_pairs={{0,3},{1,2},{2,1},{3,0},{4,7},{5,6},{6,5},{7,4},{8,11},{9,10},{10,... | collective-permute-start | bytes 1081352 | tf_op jit(solution)/shard_map/ppermute | solution.py:26
  36.7 3.4 %collective-permute-start.11 = (bf16[4,128,256]{2,1,0:T(8,128)(2,1)S(1)}, bf16[4,128,256]{2,1,0:T(8,128)(2,1)S(1)}, u32[]{:S(2)}, u32[]{:S(2)}) collective-permute-start(bf16[4,128,256]{2,1,0:T(8,128)(2,1)S(1)} %get-tuple-element.27), channel_id=1, source_target_pairs={{0,4},{1,5},{2,6},{3,7},{4,0},{5,1},{6,2},{7,3},{8,12},{9,13},{10,... | collective-permute-start | bytes 786440 | tf_op jit(solution)/shard_map/ppermute | solution.py:26
  40.1 5.7 %collective-permute-done.11.refs_5_ = bf16[4,128,256]{2,1,0:T(8,128)(2,1)S(1)} collective-permute-done((bf16[4,128,256]{2,1,0:T(8,128)(2,1)S(1)}, bf16[4,128,256]{2,1,0:T(8,128)(2,1)S(1)}, u32[]{:S(2)}, u32[]{:S(2)}) %collective-permute-start.11) | collective-permute-done | bytes 262176 | tf_op jit(solution)/shard_map/ppermute | solution.py:26
  46.0 1.4 %collective-permute-start.12 = (bf16[4,208,256]{2,1,0:T(8,128)(2,1)S(1)}, bf16[4,208,256]{2,1,0:T(8,128)(2,1)S(1)}, u32[]{:S(2)}, u32[]{:S(2)}) collective-permute-start(bf16[4,208,256]{2,1,0:T(8,128)(2,1)S(1)} %get-tuple-element.28.refs_0_), channel_id=1, source_target_pairs={{0,3},{1,2},{2,1},{3,0},{4,7},{5,6},{6,5},{7,4},{8,11},{9,10},{10,... | collective-permute-start | bytes 1277960 | tf_op jit(solution)/shard_map/ppermute | solution.py:26
  47.4 3.5 %collective-permute-start.13 = (bf16[4,176,256]{2,1,0:T(8,128)(2,1)S(1)}, bf16[4,176,256]{2,1,0:T(8,128)(2,1)S(1)}, u32[]{:S(2)}, u32[]{:S(2)}) collective-permute-start(bf16[4,176,256]{2,1,0:T(8,128)(2,1)S(1)} %get-tuple-element.29.refs_2_), channel_id=1, source_target_pairs={{0,4},{1,5},{2,6},{3,7},{4,0},{5,1},{6,2},{7,3},{8,12},{9,13},{10,... | collective-permute-start | bytes 1081352 | tf_op jit(solution)/shard_map/ppermute | solution.py:26
  50.9 5.7 %collective-permute-done.14.refs_5_ = bf16[4,128,256]{2,1,0:T(8,128)(2,1)S(1)} collective-permute-done((bf16[4,128,256]{2,1,0:T(8,128)(2,1)S(1)}, bf16[4,128,256]{2,1,0:T(8,128)(2,1)S(1)}, u32[]{:S(2)}, u32[]{:S(2)}) %collective-permute-start.14) | collective-permute-done | bytes 262176 | tf_op jit(solution)/shard_map/ppermute | solution.py:26
  56.6 1.2 %collective-permute-done.13.refs_3_ = bf16[4,176,256]{2,1,0:T(8,128)(2,1)S(1)} collective-permute-done((bf16[4,176,256]{2,1,0:T(8,128)(2,1)S(1)}, bf16[4,176,256]{2,1,0:T(8,128)(2,1)S(1)}, u32[]{:S(2)}, u32[]{:S(2)}) %collective-permute-start.13) | collective-permute-done | bytes 360480 | tf_op jit(solution)/shard_map/ppermute | solution.py:26
  58.0 2.8 %collective-permute-start.15 = (bf16[4,208,256]{2,1,0:T(8,128)(2,1)S(1)}, bf16[4,208,256]{2,1,0:T(8,128)(2,1)S(1)}, u32[]{:S(2)}, u32[]{:S(2)}) collective-permute-start(bf16[4,208,256]{2,1,0:T(8,128)(2,1)S(1)} %get-tuple-element.31.refs_0_), channel_id=1, source_target_pairs={{0,4},{1,5},{2,6},{3,7},{4,0},{5,1},{6,2},{7,3},{8,12},{9,13},{10,... | collective-permute-start | bytes 1277960 | tf_op jit(solution)/shard_map/ppermute | solution.py:26
  61.0 1.2 %collective-permute-start.17 = (bf16[4,128,256]{2,1,0:T(8,128)(2,1)S(1)}, bf16[4,128,256]{2,1,0:T(8,128)(2,1)S(1)}, u32[]{:S(2)}, u32[]{:S(2)}) collective-permute-start(bf16[4,128,256]{2,1,0:T(8,128)(2,1)S(1)} %get-tuple-element.33.refs_2_), channel_id=1, source_target_pairs={{0,3},{1,2},{2,1},{3,0},{4,7},{5,6},{6,5},{7,4},{8,11},{9,10},{10,... | collective-permute-start | bytes 786440 | tf_op jit(solution)/shard_map/ppermute | solution.py:26
  62.2 5.6 %collective-permute-done.17.refs_5_ = bf16[4,128,256]{2,1,0:T(8,128)(2,1)S(1)} collective-permute-done((bf16[4,128,256]{2,1,0:T(8,128)(2,1)S(1)}, bf16[4,128,256]{2,1,0:T(8,128)(2,1)S(1)}, u32[]{:S(2)}, u32[]{:S(2)}) %collective-permute-start.17) | collective-permute-done | bytes 262176 | tf_op jit(solution)/shard_map/ppermute | solution.py:26
  67.8 0.7 collective-permute-done.15.refs_3_
  68.5 1.2 %absorb.1 = (bf16[2,256,256]{2,1,0:T(8,128)(2,1)}, bf16[4,208,256]{2,1,0:T(8,128)(2,1)S(1)}, bf16[4,176,256]{2,1,0:T(8,128)(2,1)S(1)}, bf16[4,128,256]{2,1,0:T(8,128)(2,1)S(1)}) custom-call(bf16[16,256,256]{2,1,0:T(8,128)(2,1)S(1)} %copy-done, bf16[4,208,256]{2,1,0:T(8,128)(2,1)S(1)} %get-tuple-element.31.refs_0_, ...), custom_call_target="tpu_custom_call" | custom-call | flops 268435456 | bytes 5242880 | tf_op jit(solution)/shard_map/absorb/pallas_call | solution.py:196
  70.3 0.8 collective-permute-start.19
  71.1 2.7 %collective-permute-start.20 = (bf16[4,128,256]{2,1,0:T(8,128)(2,1)S(1)}, bf16[4,128,256]{2,1,0:T(8,128)(2,1)S(1)}, u32[]{:S(2)}, u32[]{:S(2)}) collective-permute-start(bf16[4,128,256]{2,1,0:T(8,128)(2,1)S(1)} %get-tuple-element.37.refs_4_), channel_id=1, source_target_pairs={{0,4},{1,5},{2,6},{3,7},{4,0},{5,1},{6,2},{7,3},{8,12},{9,13},{10,... | collective-permute-start | bytes 786440 | tf_op jit(solution)/shard_map/ppermute | solution.py:26
  73.8 2.5 %load.3.refs_6_ = bf16[4,10,256,256]{3,2,1,0:T(8,128)(2,1)S(1)} custom-call(bf16[4,10,256,256]{3,2,1,0:T(8,128)(2,1)} %edge_ref.3), custom_call_target="tpu_custom_call" | custom-call | bytes 10485760 | tf_op jit(solution)/shard_map/load/pallas_call | solution.py:67
  76.4 1.4 %collective-permute-done.20.refs_5_ = bf16[4,128,256]{2,1,0:T(8,128)(2,1)S(1)} collective-permute-done((bf16[4,128,256]{2,1,0:T(8,128)(2,1)S(1)}, bf16[4,128,256]{2,1,0:T(8,128)(2,1)S(1)}, u32[]{:S(2)}, u32[]{:S(2)}) %collective-permute-start.20) | collective-permute-done | bytes 262176 | tf_op jit(solution)/shard_map/ppermute | solution.py:26
  78.1 3.1 %col_partial.1 = bf16[16,4,16,256]{3,2,1,0:T(8,128)(2,1)S(1)} custom-call(s32[4,10]{1,0:T(4,128)S(1)} %copy-done.4, bf16[4,208,256]{2,1,0:T(8,128)(2,1)S(1)} %get-tuple-element.35.refs_0_, bf16[4,208,256]{2,1,0:T(8,128)(2,1)S(1)} %collective-permute-done.18.refs_1_, bf16[4,176,256]{2,1,0:T(8,128)(2,1)S(1)} %get-tuple-element.36.refs_2_, ...), custom_call_target="tpu_custom_call" | custom-call | flops 1342177280 | bytes 5242880 | tf_op jit(solution)/shard_map/col_partial/pallas_call | solution.py:244
  81.2 17.5 %all_to_all.5.part_ref = bf16[16,4,16,256]{3,2,1,0:T(8,128)(2,1)S(1)} all-to-all(bf16[16,4,16,256]{3,2,1,0:T(8,128)(2,1)S(1)} %col_partial.1), channel_id=1, replica_groups=mesh['left'=16,'right'=8] {'left'}, dimensions={0} | all-to-all | bytes 1048576 | tf_op jit(solution)/shard_map/all_to_all | solution.py:310
  98.7 0.9 finish.1
  (32 shorter events, 2.0 us)
Async XLA Ops:
  0.6 17.8 %copy-start.2 = (bf16[1,256,256]{2,1,0:T(8,128)(2,1)S(1)}, bf16[1,256,256]{2,1,0:T(8,128)(2,1)}, u32[]{:S(2)}) copy-start(bf16[1,256,256]{2,1,0:T(8,128)(2,1)} %refs_0_.1) | copy-start | bytes 393220
  0.6 8.2 %collective-permute-start.2 = (bf16[1,256,256]{2,1,0:T(8,128)(2,1)}, bf16[1,256,256]{2,1,0:T(8,128)(2,1)S(1)}, u32[]{:S(2)}, u32[]{:S(2)}) collective-permute-start(bf16[1,256,256]{2,1,0:T(8,128)(2,1)} %refs_0_.1), channel_id=1, source_target_pairs={{0,96},{8,104},{16,112},{24,120},{32,0},{40,8},{48,16},{56,24},{64... | collective-permute-start | bytes 393224 | tf_op jit(solution)/shard_map/ppermute | solution.py:286
  4.3 7.5 %collective-permute-start = (bf16[1,256,256]{2,1,0:T(8,128)(2,1)}, bf16[1,256,256]{2,1,0:T(8,128)(2,1)S(1)}, u32[]{:S(2)}, u32[]{:S(2)}) collective-permute-start(bf16[1,256,256]{2,1,0:T(8,128)(2,1)} %refs_0_.1), channel_id=1, source_target_pairs={{0,32},{8,40},{16,48},{24,56},{32,64},{40,72},{48,80},{56,88},{64,... | collective-permute-start | bytes 393224 | tf_op jit(solution)/shard_map/ppermute | solution.py:286
  4.3 14.1 %collective-permute-start.1 = (bf16[1,256,256]{2,1,0:T(8,128)(2,1)}, bf16[1,256,256]{2,1,0:T(8,128)(2,1)S(1)}, u32[]{:S(2)}, u32[]{:S(2)}) collective-permute-start(bf16[1,256,256]{2,1,0:T(8,128)(2,1)} %refs_0_.1), channel_id=1, source_target_pairs={{0,64},{8,72},{16,80},{24,88},{32,96},{40,104},{48,112},{56,120},{... | collective-permute-start | bytes 393224 | tf_op jit(solution)/shard_map/ppermute | solution.py:286
  5.9 16.6 %collective-permute-start.3 = (bf16[1,256,256]{2,1,0:T(8,128)(2,1)}, bf16[1,256,256]{2,1,0:T(8,128)(2,1)S(1)}, u32[]{:S(2)}, u32[]{:S(2)}) collective-permute-start(bf16[1,256,256]{2,1,0:T(8,128)(2,1)} %refs_0_.1), channel_id=1, source_target_pairs={{0,16},{8,24},{16,0},{24,8},{32,48},{40,56},{48,32},{56,40},{64,80... | collective-permute-start | bytes 393224 | tf_op jit(solution)/shard_map/ppermute | solution.py:286
  7.6 15.0 %collective-permute-start.4 = (bf16[1,256,256]{2,1,0:T(8,128)(2,1)}, bf16[1,256,256]{2,1,0:T(8,128)(2,1)S(1)}, u32[]{:S(2)}, u32[]{:S(2)}) collective-permute-start(bf16[1,256,256]{2,1,0:T(8,128)(2,1)} %refs_0_.1), channel_id=1, source_target_pairs={{0,48},{8,56},{16,32},{24,40},{32,80},{40,88},{48,64},{56,72},{64,... | collective-permute-start | bytes 393224 | tf_op jit(solution)/shard_map/ppermute | solution.py:286
  8.9 13.6 %collective-permute-start.5 = (bf16[1,256,256]{2,1,0:T(8,128)(2,1)}, bf16[1,256,256]{2,1,0:T(8,128)(2,1)S(1)}, u32[]{:S(2)}, u32[]{:S(2)}) collective-permute-start(bf16[1,256,256]{2,1,0:T(8,128)(2,1)} %refs_0_.1), channel_id=1, source_target_pairs={{0,80},{8,88},{16,64},{24,72},{32,112},{40,120},{48,96},{56,104},{... | collective-permute-start | bytes 393224 | tf_op jit(solution)/shard_map/ppermute | solution.py:286
  11.7 10.8 %collective-permute-start.6 = (bf16[1,256,256]{2,1,0:T(8,128)(2,1)}, bf16[1,256,256]{2,1,0:T(8,128)(2,1)S(1)}, u32[]{:S(2)}, u32[]{:S(2)}) collective-permute-start(bf16[1,256,256]{2,1,0:T(8,128)(2,1)} %refs_0_.1), channel_id=1, source_target_pairs={{0,112},{8,120},{16,96},{24,104},{32,16},{40,24},{48,0},{56,8},{64... | collective-permute-start | bytes 393224 | tf_op jit(solution)/shard_map/ppermute | solution.py:286
  18.5 5.6 %collective-permute-start.7 = (bf16[4,256,256]{2,1,0:T(8,128)(2,1)S(1)}, bf16[4,256,256]{2,1,0:T(8,128)(2,1)S(1)}, u32[]{:S(2)}, u32[]{:S(2)}) collective-permute-start(bf16[4,256,256]{2,1,0:T(8,128)(2,1)S(1)} %join.2), channel_id=1, source_target_pairs={{0,8},{8,0},{16,24},{24,16},{32,40},{40,32},{48,56},{56,48},{64,72... | collective-permute-start | bytes 1572872 | tf_op jit(solution)/shard_map/ppermute | solution.py:295
  22.6 3.1 %copy-start.3 = (s32[16,8]{0,1:T(8,128)S(1)}, s32[16,8]{0,1:T(8,128)}, u32[]{:S(2)}) copy-start(s32[16,8]{0,1:T(8,128)} %param.9) | copy-start | bytes 1540
  22.6 2.9 %collective-permute-start.8 = (bf16[4,256,256]{2,1,0:T(8,128)(2,1)S(1)}, bf16[4,256,256]{2,1,0:T(8,128)(2,1)S(1)}, u32[]{:S(2)}, u32[]{:S(2)}) collective-permute-start(bf16[4,256,256]{2,1,0:T(8,128)(2,1)S(1)} %join.3), channel_id=1, source_target_pairs={{0,8},{8,0},{16,24},{24,16},{32,40},{40,32},{48,56},{56,48},{64,72... | collective-permute-start | bytes 1572872 | tf_op jit(solution)/shard_map/ppermute | solution.py:295
  33.6 12.3 %collective-permute-start.9 = (bf16[4,208,256]{2,1,0:T(8,128)(2,1)S(1)}, bf16[4,208,256]{2,1,0:T(8,128)(2,1)S(1)}, u32[]{:S(2)}, u32[]{:S(2)}) collective-permute-start(bf16[4,208,256]{2,1,0:T(8,128)(2,1)S(1)} %get-tuple-element.23), channel_id=1, source_target_pairs={{0,1},{1,0},{2,3},{3,2},{4,5},{5,4},{6,7},{7,6},{8,9},{9,8},{10,11... | collective-permute-start | bytes 1277960 | tf_op jit(solution)/shard_map/ppermute | solution.py:26
  34.9 11.0 %collective-permute-start.10 = (bf16[4,176,256]{2,1,0:T(8,128)(2,1)S(1)}, bf16[4,176,256]{2,1,0:T(8,128)(2,1)S(1)}, u32[]{:S(2)}, u32[]{:S(2)}) collective-permute-start(bf16[4,176,256]{2,1,0:T(8,128)(2,1)S(1)} %get-tuple-element.25), channel_id=1, source_target_pairs={{0,3},{1,2},{2,1},{3,0},{4,7},{5,6},{6,5},{7,4},{8,11},{9,10},{10,... | collective-permute-start | bytes 1081352 | tf_op jit(solution)/shard_map/ppermute | solution.py:26
  36.7 9.2 %collective-permute-start.11 = (bf16[4,128,256]{2,1,0:T(8,128)(2,1)S(1)}, bf16[4,128,256]{2,1,0:T(8,128)(2,1)S(1)}, u32[]{:S(2)}, u32[]{:S(2)}) collective-permute-start(bf16[4,128,256]{2,1,0:T(8,128)(2,1)S(1)} %get-tuple-element.27), channel_id=1, source_target_pairs={{0,4},{1,5},{2,6},{3,7},{4,0},{5,1},{6,2},{7,3},{8,12},{9,13},{10,... | collective-permute-start | bytes 786440 | tf_op jit(solution)/shard_map/ppermute | solution.py:26
  45.8 22.7 %copy-start = (bf16[16,256,256]{2,1,0:T(8,128)(2,1)S(1)}, bf16[16,256,256]{2,1,0:T(8,128)(2,1)}, u32[]{:S(2)}) copy-start(bf16[16,256,256]{2,1,0:T(8,128)(2,1)} %proj_ref.2) | copy-start | bytes 6291460
  46.0 11.8 %collective-permute-start.12 = (bf16[4,208,256]{2,1,0:T(8,128)(2,1)S(1)}, bf16[4,208,256]{2,1,0:T(8,128)(2,1)S(1)}, u32[]{:S(2)}, u32[]{:S(2)}) collective-permute-start(bf16[4,208,256]{2,1,0:T(8,128)(2,1)S(1)} %get-tuple-element.28.refs_0_), channel_id=1, source_target_pairs={{0,3},{1,2},{2,1},{3,0},{4,7},{5,6},{6,5},{7,4},{8,11},{9,10},{10,... | collective-permute-start | bytes 1277960 | tf_op jit(solution)/shard_map/ppermute | solution.py:26
  47.4 10.4 %collective-permute-start.13 = (bf16[4,176,256]{2,1,0:T(8,128)(2,1)S(1)}, bf16[4,176,256]{2,1,0:T(8,128)(2,1)S(1)}, u32[]{:S(2)}, u32[]{:S(2)}) collective-permute-start(bf16[4,176,256]{2,1,0:T(8,128)(2,1)S(1)} %get-tuple-element.29.refs_2_), channel_id=1, source_target_pairs={{0,4},{1,5},{2,6},{3,7},{4,0},{5,1},{6,2},{7,3},{8,12},{9,13},{10,... | collective-permute-start | bytes 1081352 | tf_op jit(solution)/shard_map/ppermute | solution.py:26
  50.9 5.7 %collective-permute-start.14 = (bf16[4,128,256]{2,1,0:T(8,128)(2,1)S(1)}, bf16[4,128,256]{2,1,0:T(8,128)(2,1)S(1)}, u32[]{:S(2)}, u32[]{:S(2)}) collective-permute-start(bf16[4,128,256]{2,1,0:T(8,128)(2,1)S(1)} %get-tuple-element.30.refs_4_), channel_id=1, source_target_pairs={{0,1},{1,0},{2,3},{3,2},{4,5},{5,4},{6,7},{7,6},{8,9},{9,8},{10,11... | collective-permute-start | bytes 786440 | tf_op jit(solution)/shard_map/ppermute | solution.py:26
  58.0 10.4 %collective-permute-start.15 = (bf16[4,208,256]{2,1,0:T(8,128)(2,1)S(1)}, bf16[4,208,256]{2,1,0:T(8,128)(2,1)S(1)}, u32[]{:S(2)}, u32[]{:S(2)}) collective-permute-start(bf16[4,208,256]{2,1,0:T(8,128)(2,1)S(1)} %get-tuple-element.31.refs_0_), channel_id=1, source_target_pairs={{0,4},{1,5},{2,6},{3,7},{4,0},{5,1},{6,2},{7,3},{8,12},{9,13},{10,... | collective-permute-start | bytes 1277960 | tf_op jit(solution)/shard_map/ppermute | solution.py:26
  60.8 7.0 %collective-permute-start.16 = (bf16[4,176,256]{2,1,0:T(8,128)(2,1)S(1)}, bf16[4,176,256]{2,1,0:T(8,128)(2,1)S(1)}, u32[]{:S(2)}, u32[]{:S(2)}) collective-permute-start(bf16[4,176,256]{2,1,0:T(8,128)(2,1)S(1)} %get-tuple-element.32.refs_1_), channel_id=1, source_target_pairs={{0,1},{1,0},{2,3},{3,2},{4,5},{5,4},{6,7},{7,6},{8,9},{9,8},{10,11... | collective-permute-start | bytes 1081352 | tf_op jit(solution)/shard_map/ppermute | solution.py:26
  61.0 6.7 %collective-permute-start.17 = (bf16[4,128,256]{2,1,0:T(8,128)(2,1)S(1)}, bf16[4,128,256]{2,1,0:T(8,128)(2,1)S(1)}, u32[]{:S(2)}, u32[]{:S(2)}) collective-permute-start(bf16[4,128,256]{2,1,0:T(8,128)(2,1)S(1)} %get-tuple-element.33.refs_2_), channel_id=1, source_target_pairs={{0,3},{1,2},{2,1},{3,0},{4,7},{5,6},{6,5},{7,4},{8,11},{9,10},{10,... | collective-permute-start | bytes 786440 | tf_op jit(solution)/shard_map/ppermute | solution.py:26
  69.7 8.3 %collective-permute-start.18 = (bf16[4,208,256]{2,1,0:T(8,128)(2,1)S(1)}, bf16[4,208,256]{2,1,0:T(8,128)(2,1)S(1)}, u32[]{:S(2)}, u32[]{:S(2)}) collective-permute-start(bf16[4,208,256]{2,1,0:T(8,128)(2,1)S(1)} %get-tuple-element.35.refs_0_), channel_id=1, source_target_pairs={{0,1},{1,0},{2,3},{3,2},{4,5},{5,4},{6,7},{7,6},{8,9},{9,8},{10,11... | collective-permute-start | bytes 1277960 | tf_op jit(solution)/shard_map/ppermute | solution.py:26
  70.3 7.8 %collective-permute-start.19 = (bf16[4,176,256]{2,1,0:T(8,128)(2,1)S(1)}, bf16[4,176,256]{2,1,0:T(8,128)(2,1)S(1)}, u32[]{:S(2)}, u32[]{:S(2)}) collective-permute-start(bf16[4,176,256]{2,1,0:T(8,128)(2,1)S(1)} %get-tuple-element.36.refs_2_), channel_id=1, source_target_pairs={{0,3},{1,2},{2,1},{3,0},{4,7},{5,6},{6,5},{7,4},{8,11},{9,10},{10,... | collective-permute-start | bytes 1081352 | tf_op jit(solution)/shard_map/ppermute | solution.py:26
  71.1 7.0 %copy-start.4 = (s32[4,10]{1,0:T(4,128)S(1)}, s32[4,10]{1,0:T(4,128)}, u32[]{:S(2)}) copy-start(s32[4,10]{1,0:T(4,128)} %source_ref.1) | copy-start | bytes 484
  71.1 6.7 %collective-permute-start.20 = (bf16[4,128,256]{2,1,0:T(8,128)(2,1)S(1)}, bf16[4,128,256]{2,1,0:T(8,128)(2,1)S(1)}, u32[]{:S(2)}, u32[]{:S(2)}) collective-permute-start(bf16[4,128,256]{2,1,0:T(8,128)(2,1)S(1)} %get-tuple-element.37.refs_4_), channel_id=1, source_target_pairs={{0,4},{1,5},{2,6},{3,7},{4,0},{5,1},{6,2},{7,3},{8,12},{9,13},{10,... | collective-permute-start | bytes 786440 | tf_op jit(solution)/shard_map/ppermute | solution.py:26
  76.3 22.4 %copy-start.1 = (bf16[4,256,256]{2,1,0:T(8,128)(2,1)S(1)}, bf16[4,256,256]{2,1,0:T(8,128)(2,1)}, u32[]{:S(2)}) copy-start(bf16[4,256,256]{2,1,0:T(8,128)(2,1)} %proj_ref.3) | copy-start | bytes 1572868

commit v7 on v6

--- a/solution.py
+++ b/solution.py
@@ -12,7 +12,7 @@
 SIZE = 256
 COUNT = 2
 FLAT = COUNT * SIZE
-HOPS = ((2, 1), (1, 1), (3, 1), (0, 1), (2, 0), (1, 0), (3, 0))
+HOPS = ((2, 1), (1, 1), (3, 1), (0, 1), (1, 0), (3, 0), (2, 0))
 DEPTH = 4
 FLIPS = (1, 3, 4)
 ORDERS = ((0, 1, 2), (1, 2, 0), (2, 0, 1))

time: 99.7 us -> 98.6 us (0.989)
  waiting for transfers between devices: 23.3 us -> 22.2 us
    ppermute x2, starting transfers between devices: 5.38 us -> 4.24 us  [body(): lax.ppermute(owns[0], 'left', [(i, i ^ 1) for i in range(lefts)])]
    ppermute x7, waiting for transfers between devices: 1.07 us -> 0.02 us  [bring(): return lax.ppermute(corner, 'left', pairs)]
    ppermute x7, starting transfers between devices: 10.8 us -> 11.8 us  [bring(): return lax.ppermute(corner, 'left', pairs)]
  transfers between devices with their start and end apart: 21 -> 21, of which waited for: 10 -> 9; matrix products, arithmetic and copies ran while one was open for 0% -> 0% of each run, Pallas kernels for 9% -> 9%
where the time goes in v7:
time: 98.6 us; the launch traced here: 98.5 us
  starting transfers between devices  35.5 us (36%)
  waiting for transfers between devices  22.2 us (23%)
  Pallas kernels  22 us (22%)
  blocking collectives  17.7 us (18%)
    ppermute x12, waiting for transfers between devices, flip(): lax.ppermute(value, 'right', [(i, i ^ FLIPS[pairing]) for i in range(size)])  20.7 us
    ppermute x12, starting transfers between devices, flip(): lax.ppermute(value, 'right', [(i, i ^ FLIPS[pairing]) for i in range(size)])  19.5 us
    all_to_all x1, blocking collectives, body(): col_parts = lax.all_to_all(partial_cols, 'left', 0, 0, tiled=True)  17.7 us
    ppermute x7, starting transfers between devices, bring(): return lax.ppermute(corner, 'left', pairs)  11.8 us
    pallas_call x2, Pallas kernels, load(): pl.pallas_call(load_kernel, out_shape=pltpu.VMEM(edge.shape, edge.dtype),...  8.46 us
    pallas_call x1, Pallas kernels, row_partial(): pl.pallas_call(row_kernel, out_shape=tuple(outs), grid_spec=pltpu.Prefetc...  7.81 us
    ppermute x2, starting transfers between devices, body(): lax.ppermute(owns[0], 'left', [(i, i ^ 1) for i in range(lefts)])  4.24 us
    pallas_call x1, Pallas kernels, col_partial(): pl.pallas_call(col_kernel, out_shape=jax.ShapeDtypeStruct((pieces, sector...  3.14 us
  transfers between devices with their start and end apart: 21, of which 9 were waited for; matrix products, arithmetic and copies ran while one was open for 0% of the time, Pallas kernels for 9%

profile of v7, /device:TPU:1, one launch (start us, length us, event | category | flops | bytes accessed | tf_op | source)
XLA Modules:
  0.0 98.5 jit_solution(625830598845503723)
XLA Ops:
  0.6 3.8 %collective-permute-start.1 = (bf16[1,256,256]{2,1,0:T(8,128)(2,1)}, bf16[1,256,256]{2,1,0:T(8,128)(2,1)S(1)}, u32[]{:S(2)}, u32[]{:S(2)}) collective-permute-start(bf16[1,256,256]{2,1,0:T(8,128)(2,1)} %refs_0_.1), channel_id=1, source_target_pairs={{0,64},{8,72},{16,80},{24,88},{32,96},{40,104},{48,112},{56,120},{... | collective-permute-start | bytes 393224 | tf_op jit(solution)/shard_map/ppermute | solution.py:286
  4.5 0.4 collective-permute-start
  4.9 2.3 %collective-permute-start.2 = (bf16[1,256,256]{2,1,0:T(8,128)(2,1)}, bf16[1,256,256]{2,1,0:T(8,128)(2,1)S(1)}, u32[]{:S(2)}, u32[]{:S(2)}) collective-permute-start(bf16[1,256,256]{2,1,0:T(8,128)(2,1)} %refs_0_.1), channel_id=1, source_target_pairs={{0,96},{8,104},{16,112},{24,120},{32,0},{40,8},{48,16},{56,24},{64... | collective-permute-start | bytes 393224 | tf_op jit(solution)/shard_map/ppermute | solution.py:286
  7.1 1.6 %collective-permute-start.3 = (bf16[1,256,256]{2,1,0:T(8,128)(2,1)}, bf16[1,256,256]{2,1,0:T(8,128)(2,1)S(1)}, u32[]{:S(2)}, u32[]{:S(2)}) collective-permute-start(bf16[1,256,256]{2,1,0:T(8,128)(2,1)} %refs_0_.1), channel_id=1, source_target_pairs={{0,16},{8,24},{16,0},{24,8},{32,48},{40,56},{48,32},{56,40},{64,80... | collective-permute-start | bytes 393224 | tf_op jit(solution)/shard_map/ppermute | solution.py:286
  8.8 3.2 %collective-permute-start.5 = (bf16[1,256,256]{2,1,0:T(8,128)(2,1)}, bf16[1,256,256]{2,1,0:T(8,128)(2,1)S(1)}, u32[]{:S(2)}, u32[]{:S(2)}) collective-permute-start(bf16[1,256,256]{2,1,0:T(8,128)(2,1)} %refs_0_.1), channel_id=1, source_target_pairs={{0,80},{8,88},{16,64},{24,72},{32,112},{40,120},{48,96},{56,104},{... | collective-permute-start | bytes 393224 | tf_op jit(solution)/shard_map/ppermute | solution.py:286
  12.0 0.4 collective-permute-start.6
  12.4 5.9 %load.2.edge_ref = bf16[16,8,256,256]{3,2,1,0:T(8,128)(2,1)S(1)} custom-call(bf16[16,8,256,256]{3,2,1,0:T(8,128)(2,1)} %edge_ref.2), custom_call_target="tpu_custom_call" | custom-call | bytes 33554432 | tf_op jit(solution)/shard_map/load/pallas_call | solution.py:67
  18.4 2.9 %collective-permute-start.7 = (bf16[4,256,256]{2,1,0:T(8,128)(2,1)S(1)}, bf16[4,256,256]{2,1,0:T(8,128)(2,1)S(1)}, u32[]{:S(2)}, u32[]{:S(2)}) collective-permute-start(bf16[4,256,256]{2,1,0:T(8,128)(2,1)S(1)} %join.2), channel_id=1, source_target_pairs={{0,8},{8,0},{16,24},{24,16},{32,40},{40,32},{48,56},{56,48},{64,72... | collective-permute-start | bytes 1572872 | tf_op jit(solution)/shard_map/ppermute | solution.py:295
  21.4 1.4 %collective-permute-start.8 = (bf16[4,256,256]{2,1,0:T(8,128)(2,1)S(1)}, bf16[4,256,256]{2,1,0:T(8,128)(2,1)S(1)}, u32[]{:S(2)}, u32[]{:S(2)}) collective-permute-start(bf16[4,256,256]{2,1,0:T(8,128)(2,1)S(1)} %join.3), channel_id=1, source_target_pairs={{0,8},{8,0},{16,24},{24,16},{32,40},{40,32},{48,56},{56,48},{64,72... | collective-permute-start | bytes 1572872 | tf_op jit(solution)/shard_map/ppermute | solution.py:295
  22.8 1.5 %collective-permute-done.8 = bf16[4,256,256]{2,1,0:T(8,128)(2,1)S(1)} collective-permute-done((bf16[4,256,256]{2,1,0:T(8,128)(2,1)S(1)}, bf16[4,256,256]{2,1,0:T(8,128)(2,1)S(1)}, u32[]{:S(2)}, u32[]{:S(2)}) %collective-permute-start.8) | collective-permute-done | bytes 524320 | tf_op jit(solution)/shard_map/ppermute | solution.py:295
  24.6 7.8 %row_partial.1 = (bf16[4,208,256]{2,1,0:T(8,128)(2,1)S(1)}, f32[4,208,256]{2,1,0:T(8,128)S(1)}, bf16[4,176,256]{2,1,0:T(8,128)(2,1)S(1)}, f32[4,176,256]{2,1,0:T...) custom-call(s32[8,16]{1,0:T(8,128)S(1)} %bitcast.1, ...), custom_call_target="tpu_custom_call" | custom-call | flops 4294967296 | bytes 8388608 | tf_op jit(solution)/shard_map/row_partial/pallas_call | solution.py:132
  32.4 1.3 %collective-permute-start.9 = (bf16[4,208,256]{2,1,0:T(8,128)(2,1)S(1)}, bf16[4,208,256]{2,1,0:T(8,128)(2,1)S(1)}, u32[]{:S(2)}, u32[]{:S(2)}) collective-permute-start(bf16[4,208,256]{2,1,0:T(8,128)(2,1)S(1)} %get-tuple-element.23), channel_id=1, source_target_pairs={{0,1},{1,0},{2,3},{3,2},{4,5},{5,4},{6,7},{7,6},{8,9},{9,8},{10,11... | collective-permute-start | bytes 1277960 | tf_op jit(solution)/shard_map/ppermute | solution.py:26
  33.7 1.8 %collective-permute-start.10 = (bf16[4,176,256]{2,1,0:T(8,128)(2,1)S(1)}, bf16[4,176,256]{2,1,0:T(8,128)(2,1)S(1)}, u32[]{:S(2)}, u32[]{:S(2)}) collective-permute-start(bf16[4,176,256]{2,1,0:T(8,128)(2,1)S(1)} %get-tuple-element.25), channel_id=1, source_target_pairs={{0,3},{1,2},{2,1},{3,0},{4,7},{5,6},{6,5},{7,4},{8,11},{9,10},{10,... | collective-permute-start | bytes 1081352 | tf_op jit(solution)/shard_map/ppermute | solution.py:26
  35.5 3.3 %collective-permute-start.11 = (bf16[4,128,256]{2,1,0:T(8,128)(2,1)S(1)}, bf16[4,128,256]{2,1,0:T(8,128)(2,1)S(1)}, u32[]{:S(2)}, u32[]{:S(2)}) collective-permute-start(bf16[4,128,256]{2,1,0:T(8,128)(2,1)S(1)} %get-tuple-element.27), channel_id=1, source_target_pairs={{0,4},{1,5},{2,6},{3,7},{4,0},{5,1},{6,2},{7,3},{8,12},{9,13},{10,... | collective-permute-start | bytes 786440 | tf_op jit(solution)/shard_map/ppermute | solution.py:26
  38.8 5.7 %collective-permute-done.11.refs_5_ = bf16[4,128,256]{2,1,0:T(8,128)(2,1)S(1)} collective-permute-done((bf16[4,128,256]{2,1,0:T(8,128)(2,1)S(1)}, bf16[4,128,256]{2,1,0:T(8,128)(2,1)S(1)}, u32[]{:S(2)}, u32[]{:S(2)}) %collective-permute-start.11) | collective-permute-done | bytes 262176 | tf_op jit(solution)/shard_map/ppermute | solution.py:26
  44.7 1.5 %collective-permute-start.12 = (bf16[4,208,256]{2,1,0:T(8,128)(2,1)S(1)}, bf16[4,208,256]{2,1,0:T(8,128)(2,1)S(1)}, u32[]{:S(2)}, u32[]{:S(2)}) collective-permute-start(bf16[4,208,256]{2,1,0:T(8,128)(2,1)S(1)} %get-tuple-element.28.refs_0_), channel_id=1, source_target_pairs={{0,3},{1,2},{2,1},{3,0},{4,7},{5,6},{6,5},{7,4},{8,11},{9,10},{10,... | collective-permute-start | bytes 1277960 | tf_op jit(solution)/shard_map/ppermute | solution.py:26
  46.3 3.3 %collective-permute-start.13 = (bf16[4,176,256]{2,1,0:T(8,128)(2,1)S(1)}, bf16[4,176,256]{2,1,0:T(8,128)(2,1)S(1)}, u32[]{:S(2)}, u32[]{:S(2)}) collective-permute-start(bf16[4,176,256]{2,1,0:T(8,128)(2,1)S(1)} %get-tuple-element.29.refs_2_), channel_id=1, source_target_pairs={{0,4},{1,5},{2,6},{3,7},{4,0},{5,1},{6,2},{7,3},{8,12},{9,13},{10,... | collective-permute-start | bytes 1081352 | tf_op jit(solution)/shard_map/ppermute | solution.py:26
  49.6 5.7 %collective-permute-done.14.refs_5_ = bf16[4,128,256]{2,1,0:T(8,128)(2,1)S(1)} collective-permute-done((bf16[4,128,256]{2,1,0:T(8,128)(2,1)S(1)}, bf16[4,128,256]{2,1,0:T(8,128)(2,1)S(1)}, u32[]{:S(2)}, u32[]{:S(2)}) %collective-permute-start.14) | collective-permute-done | bytes 262176 | tf_op jit(solution)/shard_map/ppermute | solution.py:26
  55.3 1.2 %collective-permute-done.13.refs_3_ = bf16[4,176,256]{2,1,0:T(8,128)(2,1)S(1)} collective-permute-done((bf16[4,176,256]{2,1,0:T(8,128)(2,1)S(1)}, bf16[4,176,256]{2,1,0:T(8,128)(2,1)S(1)}, u32[]{:S(2)}, u32[]{:S(2)}) %collective-permute-start.13) | collective-permute-done | bytes 360480 | tf_op jit(solution)/shard_map/ppermute | solution.py:26
  56.8 2.8 %collective-permute-start.15 = (bf16[4,208,256]{2,1,0:T(8,128)(2,1)S(1)}, bf16[4,208,256]{2,1,0:T(8,128)(2,1)S(1)}, u32[]{:S(2)}, u32[]{:S(2)}) collective-permute-start(bf16[4,208,256]{2,1,0:T(8,128)(2,1)S(1)} %get-tuple-element.31.refs_0_), channel_id=1, source_target_pairs={{0,4},{1,5},{2,6},{3,7},{4,0},{5,1},{6,2},{7,3},{8,12},{9,13},{10,... | collective-permute-start | bytes 1277960 | tf_op jit(solution)/shard_map/ppermute | solution.py:26
  59.7 1.2 %collective-permute-start.17 = (bf16[4,128,256]{2,1,0:T(8,128)(2,1)S(1)}, bf16[4,128,256]{2,1,0:T(8,128)(2,1)S(1)}, u32[]{:S(2)}, u32[]{:S(2)}) collective-permute-start(bf16[4,128,256]{2,1,0:T(8,128)(2,1)S(1)} %get-tuple-element.33.refs_2_), channel_id=1, source_target_pairs={{0,3},{1,2},{2,1},{3,0},{4,7},{5,6},{6,5},{7,4},{8,11},{9,10},{10,... | collective-permute-start | bytes 786440 | tf_op jit(solution)/shard_map/ppermute | solution.py:26
  60.9 5.6 %collective-permute-done.17.refs_5_ = bf16[4,128,256]{2,1,0:T(8,128)(2,1)S(1)} collective-permute-done((bf16[4,128,256]{2,1,0:T(8,128)(2,1)S(1)}, bf16[4,128,256]{2,1,0:T(8,128)(2,1)S(1)}, u32[]{:S(2)}, u32[]{:S(2)}) %collective-permute-start.17) | collective-permute-done | bytes 262176 | tf_op jit(solution)/shard_map/ppermute | solution.py:26
  66.5 0.7 collective-permute-done.15.refs_3_
  67.2 1.2 %absorb.1 = (bf16[2,256,256]{2,1,0:T(8,128)(2,1)}, bf16[4,208,256]{2,1,0:T(8,128)(2,1)S(1)}, bf16[4,176,256]{2,1,0:T(8,128)(2,1)S(1)}, bf16[4,128,256]{2,1,0:T(8,128)(2,1)S(1)}) custom-call(bf16[16,256,256]{2,1,0:T(8,128)(2,1)S(1)} %copy-done, bf16[4,208,256]{2,1,0:T(8,128)(2,1)S(1)} %get-tuple-element.31.refs_0_, ...), custom_call_target="tpu_custom_call" | custom-call | flops 268435456 | bytes 5242880 | tf_op jit(solution)/shard_map/absorb/pallas_call | solution.py:196
  68.4 0.5 collective-permute-start.18
  69.0 0.8 collective-permute-start.19
  69.8 2.7 %collective-permute-start.20 = (bf16[4,128,256]{2,1,0:T(8,128)(2,1)S(1)}, bf16[4,128,256]{2,1,0:T(8,128)(2,1)S(1)}, u32[]{:S(2)}, u32[]{:S(2)}) collective-permute-start(bf16[4,128,256]{2,1,0:T(8,128)(2,1)S(1)} %get-tuple-element.37.refs_4_), channel_id=1, source_target_pairs={{0,4},{1,5},{2,6},{3,7},{4,0},{5,1},{6,2},{7,3},{8,12},{9,13},{10,... | collective-permute-start | bytes 786440 | tf_op jit(solution)/shard_map/ppermute | solution.py:26
  72.5 2.5 %load.3.refs_6_ = bf16[4,10,256,256]{3,2,1,0:T(8,128)(2,1)S(1)} custom-call(bf16[4,10,256,256]{3,2,1,0:T(8,128)(2,1)} %edge_ref.3), custom_call_target="tpu_custom_call" | custom-call | bytes 10485760 | tf_op jit(solution)/shard_map/load/pallas_call | solution.py:67
  75.1 1.4 %collective-permute-done.20.refs_5_ = bf16[4,128,256]{2,1,0:T(8,128)(2,1)S(1)} collective-permute-done((bf16[4,128,256]{2,1,0:T(8,128)(2,1)S(1)}, bf16[4,128,256]{2,1,0:T(8,128)(2,1)S(1)}, u32[]{:S(2)}, u32[]{:S(2)}) %collective-permute-start.20) | collective-permute-done | bytes 262176 | tf_op jit(solution)/shard_map/ppermute | solution.py:26
  76.8 3.1 %col_partial.1 = bf16[16,4,16,256]{3,2,1,0:T(8,128)(2,1)S(1)} custom-call(s32[4,10]{1,0:T(4,128)S(1)} %copy-done.4, bf16[4,208,256]{2,1,0:T(8,128)(2,1)S(1)} %get-tuple-element.35.refs_0_, bf16[4,208,256]{2,1,0:T(8,128)(2,1)S(1)} %collective-permute-done.18.refs_1_, bf16[4,176,256]{2,1,0:T(8,128)(2,1)S(1)} %get-tuple-element.36.refs_2_, ...), custom_call_target="tpu_custom_call" | custom-call | flops 1342177280 | bytes 5242880 | tf_op jit(solution)/shard_map/col_partial/pallas_call | solution.py:244
  79.9 17.7 %all_to_all.5.part_ref = bf16[16,4,16,256]{3,2,1,0:T(8,128)(2,1)S(1)} all-to-all(bf16[16,4,16,256]{3,2,1,0:T(8,128)(2,1)S(1)} %col_partial.1), channel_id=1, replica_groups=mesh['left'=16,'right'=8] {'left'}, dimensions={0} | all-to-all | bytes 1048576 | tf_op jit(solution)/shard_map/all_to_all | solution.py:310
  97.6 0.9 finish.1
  (32 shorter events, 1.4 us)
Async XLA Ops:
  0.6 17.8 %copy-start.2 = (bf16[1,256,256]{2,1,0:T(8,128)(2,1)S(1)}, bf16[1,256,256]{2,1,0:T(8,128)(2,1)}, u32[]{:S(2)}) copy-start(bf16[1,256,256]{2,1,0:T(8,128)(2,1)} %refs_0_.1) | copy-start | bytes 393220
  0.6 8.1 %collective-permute-start.1 = (bf16[1,256,256]{2,1,0:T(8,128)(2,1)}, bf16[1,256,256]{2,1,0:T(8,128)(2,1)S(1)}, u32[]{:S(2)}, u32[]{:S(2)}) collective-permute-start(bf16[1,256,256]{2,1,0:T(8,128)(2,1)} %refs_0_.1), channel_id=1, source_target_pairs={{0,64},{8,72},{16,80},{24,88},{32,96},{40,104},{48,112},{56,120},{... | collective-permute-start | bytes 393224 | tf_op jit(solution)/shard_map/ppermute | solution.py:286
  4.5 7.5 %collective-permute-start = (bf16[1,256,256]{2,1,0:T(8,128)(2,1)}, bf16[1,256,256]{2,1,0:T(8,128)(2,1)S(1)}, u32[]{:S(2)}, u32[]{:S(2)}) collective-permute-start(bf16[1,256,256]{2,1,0:T(8,128)(2,1)} %refs_0_.1), channel_id=1, source_target_pairs={{0,32},{8,40},{16,48},{24,56},{32,64},{40,72},{48,80},{56,88},{64,... | collective-permute-start | bytes 393224 | tf_op jit(solution)/shard_map/ppermute | solution.py:286
  4.9 13.5 %collective-permute-start.2 = (bf16[1,256,256]{2,1,0:T(8,128)(2,1)}, bf16[1,256,256]{2,1,0:T(8,128)(2,1)S(1)}, u32[]{:S(2)}, u32[]{:S(2)}) collective-permute-start(bf16[1,256,256]{2,1,0:T(8,128)(2,1)} %refs_0_.1), channel_id=1, source_target_pairs={{0,96},{8,104},{16,112},{24,120},{32,0},{40,8},{48,16},{56,24},{64... | collective-permute-start | bytes 393224 | tf_op jit(solution)/shard_map/ppermute | solution.py:286
  7.1 14.2 %collective-permute-start.3 = (bf16[1,256,256]{2,1,0:T(8,128)(2,1)}, bf16[1,256,256]{2,1,0:T(8,128)(2,1)S(1)}, u32[]{:S(2)}, u32[]{:S(2)}) collective-permute-start(bf16[1,256,256]{2,1,0:T(8,128)(2,1)} %refs_0_.1), channel_id=1, source_target_pairs={{0,16},{8,24},{16,0},{24,8},{32,48},{40,56},{48,32},{56,40},{64,80... | collective-permute-start | bytes 393224 | tf_op jit(solution)/shard_map/ppermute | solution.py:286
  8.8 12.5 %collective-permute-start.4 = (bf16[1,256,256]{2,1,0:T(8,128)(2,1)}, bf16[1,256,256]{2,1,0:T(8,128)(2,1)S(1)}, u32[]{:S(2)}, u32[]{:S(2)}) collective-permute-start(bf16[1,256,256]{2,1,0:T(8,128)(2,1)} %refs_0_.1), channel_id=1, source_target_pairs={{0,48},{8,56},{16,32},{24,40},{32,80},{40,88},{48,64},{56,72},{64,... | collective-permute-start | bytes 393224 | tf_op jit(solution)/shard_map/ppermute | solution.py:286
  8.8 12.5 %collective-permute-start.5 = (bf16[1,256,256]{2,1,0:T(8,128)(2,1)}, bf16[1,256,256]{2,1,0:T(8,128)(2,1)S(1)}, u32[]{:S(2)}, u32[]{:S(2)}) collective-permute-start(bf16[1,256,256]{2,1,0:T(8,128)(2,1)} %refs_0_.1), channel_id=1, source_target_pairs={{0,80},{8,88},{16,64},{24,72},{32,112},{40,120},{48,96},{56,104},{... | collective-permute-start | bytes 393224 | tf_op jit(solution)/shard_map/ppermute | solution.py:286
  12.0 9.3 %collective-permute-start.6 = (bf16[1,256,256]{2,1,0:T(8,128)(2,1)}, bf16[1,256,256]{2,1,0:T(8,128)(2,1)S(1)}, u32[]{:S(2)}, u32[]{:S(2)}) collective-permute-start(bf16[1,256,256]{2,1,0:T(8,128)(2,1)} %refs_0_.1), channel_id=1, source_target_pairs={{0,112},{8,120},{16,96},{24,104},{32,16},{40,24},{48,0},{56,8},{64... | collective-permute-start | bytes 393224 | tf_op jit(solution)/shard_map/ppermute | solution.py:286
  18.4 4.4 %collective-permute-start.7 = (bf16[4,256,256]{2,1,0:T(8,128)(2,1)S(1)}, bf16[4,256,256]{2,1,0:T(8,128)(2,1)S(1)}, u32[]{:S(2)}, u32[]{:S(2)}) collective-permute-start(bf16[4,256,256]{2,1,0:T(8,128)(2,1)S(1)} %join.2), channel_id=1, source_target_pairs={{0,8},{8,0},{16,24},{24,16},{32,40},{40,32},{48,56},{56,48},{64,72... | collective-permute-start | bytes 1572872 | tf_op jit(solution)/shard_map/ppermute | solution.py:295
  21.4 3.2 %copy-start.3 = (s32[16,8]{0,1:T(8,128)S(1)}, s32[16,8]{0,1:T(8,128)}, u32[]{:S(2)}) copy-start(s32[16,8]{0,1:T(8,128)} %param.9) | copy-start | bytes 1540
  21.4 2.9 %collective-permute-start.8 = (bf16[4,256,256]{2,1,0:T(8,128)(2,1)S(1)}, bf16[4,256,256]{2,1,0:T(8,128)(2,1)S(1)}, u32[]{:S(2)}, u32[]{:S(2)}) collective-permute-start(bf16[4,256,256]{2,1,0:T(8,128)(2,1)S(1)} %join.3), channel_id=1, source_target_pairs={{0,8},{8,0},{16,24},{24,16},{32,40},{40,32},{48,56},{56,48},{64,72... | collective-permute-start | bytes 1572872 | tf_op jit(solution)/shard_map/ppermute | solution.py:295
  32.4 12.2 %collective-permute-start.9 = (bf16[4,208,256]{2,1,0:T(8,128)(2,1)S(1)}, bf16[4,208,256]{2,1,0:T(8,128)(2,1)S(1)}, u32[]{:S(2)}, u32[]{:S(2)}) collective-permute-start(bf16[4,208,256]{2,1,0:T(8,128)(2,1)S(1)} %get-tuple-element.23), channel_id=1, source_target_pairs={{0,1},{1,0},{2,3},{3,2},{4,5},{5,4},{6,7},{7,6},{8,9},{9,8},{10,11... | collective-permute-start | bytes 1277960 | tf_op jit(solution)/shard_map/ppermute | solution.py:26
  33.7 10.9 %collective-permute-start.10 = (bf16[4,176,256]{2,1,0:T(8,128)(2,1)S(1)}, bf16[4,176,256]{2,1,0:T(8,128)(2,1)S(1)}, u32[]{:S(2)}, u32[]{:S(2)}) collective-permute-start(bf16[4,176,256]{2,1,0:T(8,128)(2,1)S(1)} %get-tuple-element.25), channel_id=1, source_target_pairs={{0,3},{1,2},{2,1},{3,0},{4,7},{5,6},{6,5},{7,4},{8,11},{9,10},{10,... | collective-permute-start | bytes 1081352 | tf_op jit(solution)/shard_map/ppermute | solution.py:26
  35.5 9.0 %collective-permute-start.11 = (bf16[4,128,256]{2,1,0:T(8,128)(2,1)S(1)}, bf16[4,128,256]{2,1,0:T(8,128)(2,1)S(1)}, u32[]{:S(2)}, u32[]{:S(2)}) collective-permute-start(bf16[4,128,256]{2,1,0:T(8,128)(2,1)S(1)} %get-tuple-element.27), channel_id=1, source_target_pairs={{0,4},{1,5},{2,6},{3,7},{4,0},{5,1},{6,2},{7,3},{8,12},{9,13},{10,... | collective-permute-start | bytes 786440 | tf_op jit(solution)/shard_map/ppermute | solution.py:26
  44.5 22.7 %copy-start = (bf16[16,256,256]{2,1,0:T(8,128)(2,1)S(1)}, bf16[16,256,256]{2,1,0:T(8,128)(2,1)}, u32[]{:S(2)}) copy-start(bf16[16,256,256]{2,1,0:T(8,128)(2,1)} %proj_ref.2) | copy-start | bytes 6291460
  44.7 11.8 %collective-permute-start.12 = (bf16[4,208,256]{2,1,0:T(8,128)(2,1)S(1)}, bf16[4,208,256]{2,1,0:T(8,128)(2,1)S(1)}, u32[]{:S(2)}, u32[]{:S(2)}) collective-permute-start(bf16[4,208,256]{2,1,0:T(8,128)(2,1)S(1)} %get-tuple-element.28.refs_0_), channel_id=1, source_target_pairs={{0,3},{1,2},{2,1},{3,0},{4,7},{5,6},{6,5},{7,4},{8,11},{9,10},{10,... | collective-permute-start | bytes 1277960 | tf_op jit(solution)/shard_map/ppermute | solution.py:26
  46.3 10.2 %collective-permute-start.13 = (bf16[4,176,256]{2,1,0:T(8,128)(2,1)S(1)}, bf16[4,176,256]{2,1,0:T(8,128)(2,1)S(1)}, u32[]{:S(2)}, u32[]{:S(2)}) collective-permute-start(bf16[4,176,256]{2,1,0:T(8,128)(2,1)S(1)} %get-tuple-element.29.refs_2_), channel_id=1, source_target_pairs={{0,4},{1,5},{2,6},{3,7},{4,0},{5,1},{6,2},{7,3},{8,12},{9,13},{10,... | collective-permute-start | bytes 1081352 | tf_op jit(solution)/shard_map/ppermute | solution.py:26
  49.6 5.7 %collective-permute-start.14 = (bf16[4,128,256]{2,1,0:T(8,128)(2,1)S(1)}, bf16[4,128,256]{2,1,0:T(8,128)(2,1)S(1)}, u32[]{:S(2)}, u32[]{:S(2)}) collective-permute-start(bf16[4,128,256]{2,1,0:T(8,128)(2,1)S(1)} %get-tuple-element.30.refs_4_), channel_id=1, source_target_pairs={{0,1},{1,0},{2,3},{3,2},{4,5},{5,4},{6,7},{7,6},{8,9},{9,8},{10,11... | collective-permute-start | bytes 786440 | tf_op jit(solution)/shard_map/ppermute | solution.py:26
  56.8 10.5 %collective-permute-start.15 = (bf16[4,208,256]{2,1,0:T(8,128)(2,1)S(1)}, bf16[4,208,256]{2,1,0:T(8,128)(2,1)S(1)}, u32[]{:S(2)}, u32[]{:S(2)}) collective-permute-start(bf16[4,208,256]{2,1,0:T(8,128)(2,1)S(1)} %get-tuple-element.31.refs_0_), channel_id=1, source_target_pairs={{0,4},{1,5},{2,6},{3,7},{4,0},{5,1},{6,2},{7,3},{8,12},{9,13},{10,... | collective-permute-start | bytes 1277960 | tf_op jit(solution)/shard_map/ppermute | solution.py:26
  59.5 7.0 %collective-permute-start.16 = (bf16[4,176,256]{2,1,0:T(8,128)(2,1)S(1)}, bf16[4,176,256]{2,1,0:T(8,128)(2,1)S(1)}, u32[]{:S(2)}, u32[]{:S(2)}) collective-permute-start(bf16[4,176,256]{2,1,0:T(8,128)(2,1)S(1)} %get-tuple-element.32.refs_1_), channel_id=1, source_target_pairs={{0,1},{1,0},{2,3},{3,2},{4,5},{5,4},{6,7},{7,6},{8,9},{9,8},{10,11... | collective-permute-start | bytes 1081352 | tf_op jit(solution)/shard_map/ppermute | solution.py:26
  59.7 6.7 %collective-permute-start.17 = (bf16[4,128,256]{2,1,0:T(8,128)(2,1)S(1)}, bf16[4,128,256]{2,1,0:T(8,128)(2,1)S(1)}, u32[]{:S(2)}, u32[]{:S(2)}) collective-permute-start(bf16[4,128,256]{2,1,0:T(8,128)(2,1)S(1)} %get-tuple-element.33.refs_2_), channel_id=1, source_target_pairs={{0,3},{1,2},{2,1},{3,0},{4,7},{5,6},{6,5},{7,4},{8,11},{9,10},{10,... | collective-permute-start | bytes 786440 | tf_op jit(solution)/shard_map/ppermute | solution.py:26
  68.4 8.3 %collective-permute-start.18 = (bf16[4,208,256]{2,1,0:T(8,128)(2,1)S(1)}, bf16[4,208,256]{2,1,0:T(8,128)(2,1)S(1)}, u32[]{:S(2)}, u32[]{:S(2)}) collective-permute-start(bf16[4,208,256]{2,1,0:T(8,128)(2,1)S(1)} %get-tuple-element.35.refs_0_), channel_id=1, source_target_pairs={{0,1},{1,0},{2,3},{3,2},{4,5},{5,4},{6,7},{7,6},{8,9},{9,8},{10,11... | collective-permute-start | bytes 1277960 | tf_op jit(solution)/shard_map/ppermute | solution.py:26
  69.0 7.8 %collective-permute-start.19 = (bf16[4,176,256]{2,1,0:T(8,128)(2,1)S(1)}, bf16[4,176,256]{2,1,0:T(8,128)(2,1)S(1)}, u32[]{:S(2)}, u32[]{:S(2)}) collective-permute-start(bf16[4,176,256]{2,1,0:T(8,128)(2,1)S(1)} %get-tuple-element.36.refs_2_), channel_id=1, source_target_pairs={{0,3},{1,2},{2,1},{3,0},{4,7},{5,6},{6,5},{7,4},{8,11},{9,10},{10,... | collective-permute-start | bytes 1081352 | tf_op jit(solution)/shard_map/ppermute | solution.py:26
  69.8 7.0 %copy-start.4 = (s32[4,10]{1,0:T(4,128)S(1)}, s32[4,10]{1,0:T(4,128)}, u32[]{:S(2)}) copy-start(s32[4,10]{1,0:T(4,128)} %source_ref.1) | copy-start | bytes 484
  69.8 6.7 %collective-permute-start.20 = (bf16[4,128,256]{2,1,0:T(8,128)(2,1)S(1)}, bf16[4,128,256]{2,1,0:T(8,128)(2,1)S(1)}, u32[]{:S(2)}, u32[]{:S(2)}) collective-permute-start(bf16[4,128,256]{2,1,0:T(8,128)(2,1)S(1)} %get-tuple-element.37.refs_4_), channel_id=1, source_target_pairs={{0,4},{1,5},{2,6},{3,7},{4,0},{5,1},{6,2},{7,3},{8,12},{9,13},{10,... | collective-permute-start | bytes 786440 | tf_op jit(solution)/shard_map/ppermute | solution.py:26
  75.1 22.6 %copy-start.1 = (bf16[4,256,256]{2,1,0:T(8,128)(2,1)S(1)}, bf16[4,256,256]{2,1,0:T(8,128)(2,1)}, u32[]{:S(2)}) copy-start(bf16[4,256,256]{2,1,0:T(8,128)(2,1)} %proj_ref.3) | copy-start | bytes 1572868

commit v8 on v7

--- a/solution.py
+++ b/solution.py
@@ -12,7 +12,7 @@
 SIZE = 256
 COUNT = 2
 FLAT = COUNT * SIZE
-HOPS = ((2, 1), (1, 1), (3, 1), (0, 1), (1, 0), (3, 0), (2, 0))
+HOPS = ((2, 1), (3, 1), (1, 1), (0, 1), (3, 0), (1, 0), (2, 0))
 DEPTH = 4
 FLIPS = (1, 3, 4)
 ORDERS = ((0, 1, 2), (1, 2, 0), (2, 0, 1))

time: 98.6 us -> 98.6 us (level)
  no operation moved by 1% of the time
where the time goes in v8:
time: 98.6 us; the launch traced here: 98.5 us
  starting transfers between devices  35.5 us (36%)
  waiting for transfers between devices  22.2 us (23%)
  Pallas kernels  22 us (22%)
  blocking collectives  17.7 us (18%)
    ppermute x12, waiting for transfers between devices, flip(): lax.ppermute(value, 'right', [(i, i ^ FLIPS[pairing]) for i in range(size)])  20.7 us
    ppermute x12, starting transfers between devices, flip(): lax.ppermute(value, 'right', [(i, i ^ FLIPS[pairing]) for i in range(size)])  19.5 us
    all_to_all x1, blocking collectives, body(): col_parts = lax.all_to_all(partial_cols, 'left', 0, 0, tiled=True)  17.7 us
    ppermute x7, starting transfers between devices, bring(): return lax.ppermute(corner, 'left', pairs)  11.8 us
    pallas_call x2, Pallas kernels, load(): pl.pallas_call(load_kernel, out_shape=pltpu.VMEM(edge.shape, edge.dtype),...  8.46 us
    pallas_call x1, Pallas kernels, row_partial(): pl.pallas_call(row_kernel, out_shape=tuple(outs), grid_spec=pltpu.Prefetc...  7.81 us
    ppermute x2, starting transfers between devices, body(): lax.ppermute(owns[0], 'left', [(i, i ^ 1) for i in range(lefts)])  4.24 us
    pallas_call x1, Pallas kernels, col_partial(): pl.pallas_call(col_kernel, out_shape=jax.ShapeDtypeStruct((pieces, sector...  3.14 us
  transfers between devices with their start and end apart: 21, of which 9 were waited for; matrix products, arithmetic and copies ran while one was open for 0% of the time, Pallas kernels for 9%

profile of v8, /device:TPU:1, one launch (start us, length us, event | category | flops | bytes accessed | tf_op | source)
XLA Modules:
  0.0 98.5 jit_solution(625830598845503723)
XLA Ops:
  0.6 3.8 %collective-permute-start.1 = (bf16[1,256,256]{2,1,0:T(8,128)(2,1)}, bf16[1,256,256]{2,1,0:T(8,128)(2,1)S(1)}, u32[]{:S(2)}, u32[]{:S(2)}) collective-permute-start(bf16[1,256,256]{2,1,0:T(8,128)(2,1)} %refs_0_.1), channel_id=1, source_target_pairs={{0,64},{8,72},{16,80},{24,88},{32,96},{40,104},{48,112},{56,120},{... | collective-permute-start | bytes 393224 | tf_op jit(solution)/shard_map/ppermute | solution.py:286
  4.5 0.4 collective-permute-start
  4.9 2.3 %collective-permute-start.2 = (bf16[1,256,256]{2,1,0:T(8,128)(2,1)}, bf16[1,256,256]{2,1,0:T(8,128)(2,1)S(1)}, u32[]{:S(2)}, u32[]{:S(2)}) collective-permute-start(bf16[1,256,256]{2,1,0:T(8,128)(2,1)} %refs_0_.1), channel_id=1, source_target_pairs={{0,96},{8,104},{16,112},{24,120},{32,0},{40,8},{48,16},{56,24},{64... | collective-permute-start | bytes 393224 | tf_op jit(solution)/shard_map/ppermute | solution.py:286
  7.1 1.6 %collective-permute-start.3 = (bf16[1,256,256]{2,1,0:T(8,128)(2,1)}, bf16[1,256,256]{2,1,0:T(8,128)(2,1)S(1)}, u32[]{:S(2)}, u32[]{:S(2)}) collective-permute-start(bf16[1,256,256]{2,1,0:T(8,128)(2,1)} %refs_0_.1), channel_id=1, source_target_pairs={{0,16},{8,24},{16,0},{24,8},{32,48},{40,56},{48,32},{56,40},{64,80... | collective-permute-start | bytes 393224 | tf_op jit(solution)/shard_map/ppermute | solution.py:286
  8.8 3.2 %collective-permute-start.5 = (bf16[1,256,256]{2,1,0:T(8,128)(2,1)}, bf16[1,256,256]{2,1,0:T(8,128)(2,1)S(1)}, u32[]{:S(2)}, u32[]{:S(2)}) collective-permute-start(bf16[1,256,256]{2,1,0:T(8,128)(2,1)} %refs_0_.1), channel_id=1, source_target_pairs={{0,80},{8,88},{16,64},{24,72},{32,112},{40,120},{48,96},{56,104},{... | collective-permute-start | bytes 393224 | tf_op jit(solution)/shard_map/ppermute | solution.py:286
  12.0 0.4 collective-permute-start.6
  12.4 5.9 %load.2.edge_ref = bf16[16,8,256,256]{3,2,1,0:T(8,128)(2,1)S(1)} custom-call(bf16[16,8,256,256]{3,2,1,0:T(8,128)(2,1)} %edge_ref.2), custom_call_target="tpu_custom_call" | custom-call | bytes 33554432 | tf_op jit(solution)/shard_map/load/pallas_call | solution.py:67
  18.4 2.9 %collective-permute-start.7 = (bf16[4,256,256]{2,1,0:T(8,128)(2,1)S(1)}, bf16[4,256,256]{2,1,0:T(8,128)(2,1)S(1)}, u32[]{:S(2)}, u32[]{:S(2)}) collective-permute-start(bf16[4,256,256]{2,1,0:T(8,128)(2,1)S(1)} %join.2), channel_id=1, source_target_pairs={{0,8},{8,0},{16,24},{24,16},{32,40},{40,32},{48,56},{56,48},{64,72... | collective-permute-start | bytes 1572872 | tf_op jit(solution)/shard_map/ppermute | solution.py:295
  21.4 1.4 %collective-permute-start.8 = (bf16[4,256,256]{2,1,0:T(8,128)(2,1)S(1)}, bf16[4,256,256]{2,1,0:T(8,128)(2,1)S(1)}, u32[]{:S(2)}, u32[]{:S(2)}) collective-permute-start(bf16[4,256,256]{2,1,0:T(8,128)(2,1)S(1)} %join.3), channel_id=1, source_target_pairs={{0,8},{8,0},{16,24},{24,16},{32,40},{40,32},{48,56},{56,48},{64,72... | collective-permute-start | bytes 1572872 | tf_op jit(solution)/shard_map/ppermute | solution.py:295
  22.8 1.5 %collective-permute-done.8 = bf16[4,256,256]{2,1,0:T(8,128)(2,1)S(1)} collective-permute-done((bf16[4,256,256]{2,1,0:T(8,128)(2,1)S(1)}, bf16[4,256,256]{2,1,0:T(8,128)(2,1)S(1)}, u32[]{:S(2)}, u32[]{:S(2)}) %collective-permute-start.8) | collective-permute-done | bytes 524320 | tf_op jit(solution)/shard_map/ppermute | solution.py:295
  24.6 7.8 %row_partial.1 = (bf16[4,208,256]{2,1,0:T(8,128)(2,1)S(1)}, f32[4,208,256]{2,1,0:T(8,128)S(1)}, bf16[4,176,256]{2,1,0:T(8,128)(2,1)S(1)}, f32[4,176,256]{2,1,0:T...) custom-call(s32[8,16]{1,0:T(8,128)S(1)} %bitcast.1, ...), custom_call_target="tpu_custom_call" | custom-call | flops 4294967296 | bytes 8388608 | tf_op jit(solution)/shard_map/row_partial/pallas_call | solution.py:132
  32.4 1.3 %collective-permute-start.9 = (bf16[4,208,256]{2,1,0:T(8,128)(2,1)S(1)}, bf16[4,208,256]{2,1,0:T(8,128)(2,1)S(1)}, u32[]{:S(2)}, u32[]{:S(2)}) collective-permute-start(bf16[4,208,256]{2,1,0:T(8,128)(2,1)S(1)} %get-tuple-element.23), channel_id=1, source_target_pairs={{0,1},{1,0},{2,3},{3,2},{4,5},{5,4},{6,7},{7,6},{8,9},{9,8},{10,11... | collective-permute-start | bytes 1277960 | tf_op jit(solution)/shard_map/ppermute | solution.py:26
  33.7 1.8 %collective-permute-start.10 = (bf16[4,176,256]{2,1,0:T(8,128)(2,1)S(1)}, bf16[4,176,256]{2,1,0:T(8,128)(2,1)S(1)}, u32[]{:S(2)}, u32[]{:S(2)}) collective-permute-start(bf16[4,176,256]{2,1,0:T(8,128)(2,1)S(1)} %get-tuple-element.25), channel_id=1, source_target_pairs={{0,3},{1,2},{2,1},{3,0},{4,7},{5,6},{6,5},{7,4},{8,11},{9,10},{10,... | collective-permute-start | bytes 1081352 | tf_op jit(solution)/shard_map/ppermute | solution.py:26
  35.5 3.3 %collective-permute-start.11 = (bf16[4,128,256]{2,1,0:T(8,128)(2,1)S(1)}, bf16[4,128,256]{2,1,0:T(8,128)(2,1)S(1)}, u32[]{:S(2)}, u32[]{:S(2)}) collective-permute-start(bf16[4,128,256]{2,1,0:T(8,128)(2,1)S(1)} %get-tuple-element.27), channel_id=1, source_target_pairs={{0,4},{1,5},{2,6},{3,7},{4,0},{5,1},{6,2},{7,3},{8,12},{9,13},{10,... | collective-permute-start | bytes 786440 | tf_op jit(solution)/shard_map/ppermute | solution.py:26
  38.8 5.7 %collective-permute-done.11.refs_5_ = bf16[4,128,256]{2,1,0:T(8,128)(2,1)S(1)} collective-permute-done((bf16[4,128,256]{2,1,0:T(8,128)(2,1)S(1)}, bf16[4,128,256]{2,1,0:T(8,128)(2,1)S(1)}, u32[]{:S(2)}, u32[]{:S(2)}) %collective-permute-start.11) | collective-permute-done | bytes 262176 | tf_op jit(solution)/shard_map/ppermute | solution.py:26
  44.7 1.5 %collective-permute-start.12 = (bf16[4,208,256]{2,1,0:T(8,128)(2,1)S(1)}, bf16[4,208,256]{2,1,0:T(8,128)(2,1)S(1)}, u32[]{:S(2)}, u32[]{:S(2)}) collective-permute-start(bf16[4,208,256]{2,1,0:T(8,128)(2,1)S(1)} %get-tuple-element.28.refs_0_), channel_id=1, source_target_pairs={{0,3},{1,2},{2,1},{3,0},{4,7},{5,6},{6,5},{7,4},{8,11},{9,10},{10,... | collective-permute-start | bytes 1277960 | tf_op jit(solution)/shard_map/ppermute | solution.py:26
  46.3 3.3 %collective-permute-start.13 = (bf16[4,176,256]{2,1,0:T(8,128)(2,1)S(1)}, bf16[4,176,256]{2,1,0:T(8,128)(2,1)S(1)}, u32[]{:S(2)}, u32[]{:S(2)}) collective-permute-start(bf16[4,176,256]{2,1,0:T(8,128)(2,1)S(1)} %get-tuple-element.29.refs_2_), channel_id=1, source_target_pairs={{0,4},{1,5},{2,6},{3,7},{4,0},{5,1},{6,2},{7,3},{8,12},{9,13},{10,... | collective-permute-start | bytes 1081352 | tf_op jit(solution)/shard_map/ppermute | solution.py:26
  49.6 5.7 %collective-permute-done.14.refs_5_ = bf16[4,128,256]{2,1,0:T(8,128)(2,1)S(1)} collective-permute-done((bf16[4,128,256]{2,1,0:T(8,128)(2,1)S(1)}, bf16[4,128,256]{2,1,0:T(8,128)(2,1)S(1)}, u32[]{:S(2)}, u32[]{:S(2)}) %collective-permute-start.14) | collective-permute-done | bytes 262176 | tf_op jit(solution)/shard_map/ppermute | solution.py:26
  55.3 1.2 %collective-permute-done.13.refs_3_ = bf16[4,176,256]{2,1,0:T(8,128)(2,1)S(1)} collective-permute-done((bf16[4,176,256]{2,1,0:T(8,128)(2,1)S(1)}, bf16[4,176,256]{2,1,0:T(8,128)(2,1)S(1)}, u32[]{:S(2)}, u32[]{:S(2)}) %collective-permute-start.13) | collective-permute-done | bytes 360480 | tf_op jit(solution)/shard_map/ppermute | solution.py:26
  56.8 2.8 %collective-permute-start.15 = (bf16[4,208,256]{2,1,0:T(8,128)(2,1)S(1)}, bf16[4,208,256]{2,1,0:T(8,128)(2,1)S(1)}, u32[]{:S(2)}, u32[]{:S(2)}) collective-permute-start(bf16[4,208,256]{2,1,0:T(8,128)(2,1)S(1)} %get-tuple-element.31.refs_0_), channel_id=1, source_target_pairs={{0,4},{1,5},{2,6},{3,7},{4,0},{5,1},{6,2},{7,3},{8,12},{9,13},{10,... | collective-permute-start | bytes 1277960 | tf_op jit(solution)/shard_map/ppermute | solution.py:26
  59.7 1.2 %collective-permute-start.17 = (bf16[4,128,256]{2,1,0:T(8,128)(2,1)S(1)}, bf16[4,128,256]{2,1,0:T(8,128)(2,1)S(1)}, u32[]{:S(2)}, u32[]{:S(2)}) collective-permute-start(bf16[4,128,256]{2,1,0:T(8,128)(2,1)S(1)} %get-tuple-element.33.refs_2_), channel_id=1, source_target_pairs={{0,3},{1,2},{2,1},{3,0},{4,7},{5,6},{6,5},{7,4},{8,11},{9,10},{10,... | collective-permute-start | bytes 786440 | tf_op jit(solution)/shard_map/ppermute | solution.py:26
  60.9 5.6 %collective-permute-done.17.refs_5_ = bf16[4,128,256]{2,1,0:T(8,128)(2,1)S(1)} collective-permute-done((bf16[4,128,256]{2,1,0:T(8,128)(2,1)S(1)}, bf16[4,128,256]{2,1,0:T(8,128)(2,1)S(1)}, u32[]{:S(2)}, u32[]{:S(2)}) %collective-permute-start.17) | collective-permute-done | bytes 262176 | tf_op jit(solution)/shard_map/ppermute | solution.py:26
  66.5 0.7 collective-permute-done.15.refs_3_
  67.2 1.2 %absorb.1 = (bf16[2,256,256]{2,1,0:T(8,128)(2,1)}, bf16[4,208,256]{2,1,0:T(8,128)(2,1)S(1)}, bf16[4,176,256]{2,1,0:T(8,128)(2,1)S(1)}, bf16[4,128,256]{2,1,0:T(8,128)(2,1)S(1)}) custom-call(bf16[16,256,256]{2,1,0:T(8,128)(2,1)S(1)} %copy-done, bf16[4,208,256]{2,1,0:T(8,128)(2,1)S(1)} %get-tuple-element.31.refs_0_, ...), custom_call_target="tpu_custom_call" | custom-call | flops 268435456 | bytes 5242880 | tf_op jit(solution)/shard_map/absorb/pallas_call | solution.py:196
  68.4 0.5 collective-permute-start.18
  69.0 0.8 collective-permute-start.19
  69.8 2.7 %collective-permute-start.20 = (bf16[4,128,256]{2,1,0:T(8,128)(2,1)S(1)}, bf16[4,128,256]{2,1,0:T(8,128)(2,1)S(1)}, u32[]{:S(2)}, u32[]{:S(2)}) collective-permute-start(bf16[4,128,256]{2,1,0:T(8,128)(2,1)S(1)} %get-tuple-element.37.refs_4_), channel_id=1, source_target_pairs={{0,4},{1,5},{2,6},{3,7},{4,0},{5,1},{6,2},{7,3},{8,12},{9,13},{10,... | collective-permute-start | bytes 786440 | tf_op jit(solution)/shard_map/ppermute | solution.py:26
  72.5 2.5 %load.3.refs_6_ = bf16[4,10,256,256]{3,2,1,0:T(8,128)(2,1)S(1)} custom-call(bf16[4,10,256,256]{3,2,1,0:T(8,128)(2,1)} %edge_ref.3), custom_call_target="tpu_custom_call" | custom-call | bytes 10485760 | tf_op jit(solution)/shard_map/load/pallas_call | solution.py:67
  75.1 1.4 %collective-permute-done.20.refs_5_ = bf16[4,128,256]{2,1,0:T(8,128)(2,1)S(1)} collective-permute-done((bf16[4,128,256]{2,1,0:T(8,128)(2,1)S(1)}, bf16[4,128,256]{2,1,0:T(8,128)(2,1)S(1)}, u32[]{:S(2)}, u32[]{:S(2)}) %collective-permute-start.20) | collective-permute-done | bytes 262176 | tf_op jit(solution)/shard_map/ppermute | solution.py:26
  76.8 3.1 %col_partial.1 = bf16[16,4,16,256]{3,2,1,0:T(8,128)(2,1)S(1)} custom-call(s32[4,10]{1,0:T(4,128)S(1)} %copy-done.4, bf16[4,208,256]{2,1,0:T(8,128)(2,1)S(1)} %get-tuple-element.35.refs_0_, bf16[4,208,256]{2,1,0:T(8,128)(2,1)S(1)} %collective-permute-done.18.refs_1_, bf16[4,176,256]{2,1,0:T(8,128)(2,1)S(1)} %get-tuple-element.36.refs_2_, ...), custom_call_target="tpu_custom_call" | custom-call | flops 1342177280 | bytes 5242880 | tf_op jit(solution)/shard_map/col_partial/pallas_call | solution.py:244
  79.9 17.7 %all_to_all.5.part_ref = bf16[16,4,16,256]{3,2,1,0:T(8,128)(2,1)S(1)} all-to-all(bf16[16,4,16,256]{3,2,1,0:T(8,128)(2,1)S(1)} %col_partial.1), channel_id=1, replica_groups=mesh['left'=16,'right'=8] {'left'}, dimensions={0} | all-to-all | bytes 1048576 | tf_op jit(solution)/shard_map/all_to_all | solution.py:310
  97.6 0.9 finish.1
  (32 shorter events, 1.4 us)
Async XLA Ops:
  0.6 17.8 %copy-start.2 = (bf16[1,256,256]{2,1,0:T(8,128)(2,1)S(1)}, bf16[1,256,256]{2,1,0:T(8,128)(2,1)}, u32[]{:S(2)}) copy-start(bf16[1,256,256]{2,1,0:T(8,128)(2,1)} %refs_0_.1) | copy-start | bytes 393220
  0.6 8.1 %collective-permute-start.1 = (bf16[1,256,256]{2,1,0:T(8,128)(2,1)}, bf16[1,256,256]{2,1,0:T(8,128)(2,1)S(1)}, u32[]{:S(2)}, u32[]{:S(2)}) collective-permute-start(bf16[1,256,256]{2,1,0:T(8,128)(2,1)} %refs_0_.1), channel_id=1, source_target_pairs={{0,64},{8,72},{16,80},{24,88},{32,96},{40,104},{48,112},{56,120},{... | collective-permute-start | bytes 393224 | tf_op jit(solution)/shard_map/ppermute | solution.py:286
  4.5 7.5 %collective-permute-start = (bf16[1,256,256]{2,1,0:T(8,128)(2,1)}, bf16[1,256,256]{2,1,0:T(8,128)(2,1)S(1)}, u32[]{:S(2)}, u32[]{:S(2)}) collective-permute-start(bf16[1,256,256]{2,1,0:T(8,128)(2,1)} %refs_0_.1), channel_id=1, source_target_pairs={{0,32},{8,40},{16,48},{24,56},{32,64},{40,72},{48,80},{56,88},{64,... | collective-permute-start | bytes 393224 | tf_op jit(solution)/shard_map/ppermute | solution.py:286
  4.9 13.5 %collective-permute-start.2 = (bf16[1,256,256]{2,1,0:T(8,128)(2,1)}, bf16[1,256,256]{2,1,0:T(8,128)(2,1)S(1)}, u32[]{:S(2)}, u32[]{:S(2)}) collective-permute-start(bf16[1,256,256]{2,1,0:T(8,128)(2,1)} %refs_0_.1), channel_id=1, source_target_pairs={{0,96},{8,104},{16,112},{24,120},{32,0},{40,8},{48,16},{56,24},{64... | collective-permute-start | bytes 393224 | tf_op jit(solution)/shard_map/ppermute | solution.py:286
  7.1 14.2 %collective-permute-start.3 = (bf16[1,256,256]{2,1,0:T(8,128)(2,1)}, bf16[1,256,256]{2,1,0:T(8,128)(2,1)S(1)}, u32[]{:S(2)}, u32[]{:S(2)}) collective-permute-start(bf16[1,256,256]{2,1,0:T(8,128)(2,1)} %refs_0_.1), channel_id=1, source_target_pairs={{0,16},{8,24},{16,0},{24,8},{32,48},{40,56},{48,32},{56,40},{64,80... | collective-permute-start | bytes 393224 | tf_op jit(solution)/shard_map/ppermute | solution.py:286
  8.8 12.5 %collective-permute-start.4 = (bf16[1,256,256]{2,1,0:T(8,128)(2,1)}, bf16[1,256,256]{2,1,0:T(8,128)(2,1)S(1)}, u32[]{:S(2)}, u32[]{:S(2)}) collective-permute-start(bf16[1,256,256]{2,1,0:T(8,128)(2,1)} %refs_0_.1), channel_id=1, source_target_pairs={{0,48},{8,56},{16,32},{24,40},{32,80},{40,88},{48,64},{56,72},{64,... | collective-permute-start | bytes 393224 | tf_op jit(solution)/shard_map/ppermute | solution.py:286
  8.8 12.5 %collective-permute-start.5 = (bf16[1,256,256]{2,1,0:T(8,128)(2,1)}, bf16[1,256,256]{2,1,0:T(8,128)(2,1)S(1)}, u32[]{:S(2)}, u32[]{:S(2)}) collective-permute-start(bf16[1,256,256]{2,1,0:T(8,128)(2,1)} %refs_0_.1), channel_id=1, source_target_pairs={{0,80},{8,88},{16,64},{24,72},{32,112},{40,120},{48,96},{56,104},{... | collective-permute-start | bytes 393224 | tf_op jit(solution)/shard_map/ppermute | solution.py:286
  12.0 9.3 %collective-permute-start.6 = (bf16[1,256,256]{2,1,0:T(8,128)(2,1)}, bf16[1,256,256]{2,1,0:T(8,128)(2,1)S(1)}, u32[]{:S(2)}, u32[]{:S(2)}) collective-permute-start(bf16[1,256,256]{2,1,0:T(8,128)(2,1)} %refs_0_.1), channel_id=1, source_target_pairs={{0,112},{8,120},{16,96},{24,104},{32,16},{40,24},{48,0},{56,8},{64... | collective-permute-start | bytes 393224 | tf_op jit(solution)/shard_map/ppermute | solution.py:286
  18.4 4.4 %collective-permute-start.7 = (bf16[4,256,256]{2,1,0:T(8,128)(2,1)S(1)}, bf16[4,256,256]{2,1,0:T(8,128)(2,1)S(1)}, u32[]{:S(2)}, u32[]{:S(2)}) collective-permute-start(bf16[4,256,256]{2,1,0:T(8,128)(2,1)S(1)} %join.2), channel_id=1, source_target_pairs={{0,8},{8,0},{16,24},{24,16},{32,40},{40,32},{48,56},{56,48},{64,72... | collective-permute-start | bytes 1572872 | tf_op jit(solution)/shard_map/ppermute | solution.py:295
  21.4 3.2 %copy-start.3 = (s32[16,8]{0,1:T(8,128)S(1)}, s32[16,8]{0,1:T(8,128)}, u32[]{:S(2)}) copy-start(s32[16,8]{0,1:T(8,128)} %param.9) | copy-start | bytes 1540
  21.4 2.9 %collective-permute-start.8 = (bf16[4,256,256]{2,1,0:T(8,128)(2,1)S(1)}, bf16[4,256,256]{2,1,0:T(8,128)(2,1)S(1)}, u32[]{:S(2)}, u32[]{:S(2)}) collective-permute-start(bf16[4,256,256]{2,1,0:T(8,128)(2,1)S(1)} %join.3), channel_id=1, source_target_pairs={{0,8},{8,0},{16,24},{24,16},{32,40},{40,32},{48,56},{56,48},{64,72... | collective-permute-start | bytes 1572872 | tf_op jit(solution)/shard_map/ppermute | solution.py:295
  32.4 12.2 %collective-permute-start.9 = (bf16[4,208,256]{2,1,0:T(8,128)(2,1)S(1)}, bf16[4,208,256]{2,1,0:T(8,128)(2,1)S(1)}, u32[]{:S(2)}, u32[]{:S(2)}) collective-permute-start(bf16[4,208,256]{2,1,0:T(8,128)(2,1)S(1)} %get-tuple-element.23), channel_id=1, source_target_pairs={{0,1},{1,0},{2,3},{3,2},{4,5},{5,4},{6,7},{7,6},{8,9},{9,8},{10,11... | collective-permute-start | bytes 1277960 | tf_op jit(solution)/shard_map/ppermute | solution.py:26
  33.7 10.9 %collective-permute-start.10 = (bf16[4,176,256]{2,1,0:T(8,128)(2,1)S(1)}, bf16[4,176,256]{2,1,0:T(8,128)(2,1)S(1)}, u32[]{:S(2)}, u32[]{:S(2)}) collective-permute-start(bf16[4,176,256]{2,1,0:T(8,128)(2,1)S(1)} %get-tuple-element.25), channel_id=1, source_target_pairs={{0,3},{1,2},{2,1},{3,0},{4,7},{5,6},{6,5},{7,4},{8,11},{9,10},{10,... | collective-permute-start | bytes 1081352 | tf_op jit(solution)/shard_map/ppermute | solution.py:26
  35.5 9.0 %collective-permute-start.11 = (bf16[4,128,256]{2,1,0:T(8,128)(2,1)S(1)}, bf16[4,128,256]{2,1,0:T(8,128)(2,1)S(1)}, u32[]{:S(2)}, u32[]{:S(2)}) collective-permute-start(bf16[4,128,256]{2,1,0:T(8,128)(2,1)S(1)} %get-tuple-element.27), channel_id=1, source_target_pairs={{0,4},{1,5},{2,6},{3,7},{4,0},{5,1},{6,2},{7,3},{8,12},{9,13},{10,... | collective-permute-start | bytes 786440 | tf_op jit(solution)/shard_map/ppermute | solution.py:26
  44.5 22.7 %copy-start = (bf16[16,256,256]{2,1,0:T(8,128)(2,1)S(1)}, bf16[16,256,256]{2,1,0:T(8,128)(2,1)}, u32[]{:S(2)}) copy-start(bf16[16,256,256]{2,1,0:T(8,128)(2,1)} %proj_ref.2) | copy-start | bytes 6291460
  44.7 11.8 %collective-permute-start.12 = (bf16[4,208,256]{2,1,0:T(8,128)(2,1)S(1)}, bf16[4,208,256]{2,1,0:T(8,128)(2,1)S(1)}, u32[]{:S(2)}, u32[]{:S(2)}) collective-permute-start(bf16[4,208,256]{2,1,0:T(8,128)(2,1)S(1)} %get-tuple-element.28.refs_0_), channel_id=1, source_target_pairs={{0,3},{1,2},{2,1},{3,0},{4,7},{5,6},{6,5},{7,4},{8,11},{9,10},{10,... | collective-permute-start | bytes 1277960 | tf_op jit(solution)/shard_map/ppermute | solution.py:26
  46.3 10.2 %collective-permute-start.13 = (bf16[4,176,256]{2,1,0:T(8,128)(2,1)S(1)}, bf16[4,176,256]{2,1,0:T(8,128)(2,1)S(1)}, u32[]{:S(2)}, u32[]{:S(2)}) collective-permute-start(bf16[4,176,256]{2,1,0:T(8,128)(2,1)S(1)} %get-tuple-element.29.refs_2_), channel_id=1, source_target_pairs={{0,4},{1,5},{2,6},{3,7},{4,0},{5,1},{6,2},{7,3},{8,12},{9,13},{10,... | collective-permute-start | bytes 1081352 | tf_op jit(solution)/shard_map/ppermute | solution.py:26
  49.6 5.7 %collective-permute-start.14 = (bf16[4,128,256]{2,1,0:T(8,128)(2,1)S(1)}, bf16[4,128,256]{2,1,0:T(8,128)(2,1)S(1)}, u32[]{:S(2)}, u32[]{:S(2)}) collective-permute-start(bf16[4,128,256]{2,1,0:T(8,128)(2,1)S(1)} %get-tuple-element.30.refs_4_), channel_id=1, source_target_pairs={{0,1},{1,0},{2,3},{3,2},{4,5},{5,4},{6,7},{7,6},{8,9},{9,8},{10,11... | collective-permute-start | bytes 786440 | tf_op jit(solution)/shard_map/ppermute | solution.py:26
  56.8 10.5 %collective-permute-start.15 = (bf16[4,208,256]{2,1,0:T(8,128)(2,1)S(1)}, bf16[4,208,256]{2,1,0:T(8,128)(2,1)S(1)}, u32[]{:S(2)}, u32[]{:S(2)}) collective-permute-start(bf16[4,208,256]{2,1,0:T(8,128)(2,1)S(1)} %get-tuple-element.31.refs_0_), channel_id=1, source_target_pairs={{0,4},{1,5},{2,6},{3,7},{4,0},{5,1},{6,2},{7,3},{8,12},{9,13},{10,... | collective-permute-start | bytes 1277960 | tf_op jit(solution)/shard_map/ppermute | solution.py:26
  59.5 7.0 %collective-permute-start.16 = (bf16[4,176,256]{2,1,0:T(8,128)(2,1)S(1)}, bf16[4,176,256]{2,1,0:T(8,128)(2,1)S(1)}, u32[]{:S(2)}, u32[]{:S(2)}) collective-permute-start(bf16[4,176,256]{2,1,0:T(8,128)(2,1)S(1)} %get-tuple-element.32.refs_1_), channel_id=1, source_target_pairs={{0,1},{1,0},{2,3},{3,2},{4,5},{5,4},{6,7},{7,6},{8,9},{9,8},{10,11... | collective-permute-start | bytes 1081352 | tf_op jit(solution)/shard_map/ppermute | solution.py:26
  59.7 6.7 %collective-permute-start.17 = (bf16[4,128,256]{2,1,0:T(8,128)(2,1)S(1)}, bf16[4,128,256]{2,1,0:T(8,128)(2,1)S(1)}, u32[]{:S(2)}, u32[]{:S(2)}) collective-permute-start(bf16[4,128,256]{2,1,0:T(8,128)(2,1)S(1)} %get-tuple-element.33.refs_2_), channel_id=1, source_target_pairs={{0,3},{1,2},{2,1},{3,0},{4,7},{5,6},{6,5},{7,4},{8,11},{9,10},{10,... | collective-permute-start | bytes 786440 | tf_op jit(solution)/shard_map/ppermute | solution.py:26
  68.4 8.3 %collective-permute-start.18 = (bf16[4,208,256]{2,1,0:T(8,128)(2,1)S(1)}, bf16[4,208,256]{2,1,0:T(8,128)(2,1)S(1)}, u32[]{:S(2)}, u32[]{:S(2)}) collective-permute-start(bf16[4,208,256]{2,1,0:T(8,128)(2,1)S(1)} %get-tuple-element.35.refs_0_), channel_id=1, source_target_pairs={{0,1},{1,0},{2,3},{3,2},{4,5},{5,4},{6,7},{7,6},{8,9},{9,8},{10,11... | collective-permute-start | bytes 1277960 | tf_op jit(solution)/shard_map/ppermute | solution.py:26
  69.0 7.8 %collective-permute-start.19 = (bf16[4,176,256]{2,1,0:T(8,128)(2,1)S(1)}, bf16[4,176,256]{2,1,0:T(8,128)(2,1)S(1)}, u32[]{:S(2)}, u32[]{:S(2)}) collective-permute-start(bf16[4,176,256]{2,1,0:T(8,128)(2,1)S(1)} %get-tuple-element.36.refs_2_), channel_id=1, source_target_pairs={{0,3},{1,2},{2,1},{3,0},{4,7},{5,6},{6,5},{7,4},{8,11},{9,10},{10,... | collective-permute-start | bytes 1081352 | tf_op jit(solution)/shard_map/ppermute | solution.py:26
  69.8 7.0 %copy-start.4 = (s32[4,10]{1,0:T(4,128)S(1)}, s32[4,10]{1,0:T(4,128)}, u32[]{:S(2)}) copy-start(s32[4,10]{1,0:T(4,128)} %source_ref.1) | copy-start | bytes 484
  69.8 6.7 %collective-permute-start.20 = (bf16[4,128,256]{2,1,0:T(8,128)(2,1)S(1)}, bf16[4,128,256]{2,1,0:T(8,128)(2,1)S(1)}, u32[]{:S(2)}, u32[]{:S(2)}) collective-permute-start(bf16[4,128,256]{2,1,0:T(8,128)(2,1)S(1)} %get-tuple-element.37.refs_4_), channel_id=1, source_target_pairs={{0,4},{1,5},{2,6},{3,7},{4,0},{5,1},{6,2},{7,3},{8,12},{9,13},{10,... | collective-permute-start | bytes 786440 | tf_op jit(solution)/shard_map/ppermute | solution.py:26
  75.1 22.6 %copy-start.1 = (bf16[4,256,256]{2,1,0:T(8,128)(2,1)S(1)}, bf16[4,256,256]{2,1,0:T(8,128)(2,1)}, u32[]{:S(2)}) copy-start(bf16[4,256,256]{2,1,0:T(8,128)(2,1)} %proj_ref.3) | copy-start | bytes 1572868
